TPU v7x, 256 devices: a whole 4x4x8 slice. The times are simulated.
256 devices in a mesh: centers: 256 (over y, z, x, core).
Axes of the slice: x: 4, y: 4, z: 8, core: 2. Of those that a mesh axis runs over, the one named last changes fastest.
Arguments:
- spectra: bfloat16 [131072, 2048], P('centers'), may hold values from -6 to 6
- targets: bfloat16 [131072, 300], P('centers'), may hold values from -6 to 6
- centers: bfloat16 [32768, 2048], P('centers'), may hold values from -6 to 6
- coefficients: float32 [32768, 300], P('centers'), may hold values from -3 to 3
- owners: int32 [2], replicated, may hold values from 0 to 255
- batch_rows: int32 [2, 256], replicated, may hold values from 0 to 511
Outputs:
- trained: float32 [32768, 300], P('centers')
- residuals: float32 [2, 256, 300], replicated
Inputs may be any that keep to these rules, and one draw needn't show every extreme that they name: `owners`: a device index on the axis. `batch_rows`: rows may repeat.
All inputs are finite; a program needn't handle non-finite values.
Results may differ from a plain program's by a relative error of at most 0.0022.
Values may be sent and summed in bfloat16 or wider, within the bound.
No kernel may reach another device: no remote copies, remote signals or barrier semaphores. Data moves between devices by JAX's collectives and lax.ppermute only.
A program may use at most 64 MiB of HBM per device.

v0:
```python
import math

import jax
import jax.numpy as jnp
from jax import lax
from jax.sharding import Mesh
from jax.sharding import PartitionSpec as P

ITERS = 2
CENTERS = ("centers_0", "centers_1", "centers_2", "centers_3")


EPSILON = 1e-06
STEP_RATE = 0.2


def from_root(value, axis, source):
    kept = jnp.where(lax.axis_index(axis) == source, value, 0).astype(value.dtype)
    return lax.psum(kept, axis)


def in_blocks(x, dim, size):
    dims = x.shape
    blocks = x.reshape(*dims[:dim], size, dims[dim] // size, *dims[dim + 1 :])
    return jnp.moveaxis(blocks, dim, 0)


def sent_and_summed(x, axis, dim):
    blocks = in_blocks(x, dim, lax.axis_size(axis))
    arrived = lax.all_to_all(blocks, axis, split_axis=0, concat_axis=0, tiled=True)
    return arrived.sum(axis=0)


def sum_in_two_steps(x, axes, dim):
    far, near = axes
    own = sent_and_summed(in_blocks(x, dim, lax.axis_size(far)), near, dim + 1)
    return jnp.sum(lax.all_to_all(own, far, 0, 0, tiled=True), axis=0)


def padded_to(lines, size):
    spare = -len(lines) % size
    return jnp.pad(lines, [(0, spare)] + [(0, 0)] * (lines.ndim - 1))


def copy_for_each(x, axis):
    size = lax.axis_size(axis)
    return lax.all_to_all(jnp.broadcast_to(x[None], (size, *x.shape)), axis, 0, 0, tiled=True)


def in_order(blocks, dim):
    blocks = jnp.moveaxis(blocks, 0, dim)
    dims = blocks.shape
    return blocks.reshape(*dims[:dim], dims[dim] * dims[dim + 1], *dims[dim + 2 :])


def gather_axes(x, axes, dim):
    far, near = axes
    leading = copy_for_each(x, far)
    blocks = jnp.swapaxes(copy_for_each(leading, near), 0, 1)
    return in_order(blocks.reshape(-1, *x.shape), dim)


def nested_sum(x, axes):
    lines = x.reshape(-1, x.shape[-1])
    own = sum_in_two_steps(
        padded_to(lines, lax.axis_size(axes[0]) * lax.axis_size(axes[1])), axes, 0
    )
    whole = gather_axes(own, axes, 0)
    return whole[: len(lines)].reshape(x.shape)


def kernel_tile(batch_spectra, centers, center_norms, factor):
    dots = lax.dot_general(
        batch_spectra, centers, (((1,), (1,)), ((), ())), preferred_element_type=jnp.float32
    )
    batch_norms = jnp.sqrt(jnp.sum(jnp.square(batch_spectra.astype(jnp.float32)), axis=1) + EPSILON)
    scaled = dots / (batch_norms[:, None] * center_norms[None, :]) * factor
    return (scaled + scaled * scaled * scaled / 3.0).astype(jnp.bfloat16)


def body(spectra, targets, centers, coefficients, owners, batch_rows):
    factor = math.sqrt(centers.shape[1])
    devices = lax.axis_size(CENTERS)
    root_scale = math.sqrt(centers.shape[0] * devices)
    center_norms = jnp.sqrt(jnp.sum(jnp.square(centers.astype(jnp.float32)), axis=1) + EPSILON)
    history = []
    for iteration in range(ITERS):
        chosen_rows = batch_rows[iteration]
        batch_spectra = from_root(
            jnp.take(spectra, chosen_rows, axis=0), CENTERS, owners[iteration]
        )
        batch_target = from_root(jnp.take(targets, chosen_rows, axis=0), CENTERS, owners[iteration])
        tile = kernel_tile(batch_spectra, centers, center_norms, factor)
        wide_tile = tile.astype(jnp.float32)
        partial_sum = (
            jnp.dot(
                wide_tile,
                coefficients,
                precision=lax.Precision.HIGHEST,
                preferred_element_type=jnp.float32,
            )
            / root_scale
        )
        prediction = nested_sum(
            partial_sum, (("centers_0", "centers_1"), ("centers_2", "centers_3"))
        )
        residual = prediction - batch_target.astype(jnp.float32)
        update = lax.dot_general(
            wide_tile,
            residual,
            (((0,), (0,)), ((), ())),
            precision=lax.Precision.HIGHEST,
            preferred_element_type=jnp.float32,
        )
        coefficients = coefficients - STEP_RATE / root_scale * update
        history.append(residual)
    return (coefficients, jnp.stack(history))


def solution(mesh):
    torus = Mesh(
        mesh.devices.reshape(4, 8, 4, 2), ("centers_0", "centers_1", "centers_2", "centers_3")
    )
    return jax.shard_map(
        body,
        mesh=torus,
        in_specs=(P(CENTERS, None), P(CENTERS, None), P(CENTERS, None), P(CENTERS, None), P(), P()),
        out_specs=(P(CENTERS, None), P()),
        check_vma=False,
    )
```

profile of v0, /device:TPU:1, one launch (start us, length us, event | category | flops | bytes accessed | tf_op | source)
XLA Modules:
  0.0 418.7 jit_solution(15392191228433366978)
XLA Ops:
  7.2 0.0 all-reduce.3.cloned.1.call-start
  7.2 0.8 fusion.12
  8.1 1.2 copy.19
  9.3 1.2 gather_fusion.3
  10.5 1.2 gather_fusion.1
  11.7 2.3 gather_fusion.2
  14.0 1.4 gather_fusion
  15.4 0.6 fusion.13
  17.3 0.8 select_select_fusion.2
  18.1 2.4 select_select_fusion
  20.5 0.8 select_select_fusion.3
  21.3 1.2 select_select_fusion.1
  22.4 0.0 all-reduce.3.cloned.1.call-update
  22.5 1.0 copy-done.4
  23.5 0.2 multiply_reduce_fusion.2
  23.7 267.3 %all-reduce.3.cloned.1.call-done = (bf16[256,2048]{1,0:T(8,128)(2,1)}, bf16[256,300]{1,0:T(8,128)(2,1)}, bf16[256,2048]{1,0:T(8,128)(2,1)}, bf16[256,300]{1,0:T(8,128)(2,1)}) async-done(((bf16[256,2048]{1,0:T(8,128)(2,1)}, bf16[256,300]{1,0:T(8,128)(2,1)}, bf16[256,2048]{1,0:T(8,128)(2,1)}, bf16[256,300]{1,0:T(8,128)(2,1)}), (bf16[256,2048]{1,0:T(8,128)(2,1)}, bf16[256,300]{1,0:T(8,128)(2,1)}, ...) | async-done | bytes 2404368 | tf_op jit(solution)/shard_map/psum | solution.py:19
  290.9 2.1 multiply_reduce_fusion
  293.1 0.4 fusion.8
  293.5 0.6 copy-done.6
  294.2 0.3 convolution_multiply_fusion.1
  294.5 0.2 copy.16
  294.6 0.1 copy.17
  294.7 14.7 %all_to_all.40 = f32[8,32,1,300]{3,1,2,0:T(8,128)S(1)} all-to-all(f32[8,32,1,300]{3,1,2,0:T(8,128)S(1)} %copy.17), channel_id=1, replica_groups=mesh['centers_0'=4,'centers_1'=8,'centers_2'=4,'centers_3'=2] {'centers_..., dimensions={0} | all-to-all | bytes 614400 | tf_op jit(solution)/shard_map/all_to_all | solution.py:30
  309.4 0.6 reduce_sum.69
  310.1 0.8 reduce_sum.70
  310.9 15.6 %all_to_all.41 = f32[32,1,300]{2,1,0:T(1,128)S(1)} all-to-all(f32[32,1,300]{2,1,0:T(1,128)S(1)} %reduce_sum.70), channel_id=1, replica_groups=mesh['centers_0'=4,'centers_1'=8,'centers_2'=4,'centers_3'=2] {'centers_..., dimensions={0} | all-to-all | bytes 76800 | tf_op jit(solution)/shard_map/all_to_all | solution.py:37
  326.5 0.1 reduce_sum.71
  326.6 11.9 %all_to_all.42 = f32[32,1,300]{2,1,0:T(1,128)S(1)} all-to-all(f32[32,1,300]{2,1,0:T(1,128)S(1)} %broadcast_in_dim.61), channel_id=1, replica_groups=mesh['centers_0'=4,'centers_1'=8,'centers_2'=4,'centers_3'=2] {'centers_..., dimensions={0} | all-to-all | bytes 76800 | tf_op jit(solution)/shard_map/all_to_all | solution.py:47
  338.5 0.8 broadcast_in_dim.63
  339.3 6.7 %all-to-all-start.3 = ((f32[8,32,1,300]{3,1,2,0:T(8,128)}), f32[8,32,1,300]{3,1,2,0:T(8,128)S(1)}, u32[]{:S(2)}, u32[]{:S(2)}) async-start(f32[8,32,1,300]{3,1,2,0:T(8,128)} %broadcast_in_dim.63), calls=%async_computation.3 | async-start | bytes 786432 | tf_op jit(solution)/shard_map/all_to_all | solution.py:47
  346.0 2.1 fusion.11
  348.1 5.6 %all-to-all-done.3 = f32[8,32,1,300]{3,1,2,0:T(8,128)S(1)} async-done(((f32[8,32,1,300]{3,1,2,0:T(8,128)}), f32[8,32,1,300]{3,1,2,0:T(8,128)S(1)}, u32[]{:S(2)}, u32[]{:S(2)}) %all-to-all-start.3) | async-done | bytes 307232 | tf_op jit(solution)/shard_map/all_to_all | solution.py:47
  353.7 1.6 fusion.1
  355.4 1.1 convolution_multiply_fusion
  356.5 0.2 copy.20
  356.7 0.1 copy.21
  356.7 11.7 %all_to_all.43 = f32[8,32,1,300]{3,1,2,0:T(8,128)S(1)} all-to-all(f32[8,32,1,300]{3,1,2,0:T(8,128)S(1)} %copy.21), channel_id=1, replica_groups=mesh['centers_0'=4,'centers_1'=8,'centers_2'=4,'centers_3'=2] {'centers_..., dimensions={0} | all-to-all | bytes 614400 | tf_op jit(solution)/shard_map/all_to_all | solution.py:30
  368.5 11.8 %all_to_all.44 = f32[32,1,300]{2,1,0:T(1,128)S(1)} all-to-all(f32[32,1,300]{2,1,0:T(1,128)S(1)} %reduce_sum.74), channel_id=1, replica_groups=mesh['centers_0'=4,'centers_1'=8,'centers_2'=4,'centers_3'=2] {'centers_..., dimensions={0} | all-to-all | bytes 76800 | tf_op jit(solution)/shard_map/all_to_all | solution.py:37
  380.2 0.1 reduce_sum.75
  380.3 11.9 %all_to_all.45 = f32[32,1,300]{2,1,0:T(1,128)S(1)} all-to-all(f32[32,1,300]{2,1,0:T(1,128)S(1)} %broadcast_in_dim.65), channel_id=1, replica_groups=mesh['centers_0'=4,'centers_1'=8,'centers_2'=4,'centers_3'=2] {'centers_..., dimensions={0} | all-to-all | bytes 76800 | tf_op jit(solution)/shard_map/all_to_all | solution.py:47
  392.2 0.8 broadcast_in_dim.67
  393.0 6.6 %all-to-all-start.7 = ((f32[8,32,1,300]{3,1,2,0:T(8,128)}), f32[8,32,1,300]{3,1,2,0:T(8,128)S(1)}, u32[]{:S(2)}, u32[]{:S(2)}) async-start(f32[8,32,1,300]{3,1,2,0:T(8,128)} %broadcast_in_dim.67), calls=%async_computation.7 | async-start | bytes 786432 | tf_op jit(solution)/shard_map/all_to_all | solution.py:47
  399.5 1.2 fusion.4
  400.7 6.6 %all-to-all-done.7 = f32[8,32,1,300]{3,1,2,0:T(8,128)S(1)} async-done(((f32[8,32,1,300]{3,1,2,0:T(8,128)}), f32[8,32,1,300]{3,1,2,0:T(8,128)S(1)}, u32[]{:S(2)}, u32[]{:S(2)}) %all-to-all-start.7) | async-done | bytes 307232 | tf_op jit(solution)/shard_map/all_to_all | solution.py:47
  407.2 1.2 fusion.5
  408.4 2.2 fusion
  410.6 0.1 pad_maximum_fusion
  410.7 1.1 copy.24
  (29 shorter events, 0.2 us)
Async XLA Ops:
  7.2 4.5 %copy-start = (bf16[512,2048]{1,0:T(8,128)(2,1)S(1)}, bf16[512,2048]{1,0:T(8,128)(2,1)}, u32[]{:S(2)}) copy-start(bf16[512,2048]{1,0:T(8,128)(2,1)} %param.10) | copy-start | bytes 6291460
  7.2 283.8 %all-reduce.3.cloned.1.call-start = ((), (), s32[]{:S(2)}) async-start(), calls=%async_computation.8 | async-start | bytes 4980736 | tf_op jit(solution)/shard_map/psum | solution.py:19
  14.0 1.4 copy-start.7
  22.4 1.0 copy-start.4
  290.9 2.1 copy-start.2
  290.9 3.2 copy-start.3
  293.5 0.6 copy-start.6
  294.6 51.4 %copy-start.1 = (bf16[256,2048]{1,0:T(8,128)(2,1)S(1)}, bf16[256,2048]{1,0:T(8,128)(2,1)}, u32[]{:S(2)}) copy-start(bf16[256,2048]{1,0:T(8,128)(2,1)} %get-tuple-element.12) | copy-start | bytes 3145732
  339.3 14.4 %all-to-all-start.3 = ((f32[8,32,1,300]{3,1,2,0:T(8,128)}), f32[8,32,1,300]{3,1,2,0:T(8,128)S(1)}, u32[]{:S(2)}, u32[]{:S(2)}) async-start(f32[8,32,1,300]{3,1,2,0:T(8,128)} %broadcast_in_dim.63), calls=%async_computation.3 | async-start | bytes 786432 | tf_op jit(solution)/shard_map/all_to_all | solution.py:47
  368.4 40.0 %copy-start.5 = (bf16[256,128]{1,0:T(8,128)(2,1)S(1)}, bf16[256,128]{1,0:T(8,128)(2,1)}, u32[]{:S(2)}) copy-start(bf16[256,128]{1,0:T(8,128)(2,1)} %fusion.11) | copy-start | bytes 196612
  393.0 14.3 %all-to-all-start.7 = ((f32[8,32,1,300]{3,1,2,0:T(8,128)}), f32[8,32,1,300]{3,1,2,0:T(8,128)S(1)}, u32[]{:S(2)}, u32[]{:S(2)}) async-start(f32[8,32,1,300]{3,1,2,0:T(8,128)} %broadcast_in_dim.67), calls=%async_computation.7 | async-start | bytes 786432 | tf_op jit(solution)/shard_map/all_to_all | solution.py:47
Sparse Core Ops, SparseCore 0:
  22.6 268.3 all-reduce.2
where the time goes:
time: 420 us; the launch traced here: 419 us
  waiting for transfers between devices  279 us (66%)
  blocking collectives  77.5 us (18%)
  between operations  15.5 us (4%)
  local copies, waits for them, and re-layouts  14.4 us (3%)
  starting transfers between devices  13.3 us (3%)
  other arithmetic  10.7 us (3%)
  matrix products  7.81 us (2%)
    psum x1, waiting for transfers between devices, from_root(): return lax.psum(kept, axis)  267 us
    all_to_all x2, blocking collectives, sum_in_two_steps(): return jnp.sum(lax.all_to_all(own, far, 0, 0, tiled=True), axis=0)  27.3 us
    all_to_all x2, blocking collectives, sent_and_summed(): lax.all_to_all(blocks, axis, split_axis=0, concat_axis=0, tiled=True)  26.4 us
    all_to_all x2, blocking collectives, copy_for_each(): lax.all_to_all(jnp.broadcast_to(x[None], (size, *x.shape)), axis, 0, 0, t...  23.8 us
    all_to_all x2, starting transfers between devices, copy_for_each(): lax.all_to_all(jnp.broadcast_to(x[None], (size, *x.shape)), axis, 0, 0, t...  13.3 us
    all_to_all x2, waiting for transfers between devices, copy_for_each(): lax.all_to_all(jnp.broadcast_to(x[None], (size, *x.shape)), axis, 0, 0, t...  12.2 us
  transfers between devices with their start and end apart: 3, of which 3 were waited for; matrix products, arithmetic and copies ran while one was open for 1% of the time, Pallas kernels for 0%

commit v1 on v0

v1 whole, which is shorter than its diff:
```python
import math

import jax
import jax.numpy as jnp
from jax import lax
from jax.sharding import Mesh
from jax.sharding import PartitionSpec as P

ITERS = 2
AXES = ("y", "z", "x", "core")
PLANE = ("y", "x")
EPSILON = 1e-06
STEP_RATE = 0.2
PAIR = [(0, 1), (1, 0)]


def swap(value):
    return lax.ppermute(value, "core", PAIR)


def exchange(blocks, axes):
    return lax.all_to_all(blocks, axes, 0, 0, tiled=True)


def copies(value, axes):
    size = lax.axis_size(axes)
    return exchange(jnp.broadcast_to(value[None], (size, *value.shape)), axes)


def rows_of(array, rows):
    return array.at[rows].get(mode="promise_in_bounds")


def norms_of(value):
    return jnp.sqrt(jnp.sum(jnp.square(value.astype(jnp.float32)), axis=1) + EPSILON)


def body(spectra, targets, centers, coefficients, owners, batch_rows):
    features = centers.shape[1]
    outs = coefficients.shape[1]
    batch = batch_rows.shape[1]
    half = batch // 2
    factor = math.sqrt(features)
    total = centers.shape[0] * lax.axis_size(AXES)
    root_scale = math.sqrt(total)
    sizes = [lax.axis_size(name) for name in AXES]
    y, z, x, core = (lax.axis_index(name) for name in AXES)
    root_core = owners % sizes[3]
    root_x = owners // sizes[3] % sizes[2]
    root_z = owners // (sizes[3] * sizes[2]) % sizes[1]
    root_y = owners // (sizes[3] * sizes[2] * sizes[1])
    root_plane = root_y * sizes[2] + root_x
    own_root = root_core == core
    on_root = (root_y == y) & (root_z == z) & (root_x == x)

    both_centers = jnp.concatenate([centers, swap(centers)])
    both_coefficients = jnp.concatenate([coefficients, swap(coefficients)])
    center_norms = norms_of(both_centers)

    halves = batch_rows.reshape(ITERS, 2, half)
    kept_rows = jnp.where(core == 0, halves[:, 0], halves[:, 1])
    sent_rows = jnp.where(core == 0, halves[:, 1], halves[:, 0])
    kept = rows_of(spectra, kept_rows)
    came = swap(rows_of(spectra, sent_rows))
    mine = jnp.where(own_root[:, None, None], kept, came)
    kept_targets = rows_of(targets, kept_rows)
    came_targets = swap(rows_of(targets, sent_rows))
    mine_targets = jnp.where(own_root[:, None, None], kept_targets, came_targets)

    plane = sizes[0] * sizes[2]
    each = half // plane
    blocks = mine.reshape(ITERS, plane, each, features)
    scattered = exchange(jnp.swapaxes(blocks, 0, 1), PLANE)
    piece = jnp.stack(
        [lax.dynamic_index_in_dim(scattered, root_plane[t], 0, False)[t] for t in range(ITERS)]
    )
    along = copies(piece, "z")
    piece = jnp.stack(
        [lax.dynamic_index_in_dim(along, root_z[t], 0, False)[t] for t in range(ITERS)]
    )
    gathered = copies(piece, PLANE)
    spectra_half = jnp.swapaxes(gathered, 0, 1).reshape(ITERS * half, features)

    dots = lax.dot_general(
        spectra_half, both_centers, (((1,), (1,)), ((), ())), preferred_element_type=jnp.float32
    )
    scaled = dots / (norms_of(spectra_half)[:, None] * center_norms[None, :]) * factor
    tile = (scaled + scaled * scaled * scaled / 3.0).astype(jnp.bfloat16)
    other = swap(jnp.roll(tile, centers.shape[0], axis=1))
    tile_0, tile_1 = tile[:half], tile[half:]

    partial = (
        jnp.dot(
            tile.astype(jnp.float32),
            both_coefficients,
            precision=lax.Precision.HIGHEST,
            preferred_element_type=jnp.float32,
        )
        / root_scale
    ).reshape(ITERS, half, outs)
    held = jnp.where(on_root[:, None, None], mine_targets, 0).astype(jnp.float32)
    partial = partial - held
    gram = lax.dot_general(
        tile_1,
        jnp.concatenate([tile_0, other[:half]]),
        (((1,), (1,)), ((), ())),
        preferred_element_type=jnp.float32,
    )
    lines = jnp.concatenate([partial[0], partial[1], gram], axis=1)
    own = exchange(lines.reshape(plane, each, -1), PLANE).sum(axis=0)
    own = copies(own, "z").sum(axis=0)
    whole = copies(own, PLANE).reshape(half, -1)
    whole_other = swap(whole)

    first, second = whole[:, :outs], whole_other[:, :outs]
    mixed = jnp.concatenate([whole[:, 2 * outs :], jnp.roll(whole_other[:, 2 * outs :], half, axis=1)])
    later = jnp.concatenate([whole[:, outs : 2 * outs], whole_other[:, outs : 2 * outs]])
    residual_0 = jnp.concatenate([first, second])
    residual_1 = later - STEP_RATE / total * jnp.dot(
        mixed, residual_0, precision=lax.Precision.HIGHEST, preferred_element_type=jnp.float32
    )
    own_centers = centers.shape[0]
    tiles = jnp.concatenate(
        [tile_0[:, :own_centers], other[:half, :own_centers], tile_1[:, :own_centers], other[half:, :own_centers]]
    )
    update = lax.dot_general(
        tiles.astype(jnp.float32),
        jnp.concatenate([residual_0, residual_1]),
        (((0,), (0,)), ((), ())),
        precision=lax.Precision.HIGHEST,
        preferred_element_type=jnp.float32,
    )
    trained = coefficients - STEP_RATE / root_scale * update
    residuals = jnp.stack([residual_0, residual_1]).reshape(ITERS, 2, half, outs)
    residuals = jnp.where(core == 0, residuals, residuals[:, ::-1]).reshape(ITERS, batch, outs)
    return trained, residuals


def solution(mesh):
    torus = Mesh(mesh.devices.reshape(4, 8, 4, 2), AXES)
    return jax.shard_map(
        body,
        mesh=torus,
        in_specs=(P(AXES, None), P(AXES, None), P(AXES, None), P(AXES, None), P(), P()),
        out_specs=(P(AXES, None), P()),
        check_vma=False,
    )
```

time: 420 us -> 151 us (0.36)
  waiting for transfers between devices: 279 us -> 37.6 us
  blocking collectives: 77.5 us -> 24.4 us
  starting transfers between devices: 13.3 us -> 37.2 us
  local copies, waits for them, and re-layouts: 14.4 us -> 31 us
  between operations: 15.5 us -> 8.66 us
  other arithmetic: 10.7 us -> 5.2 us
    psum x1 -> x0, waiting for transfers between devices: 267 us -> none  [from_root(): return lax.psum(kept, axis)]
    all_to_all x6 -> x2, blocking collectives: 77.5 us -> 24.4 us  [exchange(): return lax.all_to_all(blocks, axes, 0, 0, tiled=True)]
    all_to_all x2 -> x4, waiting for transfers between devices: 12.2 us -> 36.3 us  [exchange(): return lax.all_to_all(blocks, axes, 0, 0, tiled=True)]
    ppermute x0 -> x6, starting transfers between devices: none -> 13.1 us  [swap(): return lax.ppermute(value, 'core', PAIR)]
    all_to_all x2 -> x4, starting transfers between devices: 13.3 us -> 24.2 us  [exchange(): return lax.all_to_all(blocks, axes, 0, 0, tiled=True)]
  transfers between devices with their start and end apart: 3 -> 10, of which waited for: 3 -> 6; matrix products, arithmetic and copies ran while one was open for 1% -> 11% of each run, Pallas kernels for 0% -> 0%
where the time goes in v1:
time: 151 us; the launch traced here: 150 us
  waiting for transfers between devices  37.6 us (25%)
  starting transfers between devices  37.2 us (25%)
  local copies, waits for them, and re-layouts  31 us (21%)
  blocking collectives  24.4 us (16%)
  between operations  8.66 us (6%)
  matrix products  5.61 us (4%)
  other arithmetic  5.2 us (3%)
    all_to_all x4, waiting for transfers between devices, exchange(): return lax.all_to_all(blocks, axes, 0, 0, tiled=True)  36.3 us
    all_to_all x2, blocking collectives, exchange(): return lax.all_to_all(blocks, axes, 0, 0, tiled=True)  24.4 us
    all_to_all x4, starting transfers between devices, exchange(): return lax.all_to_all(blocks, axes, 0, 0, tiled=True)  24.2 us
    ppermute x6, starting transfers between devices, swap(): return lax.ppermute(value, 'core', PAIR)  13.1 us
    gather x4, local copies, waits for them, and re-layouts, rows_of(): return array.at[rows].get(mode='promise_in_bounds')  7.35 us
    unnamed x19, local copies, waits for them, and re-layouts  5.14 us
  transfers between devices with their start and end apart: 10, of which 6 were waited for; matrix products, arithmetic and copies ran while one was open for 11% of the time, Pallas kernels for 0%

profile of v1, /device:TPU:1, one launch (start us, length us, event | category | flops | bytes accessed | tf_op | source)
XLA Modules:
  0.0 149.8 jit_solution(4444056429232985346)
XLA Ops:
  0.6 0.8 reshape.114
  1.5 0.7 slice.147
  2.2 0.7 fusion.31
  2.9 2.3 %gather_fusion.1 = bf16[256,2048]{1,0:T(8,128)(2,1)} fusion(bf16[512,2048]{1,0:T(8,128)(2,1)S(1)} %copy-done, s32[1024]{0:T(1024)S(1)} %pad_clamp_fusion), kind=kCustom, calls=%fused_computation.1 | custom fusion | bytes 2098176 | tf_op jit(solution)/shard_map/gather | solution.py:31
  5.2 3.2 %collective-permute-start = (bf16[2,128,2048]{2,1,0:T(8,128)(2,1)}, bf16[2,128,2048]{2,1,0:T(8,128)(2,1)}, u32[]{:S(2)}, u32[]{:S(2)}) collective-permute-start(bf16[2,128,2048]{2,1,0:T(8,128)(2,1)} %bitcast.8), channel_id=1, source_target_pairs={{0,1},{1,0},{2,3},{3,2},{4,5},{5,4},{6,7},{7,6},{8,9},{9,8},{10,11... | collective-permute-start | bytes 3145736 | tf_op jit(solution)/shard_map/ppermute | solution.py:18
  8.4 1.4 gather_fusion
  9.8 1.2 collective-permute-done
  11.1 1.4 select_bitcast_fusion
  12.5 1.1 copy.63
  13.5 5.0 %all-to-all-start = ((bf16[16,2,8,2048]{3,2,1,0:T(8,128)(2,1)}), bf16[16,2,8,2048]{3,2,1,0:T(8,128)(2,1)S(1)}, u32[]{:S(2)}, u32[]{:S(2)}) async-start(bf16[16,2,8,2048]{3,2,1,0:T(8,128)(2,1)} %copy.63), calls=%async_computation | async-start | bytes 2097152 | tf_op jit(solution)/shard_map/all_to_all | solution.py:22
  23.1 11.9 %all-to-all-done = bf16[16,2,8,2048]{3,2,1,0:T(8,128)(2,1)S(1)} async-done(((bf16[16,2,8,2048]{3,2,1,0:T(8,128)(2,1)}), bf16[16,2,8,2048]{3,2,1,0:T(8,128)(2,1)S(1)}, u32[]{:S(2)}, u32[]{:S(2)}) %all-to-all-start) | async-done | bytes 1048608 | tf_op jit(solution)/shard_map/all_to_all | solution.py:22
  34.9 0.8 broadcast_in_dim.37
  35.8 8.2 %all-to-all-start.1 = ((bf16[8,2,8,2048]{3,2,1,0:T(8,128)(2,1)}), bf16[8,2,8,2048]{3,2,1,0:T(8,128)(2,1)S(1)}, u32[]{:S(2)}, u32[]{:S(2)}) async-start(bf16[8,2,8,2048]{3,2,1,0:T(8,128)(2,1)} %broadcast_in_dim.37), calls=%async_computation.1 | async-start | bytes 1048576 | tf_op jit(solution)/shard_map/all_to_all | solution.py:22
  44.0 2.4 %collective-permute-start.1 = (bf16[128,2048]{1,0:T(8,128)(2,1)}, bf16[128,2048]{1,0:T(8,128)(2,1)}, u32[]{:S(2)}, u32[]{:S(2)}) collective-permute-start(bf16[128,2048]{1,0:T(8,128)(2,1)} %param.8), channel_id=1, source_target_pairs={{0,1},{1,0},{2,3},{3,2},{4,5},{5,4},{6,7},{7,6},{8,9},{9,8},{10,11... | collective-permute-start | bytes 1572872 | tf_op jit(solution)/shard_map/ppermute | solution.py:18
  50.8 8.5 %all-to-all-done.1 = bf16[8,2,8,2048]{3,2,1,0:T(8,128)(2,1)S(1)} async-done(((bf16[8,2,8,2048]{3,2,1,0:T(8,128)(2,1)}), bf16[8,2,8,2048]{3,2,1,0:T(8,128)(2,1)S(1)}, u32[]{:S(2)}, u32[]{:S(2)}) %all-to-all-start.1) | async-done | bytes 524320 | tf_op jit(solution)/shard_map/all_to_all | solution.py:22
  59.2 1.1 broadcast_in_dim.38
  60.4 7.2 %all-to-all-start.2 = ((bf16[16,2,8,2048]{3,2,1,0:T(8,128)(2,1)}), bf16[16,2,8,2048]{3,2,1,0:T(8,128)(2,1)S(1)}, u32[]{:S(2)}, u32[]{:S(2)}) async-start(bf16[16,2,8,2048]{3,2,1,0:T(8,128)(2,1)} %broadcast_in_dim.38), calls=%async_computation.2 | async-start | bytes 2097152 | tf_op jit(solution)/shard_map/all_to_all | solution.py:22
  67.6 0.9 collective-permute-start.3
  68.4 1.2 copy.65
  69.6 1.8 %gather_fusion.3 = bf16[256,300]{1,0:T(8,128)(2,1)} fusion(bf16[512,300]{1,0:T(8,128)(2,1)S(1)} %copy.65, s32[1024]{0:T(1024)S(1)} %pad_clamp_fusion), kind=kCustom, calls=%fused_computation.3 | custom fusion | bytes 308224 | tf_op jit(solution)/shard_map/gather | solution.py:31
  71.5 1.8 %gather_fusion.2 = bf16[256,300]{1,0:T(8,128)(2,1)} fusion(bf16[512,300]{1,0:T(8,128)(2,1)S(1)} %copy.65, s32[1024]{0:T(1024)S(1)} %pad_clamp_fusion.1), kind=kCustom, calls=%fused_computation.2 | custom fusion | bytes 308224 | tf_op jit(solution)/shard_map/gather | solution.py:31
  73.3 1.1 constant_dynamic-update-slice_fusion.1
  74.4 1.1 constant_dynamic-update-slice_fusion
  75.8 0.7 copy-done.1
  76.4 7.4 %all-to-all-done.2 = bf16[16,2,8,2048]{3,2,1,0:T(8,128)(2,1)S(1)} async-done(((bf16[16,2,8,2048]{3,2,1,0:T(8,128)(2,1)}), bf16[16,2,8,2048]{3,2,1,0:T(8,128)(2,1)S(1)}, u32[]{:S(2)}, u32[]{:S(2)}) %all-to-all-start.2) | async-done | bytes 1048608 | tf_op jit(solution)/shard_map/all_to_all | solution.py:22
  84.3 1.1 copy-done.2
  85.9 1.3 convolution_multiply_fusion.1
  87.5 2.4 %collective-permute-start.2 = (bf16[256,256]{1,0:T(8,128)(2,1)S(1)}, bf16[256,256]{1,0:T(8,128)(2,1)S(1)}, u32[]{:S(2)}, u32[]{:S(2)}) collective-permute-start(bf16[256,256]{1,0:T(8,128)(2,1)S(1)} %pad_maximum_fusion.2), channel_id=1, source_target_pairs={{0,1},{1,0},{2,3},{3,2},{4,5},{5,4},{6,7},{7,6},{8,9},{9,8},{10,11... | collective-permute-start | bytes 393224 | tf_op jit(solution)/shard_map/ppermute | solution.py:18
  89.9 1.0 convert_subtract_fusion
  91.4 12.8 %all_to_all.30 = f32[16,8,856]{2,1,0:T(8,128)S(1)} all-to-all(f32[16,8,856]{2,1,0:T(8,128)S(1)} %pad_maximum_fusion), channel_id=1, replica_groups=mesh['y'=4,'z'=8,'x'=4,'core'=2] {'y','x'}, dimensions={0} | all-to-all | bytes 876544 | tf_op jit(solution)/shard_map/all_to_all | solution.py:22
  104.3 11.6 %all_to_all.31 = f32[8,8,856]{2,1,0:T(8,128)S(1)} all-to-all(f32[8,8,856]{2,1,0:T(8,128)S(1)} %broadcast_in_dim.42), channel_id=1, replica_groups=mesh['y'=4,'z'=8,'x'=4,'core'=2] {'z'}, dimensions={0} | all-to-all | bytes 438272 | tf_op jit(solution)/shard_map/all_to_all | solution.py:22
  115.9 0.8 broadcast_in_dim.43
  116.7 3.7 %all-to-all-start.5 = ((f32[16,8,856]{2,1,0:T(8,128)}), f32[16,8,856]{2,1,0:T(8,128)S(1)}, u32[]{:S(2)}, u32[]{:S(2)}) async-start(f32[16,8,856]{2,1,0:T(8,128)} %broadcast_in_dim.43), calls=%async_computation.5 | async-start | bytes 917504 | tf_op jit(solution)/shard_map/all_to_all | solution.py:22
  120.5 8.6 %all-to-all-done.5 = f32[16,8,856]{2,1,0:T(8,128)S(1)} async-done(((f32[16,8,856]{2,1,0:T(8,128)}), f32[16,8,856]{2,1,0:T(8,128)S(1)}, u32[]{:S(2)}, u32[]{:S(2)}) %all-to-all-start.5) | async-done | bytes 438304 | tf_op jit(solution)/shard_map/all_to_all | solution.py:22
  129.2 4.2 %collective-permute-start.5 = (f32[128,856]{0,1:T(8,128)S(1)}, f32[128,856]{0,1:T(8,128)S(1)}, u32[]{:S(2)}, u32[]{:S(2)}) collective-permute-start(f32[128,856]{0,1:T(8,128)S(1)} %copy.68), channel_id=1, source_target_pairs={{0,1},{1,0},{2,3},{3,2},{4,5},{5,4},{6,7},{7,6},{8,9},{9,8},{10,11... | collective-permute-start | bytes 1314824 | tf_op jit(solution)/shard_map/ppermute | solution.py:18
  133.4 0.6 fusion.45
  134.0 0.7 slice.164
  134.8 0.7 fusion.42
  135.7 0.9 stack.17
  136.5 1.0 constant_dynamic-update-slice_fusion.3
  137.5 0.9 fusion.43
  138.4 1.4 maximum_subtract_fusion
  139.8 0.9 stack.18
  140.7 1.0 constant_dynamic-update-slice_fusion.2
  141.7 2.9 %rev.3 = f32[2,2,128,300]{2,1,3,0:T(2,128)} reverse(f32[2,2,128,300]{2,1,3,0:T(2,128)S(1)} %constant_dynamic-update-slice_fusion.2), dimensions={1} | reverse | bytes 1228800 | tf_op jit(solution)/shard_map/rev | solution.py:135
  144.6 1.1 broadcast_select_fusion
  146.3 1.3 copy.74
  147.6 2.2 %fusion.1 = f32[128,300]{0,1:T(8,128)} fusion(f32[128,300]{0,1:T(8,128)} %param.9, f32[256,300]{0,1:T(8,128)} %copy-done.4, f32[128,300]{0,1:T(8,128)} %copy-done.3, f32[128,300]{0,1:T(8,128)S(1)} %get-tuple-element.10, bf16[128,128]{1,0:T(8,128)(2,1)} %get-tuple-element.21, bf16[128,128]{1,0:T(8,128)(2,1)S(1)} %get-tuple-element.19, ...), kind=kOutput, calls=%fused_computation.11 | convolution fusion | flops 236837888 | bytes 1052672 | tf_op jit(solution)/shard_map/dot_general | solution.py:126
  (54 shorter events, 4.2 us)
Async XLA Ops:
  0.6 2.2 %copy-start = (bf16[512,2048]{1,0:T(8,128)(2,1)S(1)}, bf16[512,2048]{1,0:T(8,128)(2,1)}, u32[]{:S(2)}) copy-start(bf16[512,2048]{1,0:T(8,128)(2,1)} %param.6) | copy-start | bytes 6291460
  5.2 5.8 %collective-permute-start = (bf16[2,128,2048]{2,1,0:T(8,128)(2,1)}, bf16[2,128,2048]{2,1,0:T(8,128)(2,1)}, u32[]{:S(2)}, u32[]{:S(2)}) collective-permute-start(bf16[2,128,2048]{2,1,0:T(8,128)(2,1)} %bitcast.8), channel_id=1, source_target_pairs={{0,1},{1,0},{2,3},{3,2},{4,5},{5,4},{6,7},{7,6},{8,9},{9,8},{10,11... | collective-permute-start | bytes 3145736 | tf_op jit(solution)/shard_map/ppermute | solution.py:18
  8.4 1.4 copy-start.7
  13.5 21.4 %all-to-all-start = ((bf16[16,2,8,2048]{3,2,1,0:T(8,128)(2,1)}), bf16[16,2,8,2048]{3,2,1,0:T(8,128)(2,1)S(1)}, u32[]{:S(2)}, u32[]{:S(2)}) async-start(bf16[16,2,8,2048]{3,2,1,0:T(8,128)(2,1)} %copy.63), calls=%async_computation | async-start | bytes 2097152 | tf_op jit(solution)/shard_map/all_to_all | solution.py:22
  35.8 23.4 %all-to-all-start.1 = ((bf16[8,2,8,2048]{3,2,1,0:T(8,128)(2,1)}), bf16[8,2,8,2048]{3,2,1,0:T(8,128)(2,1)S(1)}, u32[]{:S(2)}, u32[]{:S(2)}) async-start(bf16[8,2,8,2048]{3,2,1,0:T(8,128)(2,1)} %broadcast_in_dim.37), calls=%async_computation.1 | async-start | bytes 1048576 | tf_op jit(solution)/shard_map/all_to_all | solution.py:22
  44.0 30.4 %collective-permute-start.1 = (bf16[128,2048]{1,0:T(8,128)(2,1)}, bf16[128,2048]{1,0:T(8,128)(2,1)}, u32[]{:S(2)}, u32[]{:S(2)}) collective-permute-start(bf16[128,2048]{1,0:T(8,128)(2,1)} %param.8), channel_id=1, source_target_pairs={{0,1},{1,0},{2,3},{3,2},{4,5},{5,4},{6,7},{7,6},{8,9},{9,8},{10,11... | collective-permute-start | bytes 1572872 | tf_op jit(solution)/shard_map/ppermute | solution.py:18
  60.4 23.4 %all-to-all-start.2 = ((bf16[16,2,8,2048]{3,2,1,0:T(8,128)(2,1)}), bf16[16,2,8,2048]{3,2,1,0:T(8,128)(2,1)S(1)}, u32[]{:S(2)}, u32[]{:S(2)}) async-start(bf16[16,2,8,2048]{3,2,1,0:T(8,128)(2,1)} %broadcast_in_dim.38), calls=%async_computation.2 | async-start | bytes 2097152 | tf_op jit(solution)/shard_map/all_to_all | solution.py:22
  67.6 18.3 %collective-permute-start.3 = (f32[128,300]{0,1:T(8,128)}, f32[128,300]{0,1:T(8,128)}, u32[]{:S(2)}, u32[]{:S(2)}) collective-permute-start(f32[128,300]{0,1:T(8,128)} %param.9), channel_id=1, source_target_pairs={{0,1},{1,0},{2,3},{3,2},{4,5},{5,4},{6,7},{7,6},{8,9},{9,8},{10,11... | collective-permute-start | bytes 460808 | tf_op jit(solution)/shard_map/ppermute | solution.py:18
  71.4 18.5 %collective-permute-start.4 = (bf16[2,128,300]{2,1,0:T(8,128)(2,1)}, bf16[2,128,300]{2,1,0:T(8,128)(2,1)}, u32[]{:S(2)}, u32[]{:S(2)}) collective-permute-start(bf16[2,128,300]{2,1,0:T(8,128)(2,1)} %bitcast.62), channel_id=1, source_target_pairs={{0,1},{1,0},{2,3},{3,2},{4,5},{5,4},{6,7},{7,6},{8,9},{9,8},{10,11... | collective-permute-start | bytes 460808 | tf_op jit(solution)/shard_map/ppermute | solution.py:18
  75.5 1.0 copy-start.1
  84.2 1.2 copy-start.2
  85.4 4.5 %copy-start.5 = (bf16[256,300]{1,0:T(8,128)(2,1)S(1)}, bf16[256,300]{1,0:T(8,128)(2,1)}, u32[]{:S(2)}) copy-start(bf16[256,300]{1,0:T(8,128)(2,1)} %gather_fusion.2) | copy-start | bytes 460804
  87.5 3.5 %collective-permute-start.2 = (bf16[256,256]{1,0:T(8,128)(2,1)S(1)}, bf16[256,256]{1,0:T(8,128)(2,1)S(1)}, u32[]{:S(2)}, u32[]{:S(2)}) collective-permute-start(bf16[256,256]{1,0:T(8,128)(2,1)S(1)} %pad_maximum_fusion.2), channel_id=1, source_target_pairs={{0,1},{1,0},{2,3},{3,2},{4,5},{5,4},{6,7},{7,6},{8,9},{9,8},{10,11... | collective-permute-start | bytes 393224 | tf_op jit(solution)/shard_map/ppermute | solution.py:18
  116.7 12.3 %all-to-all-start.5 = ((f32[16,8,856]{2,1,0:T(8,128)}), f32[16,8,856]{2,1,0:T(8,128)S(1)}, u32[]{:S(2)}, u32[]{:S(2)}) async-start(f32[16,8,856]{2,1,0:T(8,128)} %broadcast_in_dim.43), calls=%async_computation.5 | async-start | bytes 917504 | tf_op jit(solution)/shard_map/all_to_all | solution.py:22
  129.2 5.6 %collective-permute-start.5 = (f32[128,856]{0,1:T(8,128)S(1)}, f32[128,856]{0,1:T(8,128)S(1)}, u32[]{:S(2)}, u32[]{:S(2)}) collective-permute-start(f32[128,856]{0,1:T(8,128)S(1)} %copy.68), channel_id=1, source_target_pairs={{0,1},{1,0},{2,3},{3,2},{4,5},{5,4},{6,7},{7,6},{8,9},{9,8},{10,11... | collective-permute-start | bytes 1314824 | tf_op jit(solution)/shard_map/ppermute | solution.py:18
  134.8 0.8 copy-start.6
  135.6 9.1 %copy-start.3 = (f32[128,300]{0,1:T(8,128)}, f32[128,300]{0,1:T(8,128)S(1)}, u32[]{:S(2)}) copy-start(f32[128,300]{0,1:T(8,128)S(1)} %get-tuple-element.12) | copy-start | bytes 460804
  139.8 4.8 %copy-start.4 = (f32[256,300]{0,1:T(8,128)}, f32[256,300]{0,1:T(8,128)S(1)}, u32[]{:S(2)}) copy-start(f32[256,300]{0,1:T(8,128)S(1)} %maximum_subtract_fusion) | copy-start | bytes 921604

commit v2 on v1

v2 whole, which is shorter than its diff:
```python
import functools
import math

import jax
import jax.numpy as jnp
from jax import lax
from jax.experimental import pallas as pl
from jax.experimental.pallas import tpu as pltpu
from jax.sharding import Mesh
from jax.sharding import PartitionSpec as P

ITERS = 2
AXES = ("y", "z", "x", "core")
PLANE = ("y", "x")
EPSILON = 1e-06
STEP_RATE = 0.2
PAIR = [(0, 1), (1, 0)]
Z_MASKS = (1, 2, 6)
HIGHEST = lax.Precision.HIGHEST
NT = (((1,), (1,)), ((), ()))


def swap(value):
    return lax.ppermute(value, "core", PAIR)


def exchange(blocks, axes):
    return lax.all_to_all(blocks, axes, 0, 0, tiled=True)


def copies(value, axes):
    size = lax.axis_size(axes)
    return exchange(jnp.broadcast_to(value[None], (size, *value.shape)), axes)


def squares(value):
    return jnp.sum(jnp.square(value.astype(jnp.float32)), axis=1)


def aligned(size):
    return -(-size // 8) * 8


def tile_kernel(batch, own, other, own_norms, other_norms, tile, *, each, factor):
    lines = batch[...]
    norms = jnp.sqrt(
        jnp.sum(jnp.square(lines.astype(jnp.float32)), axis=1, keepdims=True) + EPSILON
    )
    count = lines.shape[0] // ITERS
    width = own.shape[0]
    for at, (centers, center_norms) in enumerate(((own, own_norms), (other, other_norms))):
        dots = lax.dot_general(lines, centers[...], NT, preferred_element_type=jnp.float32)
        scaled = dots / (norms * center_norms[...]) * factor
        value = scaled + scaled * scaled * scaled / 3.0
        value = value.reshape(count // each, ITERS, each, width)
        for t in range(ITERS):
            tile[t, :, at * width : (at + 1) * width] = (
                value[:, t].reshape(count, width).astype(tile.dtype)
            )


def partial_kernel(core, tile, came, own, other, held, lines, *, root_scale):
    outs, width = own.shape
    count = tile.shape[1]
    step = aligned(outs)
    lines[...] = jnp.zeros_like(lines)
    for t in range(ITERS):
        total = lax.dot_general(
            own[...],
            tile[t, :, :width].astype(jnp.float32),
            NT,
            precision=HIGHEST,
            preferred_element_type=jnp.float32,
        ) + lax.dot_general(
            other[...],
            tile[t, :, width:].astype(jnp.float32),
            NT,
            precision=HIGHEST,
            preferred_element_type=jnp.float32,
        )
        lines[t * step : t * step + outs, :] = total / root_scale - held[
            :, t * count : (t + 1) * count
        ].astype(jnp.float32)
    mine = tile[0]
    theirs = jnp.concatenate([came[0, :, width:], came[0, :, :width]], axis=1)
    later = tile[1]
    gram = [
        lax.dot_general(value, later, NT, preferred_element_type=jnp.float32)
        for value in (mine, theirs)
    ]
    is_first = core[0] == 0
    lines[2 * step : 2 * step + count, :] = jnp.where(is_first, gram[0], gram[1])
    lines[2 * step + count : 2 * step + 2 * count, :] = jnp.where(is_first, gram[1], gram[0])


def finish_kernel(core, mine, other, tile, came, coefficients, trained, residuals, *, total):
    outs, width = coefficients.shape
    count = mine.shape[1]
    step = aligned(outs)
    is_first = core[0] == 0

    def both(start, size):
        kept, sent = mine[start : start + size, :], other[start : start + size, :]
        return jnp.concatenate(
            [jnp.where(is_first, kept, sent), jnp.where(is_first, sent, kept)], axis=1
        )

    first = both(0, outs)
    gram = both(2 * step, 2 * count)
    second = both(step, outs) - STEP_RATE / total * jnp.dot(
        first, gram, precision=HIGHEST, preferred_element_type=jnp.float32
    )
    update = None
    for t, residual in enumerate((first, second)):
        residuals[:, t, :] = residual
        kept = tile[t, :, :width].astype(jnp.float32)
        sent = came[t, :, width:].astype(jnp.float32)
        rows = jnp.concatenate(
            [jnp.where(is_first, kept, sent), jnp.where(is_first, sent, kept)], axis=0
        )
        term = jnp.dot(residual, rows, precision=HIGHEST, preferred_element_type=jnp.float32)
        update = term if update is None else update + term
    trained[...] = coefficients[...] - STEP_RATE / math.sqrt(total) * update


def whole_specs(kinds):
    return [pl.BlockSpec(memory_space=kind) for kind in kinds]


def call(kernel, out_shape, operands, scalars=0):
    kinds = [pltpu.SMEM] * scalars + [pltpu.VMEM] * (len(operands) - scalars)
    outs = out_shape if isinstance(out_shape, tuple) else (out_shape,)
    specs = tuple(whole_specs([pltpu.VMEM] * len(outs)))
    operands = operands[:scalars] + tuple(
        pltpu.with_memory_space_constraint(value, pltpu.VMEM) for value in operands[scalars:]
    )
    return pl.pallas_call(
        kernel,
        in_specs=whole_specs(kinds),
        out_specs=specs if isinstance(out_shape, tuple) else specs[0],
        out_shape=out_shape,
    )(*operands)


def body(spectra, targets, centers, coefficients, owners, batch_rows):
    width, features = centers.shape
    held_rows = targets.shape[0]
    outs = coefficients.shape[1]
    batch = batch_rows.shape[1]
    half = batch // 2
    factor = math.sqrt(features)
    total = width * lax.axis_size(AXES)
    root_scale = math.sqrt(total)
    sizes = [lax.axis_size(name) for name in AXES]
    y, z, x, core = (lax.axis_index(name) for name in AXES)
    roots = [owners[t] for t in range(ITERS)]
    bits = [size.bit_length() - 1 for size in sizes]
    root_core = [root & (sizes[3] - 1) for root in roots]
    root_x = [root >> bits[3] & (sizes[2] - 1) for root in roots]
    root_z = [root >> (bits[3] + bits[2]) & (sizes[1] - 1) for root in roots]
    root_y = [root >> (bits[3] + bits[2] + bits[1]) for root in roots]
    root_plane = [root_y[t] * sizes[2] + root_x[t] for t in range(ITERS)]
    own_root = [root_core[t] == core for t in range(ITERS)]
    on_root = [(root_y[t] == y) & (root_z[t] == z) & (root_x[t] == x) for t in range(ITERS)]
    plane = sizes[0] * sizes[2]
    each = half // plane

    halves = batch_rows.reshape(ITERS, 2, half)
    kept_rows = jnp.where(core == 0, halves[:, 0], halves[:, 1])
    sent_rows = jnp.where(core == 0, halves[:, 1], halves[:, 0])

    def spread(kept, sent, own):
        slots = kept.shape[0]

        def take(rows):
            order = jnp.swapaxes(rows.reshape(slots, plane, each), 0, 1).reshape(-1)
            return spectra.at[order].get(mode="promise_in_bounds")

        mine = take(kept).reshape(plane, slots, each, features)
        came = swap(take(sent)).reshape(plane, slots, each, features)
        return exchange(jnp.where(own.reshape(1, slots, 1, 1), mine, came), PLANE)

    def pick(scattered, slot):
        return jnp.stack(
            [
                lax.dynamic_index_in_dim(
                    scattered[:, slot[t]], root_plane[t], 0, False, allow_negative_indices=False
                )
                for t in range(ITERS)
            ]
        )

    def spread_one():
        later = on_root[1]
        return pick(
            spread(
                jnp.where(later, kept_rows[1], kept_rows[0])[None],
                jnp.where(later, sent_rows[1], sent_rows[0])[None],
                jnp.where(later, own_root[1], own_root[0])[None],
            ),
            (0, 0),
        )

    def spread_both():
        return pick(spread(kept_rows, sent_rows, jnp.stack(own_root)), (0, 1))

    piece = lax.cond(roots[0] >> bits[3] != roots[1] >> bits[3], spread_one, spread_both)

    apart = [z ^ root_z[t] for t in range(ITERS)]
    high = [apart[t] >> 2 for t in range(ITERS)]
    rest = [apart[t] ^ (Z_MASKS[2] * high[t]) for t in range(ITERS)]
    reached = [
        [rest[t] + high[t] == 0 for t in range(ITERS)],
        [(rest[t] >> 1) + high[t] == 0 for t in range(ITERS)],
        [high[t] == 0 for t in range(ITERS)],
    ]
    for mask, have in zip(Z_MASKS, reached):
        arrived = lax.ppermute(piece, "z", [(i, i ^ mask) for i in range(sizes[1])])
        piece = jnp.where(jnp.stack(have).reshape(ITERS, 1, 1), piece, arrived)
    gathered = copies(piece, PLANE).reshape(ITERS * half, features)

    def targets_of(rows):
        spots = (
            lax.broadcasted_iota(jnp.int32, (held_rows, ITERS * half), 0) == rows.reshape(1, -1)
        ).astype(targets.dtype)
        return lax.dot_general(
            targets, spots, (((0,), (0,)), ((), ())), preferred_element_type=jnp.float32
        ).astype(targets.dtype)

    def by_iteration(flags):
        return jnp.repeat(jnp.stack(flags), half).reshape(1, -1)

    held = jnp.where(by_iteration(own_root), targets_of(kept_rows), swap(targets_of(sent_rows)))
    held = jnp.where(by_iteration(on_root), held, 0).astype(targets.dtype)

    turned = coefficients.T
    turned_other = swap(turned)
    other_centers = swap(centers)
    norms = [jnp.sqrt(squares(value) + EPSILON).reshape(1, -1) for value in (centers, other_centers)]

    tile = call(
        functools.partial(tile_kernel, each=each, factor=factor),
        pltpu.VMEM((ITERS, half, 2 * width), jnp.bfloat16),
        (gathered, centers, other_centers, *norms),
    )
    came = swap(tile)
    at = core.reshape(1)
    height = -(-(2 * aligned(outs) + batch) // (8 * plane)) * 8
    lines = call(
        functools.partial(partial_kernel, root_scale=root_scale),
        pltpu.VMEM((plane * height, half), jnp.float32),
        (at, tile, came, turned, turned_other, held),
        scalars=1,
    )
    own = exchange(lines.reshape(plane, height, half), PLANE).sum(axis=0)
    own = copies(own, "z").sum(axis=0)
    whole = copies(own, PLANE).reshape(plane * height, half)
    trained, residuals = call(
        functools.partial(finish_kernel, total=total),
        (
            jax.ShapeDtypeStruct((outs, width), jnp.float32),
            jax.ShapeDtypeStruct((outs, ITERS, batch), jnp.float32),
        ),
        (at, whole, swap(whole), tile, came, turned),
        scalars=1,
    )
    return trained.T, jnp.transpose(residuals, (1, 2, 0))


def solution(mesh):
    torus = Mesh(mesh.devices.reshape(4, 8, 4, 2), AXES)
    return jax.shard_map(
        body,
        mesh=torus,
        in_specs=(P(AXES, None), P(AXES, None), P(AXES, None), P(AXES, None), P(), P()),
        out_specs=(P(AXES, None), P()),
        check_vma=False,
    )
```

time: 151 us -> 124 us (0.82)
  blocking collectives: 24.4 us -> 55.8 us
  local copies, waits for them, and re-layouts: 31 us -> 9.22 us
  waiting for transfers between devices: 37.6 us -> 19.8 us
  starting transfers between devices: 37.2 us -> 26.7 us
  matrix products: 5.61 us -> 0.6 us
  Pallas kernels: 0 us -> 3.69 us
  other arithmetic: 5.2 us -> 1.87 us
  between operations: 8.66 us -> 6.01 us
    all_to_all x2 -> x4, blocking collectives: 24.4 us -> 55.8 us  [exchange(): return lax.all_to_all(blocks, axes, 0, 0, tiled=True)]
    all_to_all x4 -> x1, waiting for transfers between devices: 36.3 us -> 13.6 us  [exchange(): return lax.all_to_all(blocks, axes, 0, 0, tiled=True)]
    all_to_all x4 -> x1, starting transfers between devices: 24.2 us -> 3.65 us  [exchange(): return lax.all_to_all(blocks, axes, 0, 0, tiled=True)]
    ppermute x0 -> x3, starting transfers between devices: none -> 8.72 us  [body(): arrived = lax.ppermute(piece, 'z', [(i, i ^ mask) for i in range(sizes[1])])]
    unnamed x19 -> x6, local copies, waits for them, and re-layouts: 5.14 us -> 0.02 us
    dot_general x5 -> x2, matrix products: 5.61 us -> 0.6 us  [targets_of(): lax.dot_general(targets, spots, (((0,), (0,)), ((), ())), preferred_eleme...]
    ppermute x0 -> x3, waiting for transfers between devices: none -> 4.15 us  [body(): arrived = lax.ppermute(piece, 'z', [(i, i ^ mask) for i in range(sizes[1])])]
    pallas_call x0 -> x3, Pallas kernels: none -> 3.69 us  [call(): pl.pallas_call(kernel, in_specs=whole_specs(kinds), out_specs=specs if is...]
  transfers between devices with their start and end apart: 10 -> 10, of which waited for: 6 -> 5; matrix products, arithmetic and copies ran while one was open for 11% -> 5% of each run, Pallas kernels for 0% -> 1%
where the time goes in v2:
time: 124 us
  blocking collectives  55.8 us (45%)
  starting transfers between devices  26.7 us (22%)
  waiting for transfers between devices  19.8 us (16%)
  local copies, waits for them, and re-layouts  9.22 us (7%)
  between operations  6.01 us (5%)
  Pallas kernels  3.69 us (3%)
  other arithmetic  1.87 us (2%)
    all_to_all x4, blocking collectives, exchange(): return lax.all_to_all(blocks, axes, 0, 0, tiled=True)  55.8 us
    ppermute x6, starting transfers between devices, swap(): return lax.ppermute(value, 'core', PAIR)  14.3 us
    all_to_all x1, waiting for transfers between devices, exchange(): return lax.all_to_all(blocks, axes, 0, 0, tiled=True)  13.6 us
    ppermute x3, starting transfers between devices, body(): arrived = lax.ppermute(piece, 'z', [(i, i ^ mask) for i in range(sizes[1])])  8.72 us
    gather x2, local copies, waits for them, and re-layouts, take(): return spectra.at[order].get(mode='promise_in_bounds')  6.67 us
    ppermute x3, waiting for transfers between devices, body(): arrived = lax.ppermute(piece, 'z', [(i, i ^ mask) for i in range(sizes[1])])  4.15 us
    pallas_call x3, Pallas kernels, call(): pl.pallas_call(kernel, in_specs=whole_specs(kinds), out_specs=specs if is...  3.69 us
    all_to_all x1, starting transfers between devices, exchange(): return lax.all_to_all(blocks, axes, 0, 0, tiled=True)  3.65 us
  transfers between devices with their start and end apart: 10, of which 5 were waited for; matrix products, arithmetic and copies ran while one was open for 5% of the time, Pallas kernels for 1%

profile of v2, /device:TPU:1, one launch (start us, length us, event | category | flops | bytes accessed | tf_op | source)
XLA Modules:
  0.0 123.7 jit_solution(16242359220254358098)
XLA Ops:
  0.6 0.0 copy-start
  0.6 1.3 %fusion.15 = (s32[1]{0:T(128)}, s32[1]{0:T(128)}) fusion(s32[2]{0:T(128)} %param.12), kind=kLoop, calls=%fused_computation.58 | loop fusion | bytes 16 | tf_op jit(solution)/shard_map/slice | solution.py:156
  6.5 0.7 fusion.10
  7.2 26.0 %conditional.1 = (bf16[2,8,2048]{2,1,0:T(8,128)(2,1)S(1)}) conditional(s32[]{:T(128)} %bitcast.27, (pred[]{:T(512)}, pred[]{:T(512)}, s32[2,128]{1,0:T(2,128)S(1)}, bf16[512,2048]{1,0:T(8,128)(2,1)}, s32[2,128]{1,0:T(2,128)S(1)}, /*index=5*/s32[]{:T(128)}, s32[]{:T(128)}) %tuple.14, (pred[]{:T(512)}, pred[]{:T(512)}, pred[]{:T(512)}, ...), branch_computations={%region_0.1_spmd, %region_1.2_spmd} | conditional | flops 560642 | bytes 16019518 | solution.py:207
  7.3 3.4 %gather_fusion.1 = bf16[128,2048]{1,0:T(8,128)(2,1)S(1)} fusion(bf16[512,2048]{1,0:T(8,128)(2,1)} %get-tuple-element.43, s32[1024]{0:T(1024)S(1)} %pad_clamp_fusion.2), kind=kCustom, calls=%fused_computation.3 | custom fusion | bytes 1049088 | tf_op jit(solution)/shard_map/cond/branch_1_fun/gather | solution.py:177
  10.6 3.3 %collective-permute-start = (bf16[128,2048]{1,0:T(8,128)(2,1)S(1)}, bf16[128,2048]{1,0:T(8,128)(2,1)S(1)}, u32[]{:S(2)}, u32[]{:S(2)}) collective-permute-start(bf16[128,2048]{1,0:T(8,128)(2,1)S(1)} %gather_fusion.1), channel_id=1, source_target_pairs={{0,1},{1,0},{2,3},{3,2},{4,5},{5,4},{6,7},{7,6},{8,9},{9,8},{10,11... | collective-permute-start | bytes 1572872 | tf_op jit(solution)/shard_map/cond/branch_1_fun/ppermute | solution.py:24
  13.9 3.3 %gather_fusion = bf16[128,2048]{1,0:T(8,128)(2,1)S(1)} fusion(bf16[512,2048]{1,0:T(8,128)(2,1)} %get-tuple-element.43, s32[1024]{0:T(1024)S(1)} %pad_clamp_fusion.3), kind=kCustom, calls=%fused_computation.2 | custom fusion | bytes 1049088 | tf_op jit(solution)/shard_map/cond/branch_1_fun/gather | solution.py:177
  17.3 0.0 collective-permute-done
  17.3 0.1 select_bitcast_fusion
  17.3 15.9 %all_to_all.29 = bf16[16,1,8,2048]{3,2,1,0:T(8,128)(2,1)S(1)} all-to-all(bf16[16,1,8,2048]{3,2,1,0:T(8,128)(2,1)S(1)} %select_bitcast_fusion), channel_id=1, replica_groups=mesh['y'=4,'z'=8,'x'=4,'core'=2] {'y','x'}, dimensions={0} | all-to-all | bytes 1048576 | tf_op jit(solution)/shard_map/cond/branch_1_fun/all_to_all | solution.py:28
  33.2 1.7 %collective-permute-start.2 = (bf16[2,8,2048]{2,1,0:T(8,128)(2,1)S(1)}, bf16[2,8,2048]{2,1,0:T(8,128)(2,1)S(1)}, u32[]{:S(2)}, u32[]{:S(2)}) collective-permute-start(bf16[2,8,2048]{2,1,0:T(8,128)(2,1)S(1)} %get-tuple-element.68), channel_id=1, source_target_pairs={{0,8},{8,0},{16,24},{24,16},{32,40},{40,32},{48,56},{56,48},{1,9},... | collective-permute-start | bytes 196616 | tf_op jit(solution)/shard_map/ppermute | solution.py:218
  35.0 1.7 %collective-permute-start.5 = (bf16[128,2048]{1,0:T(8,128)(2,1)S(1)}, bf16[128,2048]{1,0:T(8,128)(2,1)S(1)}, u32[]{:S(2)}, u32[]{:S(2)}) collective-permute-start(bf16[128,2048]{1,0:T(8,128)(2,1)S(1)} %copy-done.1), channel_id=1, source_target_pairs={{0,1},{1,0},{2,3},{3,2},{4,5},{5,4},{6,7},{7,6},{8,9},{9,8},{10,11... | collective-permute-start | bytes 1572872 | tf_op jit(solution)/shard_map/ppermute | solution.py:24
  36.7 0.3 fusion.7
  37.0 0.1 collective-permute-start.8
  37.1 0.5 collective-permute-start.7
  38.3 0.2 multiply_reduce_fusion.1
  38.5 0.1 pad_add_fusion.3
  38.6 0.0 collective-permute-done.2
  38.6 0.1 broadcast_select_fusion.3
  38.7 3.2 %collective-permute-start.3 = (bf16[2,8,2048]{2,1,0:T(8,128)(2,1)S(1)}, bf16[2,8,2048]{2,1,0:T(8,128)(2,1)S(1)}, u32[]{:S(2)}, u32[]{:S(2)}) collective-permute-start(bf16[2,8,2048]{2,1,0:T(8,128)(2,1)S(1)} %broadcast_select_fusion.3), channel_id=1, source_target_pairs={{0,16},{8,24},{16,0},{24,8},{32,48},{40,56},{48,32},{56,40},{1,17}... | collective-permute-start | bytes 196616 | tf_op jit(solution)/shard_map/ppermute | solution.py:218
  41.9 0.1 pad_add_fusion.2
  41.9 2.4 %collective-permute-done.3 = bf16[2,8,2048]{2,1,0:T(8,128)(2,1)S(1)} collective-permute-done((bf16[2,8,2048]{2,1,0:T(8,128)(2,1)S(1)}, bf16[2,8,2048]{2,1,0:T(8,128)(2,1)S(1)}, u32[]{:S(2)}, u32[]{:S(2)}) %collective-permute-start.3) | collective-permute-done | bytes 65568 | tf_op jit(solution)/shard_map/ppermute | solution.py:218
  44.4 0.1 broadcast_select_fusion.4
  44.4 3.8 %collective-permute-start.4 = (bf16[2,8,2048]{2,1,0:T(8,128)(2,1)S(1)}, bf16[2,8,2048]{2,1,0:T(8,128)(2,1)S(1)}, u32[]{:S(2)}, u32[]{:S(2)}) collective-permute-start(bf16[2,8,2048]{2,1,0:T(8,128)(2,1)S(1)} %broadcast_select_fusion.4), channel_id=1, source_target_pairs={{0,48},{8,56},{16,32},{24,40},{32,16},{40,24},{48,0},{56,8},{1,49}... | collective-permute-start | bytes 196616 | tf_op jit(solution)/shard_map/ppermute | solution.py:218
  48.2 0.1 pad_add_fusion.1
  48.3 1.7 %collective-permute-done.4 = bf16[2,8,2048]{2,1,0:T(8,128)(2,1)S(1)} collective-permute-done((bf16[2,8,2048]{2,1,0:T(8,128)(2,1)S(1)}, bf16[2,8,2048]{2,1,0:T(8,128)(2,1)S(1)}, u32[]{:S(2)}, u32[]{:S(2)}) %collective-permute-start.4) | collective-permute-done | bytes 65568 | tf_op jit(solution)/shard_map/ppermute | solution.py:218
  50.0 0.1 broadcast_select_fusion.5
  50.1 1.1 broadcast_in_dim.90
  51.2 3.7 %all-to-all-start.2 = ((bf16[16,2,8,2048]{3,2,1,0:T(8,128)(2,1)}), bf16[16,2,8,2048]{3,2,1,0:T(8,128)(2,1)S(1)}, u32[]{:S(2)}, u32[]{:S(2)}) async-start(bf16[16,2,8,2048]{3,2,1,0:T(8,128)(2,1)} %broadcast_in_dim.90), calls=%async_computation.2 | async-start | bytes 2097152 | tf_op jit(solution)/shard_map/all_to_all | solution.py:28
  54.9 0.1 pad_add_fusion.4
  54.9 0.1 pad_add_fusion.5
  55.0 0.1 broadcast_bitcast_fusion
  55.1 0.0 collective-permute-done.5.other
  55.1 0.2 multiply_reduce_fusion
  55.3 13.6 %all-to-all-done.2 = bf16[16,2,8,2048]{3,2,1,0:T(8,128)(2,1)S(1)} async-done(((bf16[16,2,8,2048]{3,2,1,0:T(8,128)(2,1)}), bf16[16,2,8,2048]{3,2,1,0:T(8,128)(2,1)S(1)}, u32[]{:S(2)}, u32[]{:S(2)}) %all-to-all-start.2) | async-done | bytes 1048608 | tf_op jit(solution)/shard_map/all_to_all | solution.py:28
  68.9 0.7 shard_map.77.tile
  69.6 4.6 %collective-permute-start.6 = (bf16[2,128,256]{2,1,0:T(8,128)(2,1)S(1)}, bf16[2,128,256]{2,1,0:T(8,128)(2,1)S(1)}, u32[]{:S(2)}, u32[]{:S(2)}) collective-permute-start(bf16[2,128,256]{2,1,0:T(8,128)(2,1)S(1)} %shard_map.77.tile), channel_id=1, source_target_pairs={{0,1},{1,0},{2,3},{3,2},{4,5},{5,4},{6,7},{7,6},{8,9},{9,8},{10,11... | collective-permute-start | bytes 393224 | tf_op jit(solution)/shard_map/ppermute | solution.py:24
  74.2 0.0 collective-permute-done.8
  74.2 0.3 fusion.6.held
  74.5 0.0 collective-permute-done.7.other
  74.5 0.7 collective-permute-done.6.came
  75.2 0.7 shard_map.78
  75.9 12.7 %all_to_all.30 = f32[16,56,128]{2,1,0:T(8,128)S(1)} all-to-all(f32[16,56,128]{2,1,0:T(8,128)S(1)} %bitcast.92), channel_id=1, replica_groups=mesh['y'=4,'z'=8,'x'=4,'core'=2] {'y','x'}, dimensions={0} | all-to-all | bytes 917504 | tf_op jit(solution)/shard_map/all_to_all | solution.py:28
  88.6 14.9 %all_to_all.31 = f32[8,56,128]{2,1,0:T(8,128)S(1)} all-to-all(f32[8,56,128]{2,1,0:T(8,128)S(1)} %broadcast_in_dim.98), channel_id=1, replica_groups=mesh['y'=4,'z'=8,'x'=4,'core'=2] {'z'}, dimensions={0} | all-to-all | bytes 458752 | tf_op jit(solution)/shard_map/all_to_all | solution.py:28
  103.5 12.3 %all_to_all.32 = f32[16,56,128]{2,1,0:T(8,128)S(1)} all-to-all(f32[16,56,128]{2,1,0:T(8,128)S(1)} %broadcast_in_dim.99), channel_id=1, replica_groups=mesh['y'=4,'z'=8,'x'=4,'core'=2] {'y','x'}, dimensions={0} | all-to-all | bytes 917504 | tf_op jit(solution)/shard_map/all_to_all | solution.py:28
  115.9 4.1 %collective-permute-start.9 = (f32[896,128]{1,0:T(8,128)S(1)}, f32[896,128]{1,0:T(8,128)S(1)}, u32[]{:S(2)}, u32[]{:S(2)}) collective-permute-start(f32[896,128]{1,0:T(8,128)S(1)} %bitcast.90), channel_id=1, source_target_pairs={{0,1},{1,0},{2,3},{3,2},{4,5},{5,4},{6,7},{7,6},{8,9},{9,8},{10,11... | collective-permute-start | bytes 1376264 | tf_op jit(solution)/shard_map/ppermute | solution.py:24
  120.0 1.4 %collective-permute-done.9.other = f32[896,128]{1,0:T(8,128)S(1)} collective-permute-done((f32[896,128]{1,0:T(8,128)S(1)}, f32[896,128]{1,0:T(8,128)S(1)}, u32[]{:S(2)}, u32[]{:S(2)}) %collective-permute-start.9) | collective-permute-done | bytes 458784 | tf_op jit(solution)/shard_map/ppermute | solution.py:24
  121.4 2.3 %shard_map.79 = (f32[300,128]{1,0:T(8,128)}, f32[300,2,256]{2,1,0:T(2,128)}) custom-call(s32[1]{0:T(128)} %bitcast.18.core, f32[896,128]{1,0:T(8,128)S(1)} %bitcast.91, f32[896,128]{1,0:T(8,128)S(1)} %collective-permute-done.9.other, bf16[2,128,256]{2,1,0:T(8,128)(2,1)S(1)} %shard_map.77.tile, bf16[2,128,256]{2,1,0:T(8,128)(2,1)S(1)} %collective-permute-done.6.came, ...), custom_call_target="tpu_custom_call" | custom-call | tf_op jit(solution)/shard_map/pallas_call | solution.py:137
  (17 shorter events, 0.2 us)
Async XLA Ops:
  0.6 36.1 %copy-start = (bf16[512,300]{0,1:T(8,128)(2,1)S(1)}, bf16[512,300]{0,1:T(8,128)(2,1)}, u32[]{:S(2)}) copy-start(bf16[512,300]{0,1:T(8,128)(2,1)} %param.9) | copy-start | bytes 921604
  7.2 27.7 %copy-start.1 = (bf16[128,2048]{1,0:T(8,128)(2,1)S(1)}, bf16[128,2048]{1,0:T(8,128)(2,1)}, u32[]{:S(2)}) copy-start(bf16[128,2048]{1,0:T(8,128)(2,1)} %own.1) | copy-start | bytes 1572868
  7.2 29.9 %copy-start.2 = (f32[128,300]{0,1:T(8,128)S(1)}, f32[128,300]{0,1:T(8,128)}, u32[]{:S(2)}) copy-start(f32[128,300]{0,1:T(8,128)} %param.11) | copy-start | bytes 460804
  10.6 6.6 %collective-permute-start = (bf16[128,2048]{1,0:T(8,128)(2,1)S(1)}, bf16[128,2048]{1,0:T(8,128)(2,1)S(1)}, u32[]{:S(2)}, u32[]{:S(2)}) collective-permute-start(bf16[128,2048]{1,0:T(8,128)(2,1)S(1)} %gather_fusion.1), channel_id=1, source_target_pairs={{0,1},{1,0},{2,3},{3,2},{4,5},{5,4},{6,7},{7,6},{8,9},{9,8},{10,11... | collective-permute-start | bytes 1572872 | tf_op jit(solution)/shard_map/cond/branch_1_fun/ppermute | solution.py:24
  33.2 5.3 %collective-permute-start.2 = (bf16[2,8,2048]{2,1,0:T(8,128)(2,1)S(1)}, bf16[2,8,2048]{2,1,0:T(8,128)(2,1)S(1)}, u32[]{:S(2)}, u32[]{:S(2)}) collective-permute-start(bf16[2,8,2048]{2,1,0:T(8,128)(2,1)S(1)} %get-tuple-element.68), channel_id=1, source_target_pairs={{0,8},{8,0},{16,24},{24,16},{32,40},{40,32},{48,56},{56,48},{1,9},... | collective-permute-start | bytes 196616 | tf_op jit(solution)/shard_map/ppermute | solution.py:218
  35.0 20.1 %collective-permute-start.5 = (bf16[128,2048]{1,0:T(8,128)(2,1)S(1)}, bf16[128,2048]{1,0:T(8,128)(2,1)S(1)}, u32[]{:S(2)}, u32[]{:S(2)}) collective-permute-start(bf16[128,2048]{1,0:T(8,128)(2,1)S(1)} %copy-done.1), channel_id=1, source_target_pairs={{0,1},{1,0},{2,3},{3,2},{4,5},{5,4},{6,7},{7,6},{8,9},{9,8},{10,11... | collective-permute-start | bytes 1572872 | tf_op jit(solution)/shard_map/ppermute | solution.py:24
  37.0 37.2 %collective-permute-start.8 = (bf16[300,256]{1,0:T(8,128)(2,1)S(1)}, bf16[300,256]{1,0:T(8,128)(2,1)S(1)}, u32[]{:S(2)}, u32[]{:S(2)}) collective-permute-start(bf16[300,256]{1,0:T(8,128)(2,1)S(1)} %fusion.7), channel_id=1, source_target_pairs={{0,1},{1,0},{2,3},{3,2},{4,5},{5,4},{6,7},{7,6},{8,9},{9,8},{10,11... | collective-permute-start | bytes 460808 | tf_op jit(solution)/shard_map/ppermute | solution.py:24
  37.1 37.4 %collective-permute-start.7 = (f32[300,128]{1,0:T(8,128)S(1)}, f32[300,128]{1,0:T(8,128)S(1)}, u32[]{:S(2)}, u32[]{:S(2)}) collective-permute-start(f32[300,128]{1,0:T(8,128)S(1)} %bitcast.93), channel_id=1, source_target_pairs={{0,1},{1,0},{2,3},{3,2},{4,5},{5,4},{6,7},{7,6},{8,9},{9,8},{10,11... | collective-permute-start | bytes 460808 | tf_op jit(solution)/shard_map/ppermute | solution.py:24
  38.7 5.7 %collective-permute-start.3 = (bf16[2,8,2048]{2,1,0:T(8,128)(2,1)S(1)}, bf16[2,8,2048]{2,1,0:T(8,128)(2,1)S(1)}, u32[]{:S(2)}, u32[]{:S(2)}) collective-permute-start(bf16[2,8,2048]{2,1,0:T(8,128)(2,1)S(1)} %broadcast_select_fusion.3), channel_id=1, source_target_pairs={{0,16},{8,24},{16,0},{24,8},{32,48},{40,56},{48,32},{56,40},{1,17}... | collective-permute-start | bytes 196616 | tf_op jit(solution)/shard_map/ppermute | solution.py:218
  44.4 5.6 %collective-permute-start.4 = (bf16[2,8,2048]{2,1,0:T(8,128)(2,1)S(1)}, bf16[2,8,2048]{2,1,0:T(8,128)(2,1)S(1)}, u32[]{:S(2)}, u32[]{:S(2)}) collective-permute-start(bf16[2,8,2048]{2,1,0:T(8,128)(2,1)S(1)} %broadcast_select_fusion.4), channel_id=1, source_target_pairs={{0,48},{8,56},{16,32},{24,40},{32,16},{40,24},{48,0},{56,8},{1,49}... | collective-permute-start | bytes 196616 | tf_op jit(solution)/shard_map/ppermute | solution.py:218
  51.2 17.7 %all-to-all-start.2 = ((bf16[16,2,8,2048]{3,2,1,0:T(8,128)(2,1)}), bf16[16,2,8,2048]{3,2,1,0:T(8,128)(2,1)S(1)}, u32[]{:S(2)}, u32[]{:S(2)}) async-start(bf16[16,2,8,2048]{3,2,1,0:T(8,128)(2,1)} %broadcast_in_dim.90), calls=%async_computation.2 | async-start | bytes 2097152 | tf_op jit(solution)/shard_map/all_to_all | solution.py:28
  69.6 5.6 %collective-permute-start.6 = (bf16[2,128,256]{2,1,0:T(8,128)(2,1)S(1)}, bf16[2,128,256]{2,1,0:T(8,128)(2,1)S(1)}, u32[]{:S(2)}, u32[]{:S(2)}) collective-permute-start(bf16[2,128,256]{2,1,0:T(8,128)(2,1)S(1)} %shard_map.77.tile), channel_id=1, source_target_pairs={{0,1},{1,0},{2,3},{3,2},{4,5},{5,4},{6,7},{7,6},{8,9},{9,8},{10,11... | collective-permute-start | bytes 393224 | tf_op jit(solution)/shard_map/ppermute | solution.py:24
  115.9 5.6 %collective-permute-start.9 = (f32[896,128]{1,0:T(8,128)S(1)}, f32[896,128]{1,0:T(8,128)S(1)}, u32[]{:S(2)}, u32[]{:S(2)}) collective-permute-start(f32[896,128]{1,0:T(8,128)S(1)} %bitcast.90), channel_id=1, source_target_pairs={{0,1},{1,0},{2,3},{3,2},{4,5},{5,4},{6,7},{7,6},{8,9},{9,8},{10,11... | collective-permute-start | bytes 1376264 | tf_op jit(solution)/shard_map/ppermute | solution.py:24

commit v3 on v2

v3 whole, which is shorter than its diff:
```python
import functools
import math

import jax
import jax.numpy as jnp
from jax import lax
from jax.experimental import pallas as pl
from jax.experimental.pallas import tpu as pltpu
from jax.sharding import Mesh
from jax.sharding import PartitionSpec as P

ITERS = 2
AXES = ("y", "z", "x", "core")
PLANE = ("y", "x")
EPSILON = 1e-06
STEP_RATE = 0.2
PAIR = [(0, 1), (1, 0)]
Z_MASKS = (1, 2, 7)
SCRATCH = 16 << 20
HIGHEST = lax.Precision.HIGHEST
NT = (((1,), (1,)), ((), ()))


def swap(value):
    return lax.ppermute(value, "core", PAIR)


def exchange(blocks, axes):
    return lax.all_to_all(blocks, axes, 0, 0, tiled=True)


def place(device, sizes):
    bits = [size.bit_length() - 1 for size in sizes]
    core = device & (sizes[3] - 1)
    x = device >> bits[3] & (sizes[2] - 1)
    z = device >> (bits[3] + bits[2]) & (sizes[1] - 1)
    return device >> (bits[3] + bits[2] + bits[1]), z, x, core


def chosen(rows, held, own):
    spots = lax.broadcasted_iota(jnp.int32, (held, rows.shape[1]), 0) == rows
    return jnp.where(spots & own, 1.0, 0.0).astype(jnp.bfloat16)


def halves_of(batch_rows, t, core):
    rows = batch_rows[pl.ds(t, 1), :] if not isinstance(t, int) else batch_rows[t : t + 1, :]
    half = rows.shape[1] // 2
    first, second = rows[:, :half], rows[:, half:]
    return jnp.where(core == 0, first, second), jnp.where(core == 0, second, first)


def copies(value, axes):
    size = lax.axis_size(axes)
    return exchange(jnp.broadcast_to(value[None], (size, *value.shape)), axes)


def squares(value):
    return jnp.sum(jnp.square(value.astype(jnp.float32)), axis=1)


def aligned(size):
    return -(-size // 8) * 8


def rows_kernel(device, owners, batch_rows, spectra, kept, sent, *flag, sizes):
    here = device[0]
    core = here & (sizes[3] - 1)
    plane, slots, each, features = kept.shape
    if flag:
        flag[0][0] = jnp.where(owners[0] // 2 != owners[1] // 2, 1, 0)
    for slot in range(slots):
        t = slot if slots > 1 else jnp.where(owners[1] // 2 == here // 2, 1, 0)
        own = owners[t] == here
        for rows, out in zip(halves_of(batch_rows, t, core), (kept, sent)):
            value = lax.dot_general(
                chosen(rows, spectra.shape[0], own),
                spectra[...],
                (((0,), (0,)), ((), ())),
                preferred_element_type=jnp.float32,
            )
            out[:, slot] = value.astype(out.dtype).reshape(plane, each, features)


def targets_kernel(device, owners, batch_rows, targets, kept, sent, *, sizes):
    here = device[0]
    core = here & (sizes[3] - 1)
    half = batch_rows.shape[1] // 2
    for t in range(ITERS):
        own = owners[t] == here
        for rows, out in zip(halves_of(batch_rows, t, core), (kept, sent)):
            out[:, t * half : (t + 1) * half] = jnp.dot(
                targets[...],
                chosen(rows, targets.shape[1], own),
                preferred_element_type=jnp.float32,
            ).astype(out.dtype)


def pick_kernel(device, owners, scattered, piece, *, sizes):
    _, z, _, _ = place(device[0], sizes)
    slots = scattered.shape[1]
    for t in range(ITERS):
        root_y, root_z, root_x, _ = place(owners[t], sizes)
        block = scattered[root_y * sizes[2] + root_x, t if slots > 1 else 0]
        piece[t] = jnp.where(root_z == z, block, jnp.zeros_like(block))


def spread_kernel(piece, arrived, out):
    out[...] = jnp.broadcast_to((piece[...] + arrived[...])[None], out.shape)


def tile_kernel(batch, own, other, own_norms, other_norms, tile, *, each, factor):
    lines = batch[...]
    norms = jnp.sqrt(
        jnp.sum(jnp.square(lines.astype(jnp.float32)), axis=1, keepdims=True) + EPSILON
    )
    count = lines.shape[0] // ITERS
    width = own.shape[0]
    for at, (centers, center_norms) in enumerate(((own, own_norms), (other, other_norms))):
        dots = lax.dot_general(lines, centers[...], NT, preferred_element_type=jnp.float32)
        scaled = dots / (norms * center_norms[...]) * factor
        value = scaled + scaled * scaled * scaled / 3.0
        value = value.reshape(count // each, ITERS, each, width)
        for t in range(ITERS):
            tile[t, :, at * width : (at + 1) * width] = (
                value[:, t].reshape(count, width).astype(tile.dtype)
            )


def partial_kernel(core, tile, came, own, other, kept, arrived, lines, *, root_scale):
    outs, width = own.shape
    count = tile.shape[1]
    step = aligned(outs)
    lines[...] = jnp.zeros_like(lines)
    held = kept[...].astype(jnp.float32) + arrived[...].astype(jnp.float32)
    for t in range(ITERS):
        total = lax.dot_general(
            own[...],
            tile[t, :, :width].astype(jnp.float32),
            NT,
            precision=HIGHEST,
            preferred_element_type=jnp.float32,
        ) + lax.dot_general(
            other[...],
            tile[t, :, width:].astype(jnp.float32),
            NT,
            precision=HIGHEST,
            preferred_element_type=jnp.float32,
        )
        lines[t * step : t * step + outs, :] = (
            total / root_scale - held[:, t * count : (t + 1) * count]
        )
    mine = tile[0]
    theirs = jnp.concatenate([came[0, :, width:], came[0, :, :width]], axis=1)
    later = tile[1]
    gram = [
        lax.dot_general(value, later, NT, preferred_element_type=jnp.float32)
        for value in (mine, theirs)
    ]
    is_first = core[0] == 0
    lines[2 * step : 2 * step + count, :] = jnp.where(is_first, gram[0], gram[1])
    lines[2 * step + count : 2 * step + 2 * count, :] = jnp.where(is_first, gram[1], gram[0])


def finish_kernel(core, mine, other, tile, came, coefficients, trained, residuals, *, total):
    outs, width = coefficients.shape
    count = mine.shape[1]
    step = aligned(outs)
    is_first = core[0] == 0

    def both(start, size):
        kept, sent = mine[start : start + size, :], other[start : start + size, :]
        return jnp.concatenate(
            [jnp.where(is_first, kept, sent), jnp.where(is_first, sent, kept)], axis=1
        )

    first = both(0, outs)
    gram = both(2 * step, 2 * count)
    second = both(step, outs) - STEP_RATE / total * jnp.dot(
        first, gram, precision=HIGHEST, preferred_element_type=jnp.float32
    )
    update = None
    for t, residual in enumerate((first, second)):
        residuals[:, t, :] = residual
        kept = tile[t, :, :width].astype(jnp.float32)
        sent = came[t, :, width:].astype(jnp.float32)
        rows = jnp.concatenate(
            [jnp.where(is_first, kept, sent), jnp.where(is_first, sent, kept)], axis=0
        )
        term = jnp.dot(residual, rows, precision=HIGHEST, preferred_element_type=jnp.float32)
        update = term if update is None else update + term
    trained[...] = coefficients[...] - STEP_RATE / math.sqrt(total) * update


def call(kernel, out_shape, operands, scalars=0, out_kinds=None):
    outs = out_shape if isinstance(out_shape, tuple) else (out_shape,)
    out_kinds = out_kinds or [pltpu.VMEM] * len(outs)
    specs = tuple(pl.BlockSpec(memory_space=kind) for kind in out_kinds)
    kinds = [pltpu.SMEM] * scalars + [pltpu.VMEM] * (len(operands) - scalars)
    operands = operands[:scalars] + tuple(
        pltpu.with_memory_space_constraint(value, pltpu.VMEM) for value in operands[scalars:]
    )
    return pl.pallas_call(
        kernel,
        in_specs=[pl.BlockSpec(memory_space=kind) for kind in kinds],
        out_specs=specs if isinstance(out_shape, tuple) else specs[0],
        out_shape=out_shape,
        compiler_params=pltpu.CompilerParams(vmem_limit_bytes=SCRATCH),
    )(*operands)


def body(spectra, targets, centers, coefficients, owners, batch_rows):
    width, features = centers.shape
    outs = coefficients.shape[1]
    batch = batch_rows.shape[1]
    half = batch // 2
    total = width * lax.axis_size(AXES)
    sizes = tuple(lax.axis_size(name) for name in AXES)
    plane = sizes[0] * sizes[2]
    each = half // plane
    device = lax.axis_index(AXES).reshape(1)
    core = lax.axis_index("core").reshape(1)
    narrow = jnp.bfloat16

    def rows_for(slots):
        block = pltpu.VMEM((plane, slots, each, features), narrow)
        flag = (jax.ShapeDtypeStruct((1,), jnp.int32),) if slots == 1 else ()
        return call(
            functools.partial(rows_kernel, sizes=sizes),
            (block, block) + flag,
            (device, owners, batch_rows, spectra),
            scalars=2,
            out_kinds=[pltpu.VMEM, pltpu.VMEM] + [pltpu.SMEM] * len(flag),
        )

    def spread(kept, sent):
        scattered = exchange(kept + swap(sent), PLANE)
        return call(
            functools.partial(pick_kernel, sizes=sizes),
            pltpu.VMEM((ITERS, each, features), narrow),
            (device, owners, scattered),
            scalars=2,
        )

    kept, sent, apart = rows_for(1)
    piece = lax.cond(apart[0] != 0, lambda: spread(kept, sent), lambda: spread(*rows_for(2)))

    arrived = None
    for mask in Z_MASKS:
        piece = piece if arrived is None else piece + arrived
        arrived = lax.ppermute(piece, "z", [(i, i ^ mask) for i in range(sizes[1])])
    spread_out = call(
        spread_kernel,
        pltpu.VMEM((plane, ITERS, each, features), narrow),
        (piece, arrived),
    )
    gathered = exchange(spread_out, PLANE).reshape(ITERS * half, features)

    shown = pltpu.VMEM((outs, ITERS * half), narrow)
    kept_targets, sent_targets = call(
        functools.partial(targets_kernel, sizes=sizes),
        (shown, shown),
        (device, owners, batch_rows, targets.T),
        scalars=2,
    )
    came_targets = swap(sent_targets)

    turned = coefficients.T
    turned_other = swap(turned)
    other_centers = swap(centers)
    norms = [jnp.sqrt(squares(value) + EPSILON).reshape(1, -1) for value in (centers, other_centers)]

    tile = call(
        functools.partial(tile_kernel, each=each, factor=math.sqrt(features)),
        pltpu.VMEM((ITERS, half, 2 * width), narrow),
        (gathered, centers, other_centers, *norms),
    )
    came = swap(tile)
    height = -(-(2 * aligned(outs) + batch) // (8 * plane)) * 8
    lines = call(
        functools.partial(partial_kernel, root_scale=math.sqrt(total)),
        pltpu.VMEM((plane * height, half), jnp.float32),
        (core, tile, came, turned, turned_other, kept_targets, came_targets),
        scalars=1,
    )
    own = exchange(lines.reshape(plane, height, half), PLANE).sum(axis=0)
    own = copies(own, "z").sum(axis=0)
    whole = copies(own, PLANE).reshape(plane * height, half)
    trained, residuals = call(
        functools.partial(finish_kernel, total=total),
        (
            jax.ShapeDtypeStruct((outs, width), jnp.float32),
            jax.ShapeDtypeStruct((outs, ITERS, batch), jnp.float32),
        ),
        (core, whole, swap(whole), tile, came, turned),
        scalars=1,
    )
    return trained.T, jnp.transpose(residuals, (1, 2, 0))


def solution(mesh):
    torus = Mesh(mesh.devices.reshape(4, 8, 4, 2), AXES)
    return jax.shard_map(
        body,
        mesh=torus,
        in_specs=(P(AXES, None), P(AXES, None), P(AXES, None), P(AXES, None), P(), P()),
        out_specs=(P(AXES, None), P()),
        check_vma=False,
    )
```

time: 124 us -> 116 us (0.935)
  local copies, waits for them, and re-layouts: 9.22 us -> 2.34 us
  starting transfers between devices: 26.7 us -> 32.9 us
  between operations: 6.01 us -> 1.45 us
  Pallas kernels: 3.69 us -> 8.04 us
  waiting for transfers between devices: 19.8 us -> 15.7 us
  other arithmetic: 1.87 us -> 0.6 us
    all_to_all x1, waiting for transfers between devices: 13.6 us -> 6.2 us  [exchange(): return lax.all_to_all(blocks, axes, 0, 0, tiled=True)]
    gather x2 -> x0, local copies, waits for them, and re-layouts: 6.67 us -> none  [take(): return spectra.at[order].get(mode='promise_in_bounds')]
    ppermute x6, starting transfers between devices: 14.3 us -> 18.9 us  [swap(): return lax.ppermute(value, 'core', PAIR)]
    pallas_call x3 -> x7, Pallas kernels: 3.69 us -> 8.04 us  [call(): pl.pallas_call(kernel, in_specs=[pl.BlockSpec(memory_space=kind) for kind...]
    unnamed x6 -> x14, local copies, waits for them, and re-layouts: 0.02 us -> 2.29 us
    ppermute x6, waiting for transfers between devices: 2.12 us -> 3.97 us  [swap(): return lax.ppermute(value, 'core', PAIR)]
    ppermute x3, starting transfers between devices: 8.72 us -> 10.4 us  [body(): arrived = lax.ppermute(piece, 'z', [(i, i ^ mask) for i in range(sizes[1])])]
    ppermute x3, waiting for transfers between devices: 4.15 us -> 5.51 us  [body(): arrived = lax.ppermute(piece, 'z', [(i, i ^ mask) for i in range(sizes[1])])]
  transfers between devices with their start and end apart: 10 -> 10, of which waited for: 5 -> 7; matrix products, arithmetic and copies ran while one was open for 5% -> 0% of each run, Pallas kernels for 1% -> 2%
where the time goes in v3:
time: 116 us
  blocking collectives  54.8 us (47%)
  starting transfers between devices  32.9 us (28%)
  waiting for transfers between devices  15.7 us (14%)
  Pallas kernels  8.04 us (7%)
  local copies, waits for them, and re-layouts  2.34 us (2%)
  between operations  1.45 us (1%)
    all_to_all x4, blocking collectives, exchange(): return lax.all_to_all(blocks, axes, 0, 0, tiled=True)  54.8 us
    ppermute x6, starting transfers between devices, swap(): return lax.ppermute(value, 'core', PAIR)  18.9 us
    ppermute x3, starting transfers between devices, body(): arrived = lax.ppermute(piece, 'z', [(i, i ^ mask) for i in range(sizes[1])])  10.4 us
    pallas_call x7, Pallas kernels, call(): pl.pallas_call(kernel, in_specs=[pl.BlockSpec(memory_space=kind) for kind...  8.04 us
    all_to_all x1, waiting for transfers between devices, exchange(): return lax.all_to_all(blocks, axes, 0, 0, tiled=True)  6.2 us
    ppermute x3, waiting for transfers between devices, body(): arrived = lax.ppermute(piece, 'z', [(i, i ^ mask) for i in range(sizes[1])])  5.51 us
    ppermute x6, waiting for transfers between devices, swap(): return lax.ppermute(value, 'core', PAIR)  3.97 us
    all_to_all x1, starting transfers between devices, exchange(): return lax.all_to_all(blocks, axes, 0, 0, tiled=True)  3.65 us
  transfers between devices with their start and end apart: 10, of which 7 were waited for; matrix products, arithmetic and copies ran while one was open for 0% of the time, Pallas kernels for 2%

profile of v3, /device:TPU:1, one launch (start us, length us, event | category | flops | bytes accessed | tf_op | source)
XLA Modules:
  0.0 115.8 jit_solution(1355008284431313412)
XLA Ops:
  0.6 0.0 copy-start.6
  0.7 0.0 copy-start
  0.7 1.6 %copy-done = bf16[512,2048]{1,0:T(8,128)(2,1)S(1)} copy-done((bf16[512,2048]{1,0:T(8,128)(2,1)S(1)}, bf16[512,2048]{1,0:T(8,128)(2,1)}, u32[]{:S(2)}) %copy-start) | copy-done | bytes 2097176
  2.2 0.7 copy-done.4
  2.9 1.7 %shard_map.77 = (bf16[16,1,8,2048]{3,2,1,0:T(8,128)(2,1)S(1)}, bf16[16,1,8,2048]{3,2,1,0:T(8,128)(2,1)S(1)}, s32[1]{0:T(128)}) custom-call(s32[1]{0:T(128)} %bitcast.1.device, s32[2]{0:T(128)} %owners.3, s32[2,256]{1,0:T(2,128)S(1)} %copy-done.4, bf16[512,2048]{1,0:T(8,128)(2,1)S(1)} %copy-done), custom_call_target="tpu_custom_call" | custom-call | tf_op jit(solution)/shard_map/pallas_call | solution.py:202
  5.3 0.0 copy-done.6
  5.3 21.1 %conditional.1 = (bf16[2,8,2048]{2,1,0:T(8,128)(2,1)S(1)}) conditional(s32[]{:T(128)} %bitcast.2, (s32[1]{0:T(128)}, s32[2]{0:T(128)S(1)}, s32[2,256]{1,0:T(2,128)S(1)}, bf16[512,2048]{1,0:T(8,128)(2,1)S(1)}) %tuple.21, (bf16[16,1,8,2048]{3,2,1,0:T(8,128)(2,1)S(1)}, bf16[16,1,8,2048]{3,2,1,0:T(8,128)(2,1)S(1)}, s32[1]{0:T(128)}, s32[2]{0:T(128)S(1)}) %tuple.22), branch_computations={%region_0.0_spmd, %region_1.0_spmd} | conditional | flops 524288 | bytes 9437232 | solution.py:245
  5.3 3.3 %collective-permute-start.1 = (bf16[16,1,8,2048]{3,2,1,0:T(8,128)(2,1)S(1)}, bf16[16,1,8,2048]{3,2,1,0:T(8,128)(2,1)S(1)}, u32[]{:S(2)}, u32[]{:S(2)}) collective-permute-start(bf16[16,1,8,2048]{3,2,1,0:T(8,128)(2,1)S(1)} %get-tuple-element.28), channel_id=1, source_target_pairs={{0,1},{1,0},{2,3},{3,2},{4,5},{5,4},{6,7},{7,6},{8,9},{9,8},{10,11... | collective-permute-start | bytes 1572872 | tf_op jit(solution)/shard_map/cond/branch_1_fun/ppermute | solution.py:25
  8.6 1.5 %collective-permute-done.1 = bf16[16,1,8,2048]{3,2,1,0:T(8,128)(2,1)S(1)} collective-permute-done((bf16[16,1,8,2048]{3,2,1,0:T(8,128)(2,1)S(1)}, bf16[16,1,8,2048]{3,2,1,0:T(8,128)(2,1)S(1)}, u32[]{:S(2)}, u32[]{:S(2)}) %collective-permute-start.1) | collective-permute-done | bytes 524320 | tf_op jit(solution)/shard_map/cond/branch_1_fun/ppermute | solution.py:25
  10.1 0.1 add.35
  10.2 15.6 %all_to_all.29.scattered = bf16[16,1,8,2048]{3,2,1,0:T(8,128)(2,1)S(1)} all-to-all(bf16[16,1,8,2048]{3,2,1,0:T(8,128)(2,1)S(1)} %add.35), channel_id=1, replica_groups=mesh['y'=4,'z'=8,'x'=4,'core'=2] {'y','x'}, dimensions={0} | all-to-all | bytes 1048576 | tf_op jit(solution)/shard_map/cond/branch_1_fun/all_to_all | solution.py:29
  25.8 0.6 branch_1_fun.1
  26.4 0.0 copy-start.1
  26.4 0.0 copy-start.2
  26.4 0.0 copy-start.3
  26.4 0.0 copy-start.5
  26.4 1.7 %collective-permute-start.2 = (bf16[2,8,2048]{2,1,0:T(8,128)(2,1)S(1)}, bf16[2,8,2048]{2,1,0:T(8,128)(2,1)S(1)}, u32[]{:S(2)}, u32[]{:S(2)}) collective-permute-start(bf16[2,8,2048]{2,1,0:T(8,128)(2,1)S(1)} %get-tuple-element.45), channel_id=1, source_target_pairs={{0,8},{8,0},{16,24},{24,16},{32,40},{40,32},{48,56},{56,48},{1,9},... | collective-permute-start | bytes 196616 | tf_op jit(solution)/shard_map/ppermute | solution.py:250
  28.2 1.7 %collective-permute-done.2 = bf16[2,8,2048]{2,1,0:T(8,128)(2,1)S(1)} collective-permute-done((bf16[2,8,2048]{2,1,0:T(8,128)(2,1)S(1)}, bf16[2,8,2048]{2,1,0:T(8,128)(2,1)S(1)}, u32[]{:S(2)}, u32[]{:S(2)}) %collective-permute-start.2) | collective-permute-done | bytes 65568 | tf_op jit(solution)/shard_map/ppermute | solution.py:250
  29.8 3.1 %collective-permute-start.3 = (bf16[2,8,2048]{2,1,0:T(8,128)(2,1)S(1)}, bf16[2,8,2048]{2,1,0:T(8,128)(2,1)S(1)}, u32[]{:S(2)}, u32[]{:S(2)}) collective-permute-start(bf16[2,8,2048]{2,1,0:T(8,128)(2,1)S(1)} %add.46), channel_id=1, source_target_pairs={{0,16},{8,24},{16,0},{24,8},{32,48},{40,56},{48,32},{56,40},{1,17}... | collective-permute-start | bytes 196616 | tf_op jit(solution)/shard_map/ppermute | solution.py:250
  32.9 1.7 %collective-permute-done.3 = bf16[2,8,2048]{2,1,0:T(8,128)(2,1)S(1)} collective-permute-done((bf16[2,8,2048]{2,1,0:T(8,128)(2,1)S(1)}, bf16[2,8,2048]{2,1,0:T(8,128)(2,1)S(1)}, u32[]{:S(2)}, u32[]{:S(2)}) %collective-permute-start.3) | collective-permute-done | bytes 65568 | tf_op jit(solution)/shard_map/ppermute | solution.py:250
  34.6 5.5 %collective-permute-start.4 = (bf16[2,8,2048]{2,1,0:T(8,128)(2,1)S(1)}, bf16[2,8,2048]{2,1,0:T(8,128)(2,1)S(1)}, u32[]{:S(2)}, u32[]{:S(2)}) collective-permute-start(bf16[2,8,2048]{2,1,0:T(8,128)(2,1)S(1)} %add.47.piece), channel_id=1, source_target_pairs={{0,56},{8,48},{16,40},{24,32},{32,24},{40,16},{48,8},{56,0},{1,57}... | collective-permute-start | bytes 196616 | tf_op jit(solution)/shard_map/ppermute | solution.py:250
  40.1 2.2 %collective-permute-done.4.arrived = bf16[2,8,2048]{2,1,0:T(8,128)(2,1)S(1)} collective-permute-done((bf16[2,8,2048]{2,1,0:T(8,128)(2,1)S(1)}, bf16[2,8,2048]{2,1,0:T(8,128)(2,1)S(1)}, u32[]{:S(2)}, u32[]{:S(2)}) %collective-permute-start.4) | collective-permute-done | bytes 65568 | tf_op jit(solution)/shard_map/ppermute | solution.py:250
  42.3 1.1 shard_map.78
  43.4 3.7 %all-to-all-start.2 = ((bf16[16,2,8,2048]{3,2,1,0:T(8,128)(2,1)}), bf16[16,2,8,2048]{3,2,1,0:T(8,128)(2,1)S(1)}, u32[]{:S(2)}, u32[]{:S(2)}) async-start(bf16[16,2,8,2048]{3,2,1,0:T(8,128)(2,1)} %shard_map.78), calls=%async_computation.2 | async-start | bytes 2097152 | tf_op jit(solution)/shard_map/all_to_all | solution.py:29
  47.1 0.0 copy-done.1
  47.1 5.0 %collective-permute-start.5 = (bf16[128,2048]{1,0:T(8,128)(2,1)S(1)}, bf16[128,2048]{1,0:T(8,128)(2,1)S(1)}, u32[]{:S(2)}, u32[]{:S(2)}) collective-permute-start(bf16[128,2048]{1,0:T(8,128)(2,1)S(1)} %copy-done.1), channel_id=1, source_target_pairs={{0,1},{1,0},{2,3},{3,2},{4,5},{5,4},{6,7},{7,6},{8,9},{9,8},{10,11... | collective-permute-start | bytes 1572872 | tf_op jit(solution)/shard_map/ppermute | solution.py:25
  52.1 0.0 copy-done.2
  52.1 0.1 collective-permute-start.7
  52.2 0.0 copy-done.3
  52.2 0.0 copy-done.5
  52.2 1.0 shard_map.80
  53.3 0.5 collective-permute-start.8
  53.8 0.2 multiply_reduce_fusion.1
  54.0 0.0 collective-permute-done.5.other
  54.0 0.2 multiply_reduce_fusion
  54.2 6.2 %all-to-all-done.2 = bf16[16,2,8,2048]{3,2,1,0:T(8,128)(2,1)S(1)} async-done(((bf16[16,2,8,2048]{3,2,1,0:T(8,128)(2,1)}), bf16[16,2,8,2048]{3,2,1,0:T(8,128)(2,1)S(1)}, u32[]{:S(2)}, u32[]{:S(2)}) %all-to-all-start.2) | async-done | bytes 1048608 | tf_op jit(solution)/shard_map/all_to_all | solution.py:29
  60.4 0.7 shard_map.79.tile
  61.1 5.7 %collective-permute-start.6 = (bf16[2,128,256]{2,1,0:T(8,128)(2,1)S(1)}, bf16[2,128,256]{2,1,0:T(8,128)(2,1)S(1)}, u32[]{:S(2)}, u32[]{:S(2)}) collective-permute-start(bf16[2,128,256]{2,1,0:T(8,128)(2,1)S(1)} %shard_map.79.tile), channel_id=1, source_target_pairs={{0,1},{1,0},{2,3},{3,2},{4,5},{5,4},{6,7},{7,6},{8,9},{9,8},{10,11... | collective-permute-start | bytes 393224 | tf_op jit(solution)/shard_map/ppermute | solution.py:25
  66.8 0.0 collective-permute-done.7.other
  66.8 0.0 collective-permute-done.8.arrived
  66.8 1.0 collective-permute-done.6.came
  67.8 0.7 shard_map.81
  68.5 12.7 %all_to_all.30 = f32[16,56,128]{2,1,0:T(8,128)S(1)} all-to-all(f32[16,56,128]{2,1,0:T(8,128)S(1)} %bitcast.17), channel_id=1, replica_groups=mesh['y'=4,'z'=8,'x'=4,'core'=2] {'y','x'}, dimensions={0} | all-to-all | bytes 917504 | tf_op jit(solution)/shard_map/all_to_all | solution.py:29
  81.3 14.5 %all_to_all.31 = f32[8,56,128]{2,1,0:T(8,128)S(1)} all-to-all(f32[8,56,128]{2,1,0:T(8,128)S(1)} %broadcast_in_dim.4), channel_id=1, replica_groups=mesh['y'=4,'z'=8,'x'=4,'core'=2] {'z'}, dimensions={0} | all-to-all | bytes 458752 | tf_op jit(solution)/shard_map/all_to_all | solution.py:29
  95.8 12.1 %all_to_all.32 = f32[16,56,128]{2,1,0:T(8,128)S(1)} all-to-all(f32[16,56,128]{2,1,0:T(8,128)S(1)} %broadcast_in_dim.5), channel_id=1, replica_groups=mesh['y'=4,'z'=8,'x'=4,'core'=2] {'y','x'}, dimensions={0} | all-to-all | bytes 917504 | tf_op jit(solution)/shard_map/all_to_all | solution.py:29
  107.9 4.2 %collective-permute-start.9 = (f32[896,128]{1,0:T(8,128)S(1)}, f32[896,128]{1,0:T(8,128)S(1)}, u32[]{:S(2)}, u32[]{:S(2)}) collective-permute-start(f32[896,128]{1,0:T(8,128)S(1)} %bitcast.15), channel_id=1, source_target_pairs={{0,1},{1,0},{2,3},{3,2},{4,5},{5,4},{6,7},{7,6},{8,9},{9,8},{10,11... | collective-permute-start | bytes 1376264 | tf_op jit(solution)/shard_map/ppermute | solution.py:25
  112.1 1.4 %collective-permute-done.9.other = f32[896,128]{1,0:T(8,128)S(1)} collective-permute-done((f32[896,128]{1,0:T(8,128)S(1)}, f32[896,128]{1,0:T(8,128)S(1)}, u32[]{:S(2)}, u32[]{:S(2)}) %collective-permute-start.9) | collective-permute-done | bytes 458784 | tf_op jit(solution)/shard_map/ppermute | solution.py:25
  113.6 2.3 %shard_map.82 = (f32[300,128]{1,0:T(8,128)}, f32[300,2,256]{2,1,0:T(2,128)}) custom-call(s32[1]{0:T(128)} %bitcast.core, f32[896,128]{1,0:T(8,128)S(1)} %bitcast.16, f32[896,128]{1,0:T(8,128)S(1)} %collective-permute-done.9.other, bf16[2,128,256]{2,1,0:T(8,128)(2,1)S(1)} %shard_map.79.tile, bf16[2,128,256]{2,1,0:T(8,128)(2,1)S(1)} %collective-permute-done.6.came, ...), custom_call_target="tpu_custom_call" | custom-call | tf_op jit(solution)/shard_map/pallas_call | solution.py:202
  (9 shorter events, 0.2 us)
Async XLA Ops:
  0.6 4.6 %copy-start.6 = (s32[2]{0:T(128)S(1)}, s32[2]{0:T(128)}, u32[]{:S(2)}) copy-start(s32[2]{0:T(128)} %owners.3) | copy-start | bytes 28
  0.7 1.6 %copy-start = (bf16[512,2048]{1,0:T(8,128)(2,1)S(1)}, bf16[512,2048]{1,0:T(8,128)(2,1)}, u32[]{:S(2)}) copy-start(bf16[512,2048]{1,0:T(8,128)(2,1)} %spectra.1) | copy-start | bytes 6291460
  2.2 0.7 copy-start.4
  5.3 4.8 %collective-permute-start.1 = (bf16[16,1,8,2048]{3,2,1,0:T(8,128)(2,1)S(1)}, bf16[16,1,8,2048]{3,2,1,0:T(8,128)(2,1)S(1)}, u32[]{:S(2)}, u32[]{:S(2)}) collective-permute-start(bf16[16,1,8,2048]{3,2,1,0:T(8,128)(2,1)S(1)} %get-tuple-element.28), channel_id=1, source_target_pairs={{0,1},{1,0},{2,3},{3,2},{4,5},{5,4},{6,7},{7,6},{8,9},{9,8},{10,11... | collective-permute-start | bytes 1572872 | tf_op jit(solution)/shard_map/cond/branch_1_fun/ppermute | solution.py:25
  26.4 20.7 %copy-start.1 = (bf16[128,2048]{1,0:T(8,128)(2,1)S(1)}, bf16[128,2048]{1,0:T(8,128)(2,1)}, u32[]{:S(2)}) copy-start(bf16[128,2048]{1,0:T(8,128)(2,1)} %own.1) | copy-start | bytes 1572868
  26.4 25.7 %copy-start.2 = (f32[128,300]{0,1:T(8,128)S(1)}, f32[128,300]{0,1:T(8,128)}, u32[]{:S(2)}) copy-start(f32[128,300]{0,1:T(8,128)} %param.11) | copy-start | bytes 460804
  26.4 25.8 %copy-start.3 = (bf16[512,300]{0,1:T(8,128)(2,1)S(1)}, bf16[512,300]{0,1:T(8,128)(2,1)}, u32[]{:S(2)}) copy-start(bf16[512,300]{0,1:T(8,128)(2,1)} %param.9) | copy-start | bytes 921604
  26.4 25.8 %copy-start.5 = (s32[2,256]{1,0:T(2,128)S(1)}, s32[2,256]{1,0:T(2,128)}, u32[]{:S(2)}) copy-start(s32[2,256]{1,0:T(2,128)} %batch_rows.3) | copy-start | bytes 6148
  26.4 3.4 %collective-permute-start.2 = (bf16[2,8,2048]{2,1,0:T(8,128)(2,1)S(1)}, bf16[2,8,2048]{2,1,0:T(8,128)(2,1)S(1)}, u32[]{:S(2)}, u32[]{:S(2)}) collective-permute-start(bf16[2,8,2048]{2,1,0:T(8,128)(2,1)S(1)} %get-tuple-element.45), channel_id=1, source_target_pairs={{0,8},{8,0},{16,24},{24,16},{32,40},{40,32},{48,56},{56,48},{1,9},... | collective-permute-start | bytes 196616 | tf_op jit(solution)/shard_map/ppermute | solution.py:250
  29.8 4.7 %collective-permute-start.3 = (bf16[2,8,2048]{2,1,0:T(8,128)(2,1)S(1)}, bf16[2,8,2048]{2,1,0:T(8,128)(2,1)S(1)}, u32[]{:S(2)}, u32[]{:S(2)}) collective-permute-start(bf16[2,8,2048]{2,1,0:T(8,128)(2,1)S(1)} %add.46), channel_id=1, source_target_pairs={{0,16},{8,24},{16,0},{24,8},{32,48},{40,56},{48,32},{56,40},{1,17}... | collective-permute-start | bytes 196616 | tf_op jit(solution)/shard_map/ppermute | solution.py:250
  34.6 7.7 %collective-permute-start.4 = (bf16[2,8,2048]{2,1,0:T(8,128)(2,1)S(1)}, bf16[2,8,2048]{2,1,0:T(8,128)(2,1)S(1)}, u32[]{:S(2)}, u32[]{:S(2)}) collective-permute-start(bf16[2,8,2048]{2,1,0:T(8,128)(2,1)S(1)} %add.47.piece), channel_id=1, source_target_pairs={{0,56},{8,48},{16,40},{24,32},{32,24},{40,16},{48,8},{56,0},{1,57}... | collective-permute-start | bytes 196616 | tf_op jit(solution)/shard_map/ppermute | solution.py:250
  43.4 16.9 %all-to-all-start.2 = ((bf16[16,2,8,2048]{3,2,1,0:T(8,128)(2,1)}), bf16[16,2,8,2048]{3,2,1,0:T(8,128)(2,1)S(1)}, u32[]{:S(2)}, u32[]{:S(2)}) async-start(bf16[16,2,8,2048]{3,2,1,0:T(8,128)(2,1)} %shard_map.78), calls=%async_computation.2 | async-start | bytes 2097152 | tf_op jit(solution)/shard_map/all_to_all | solution.py:29
  47.1 6.9 %collective-permute-start.5 = (bf16[128,2048]{1,0:T(8,128)(2,1)S(1)}, bf16[128,2048]{1,0:T(8,128)(2,1)S(1)}, u32[]{:S(2)}, u32[]{:S(2)}) collective-permute-start(bf16[128,2048]{1,0:T(8,128)(2,1)S(1)} %copy-done.1), channel_id=1, source_target_pairs={{0,1},{1,0},{2,3},{3,2},{4,5},{5,4},{6,7},{7,6},{8,9},{9,8},{10,11... | collective-permute-start | bytes 1572872 | tf_op jit(solution)/shard_map/ppermute | solution.py:25
  52.1 14.7 %collective-permute-start.7 = (f32[300,128]{1,0:T(8,128)S(1)}, f32[300,128]{1,0:T(8,128)S(1)}, u32[]{:S(2)}, u32[]{:S(2)}) collective-permute-start(f32[300,128]{1,0:T(8,128)S(1)} %bitcast.18), channel_id=1, source_target_pairs={{0,1},{1,0},{2,3},{3,2},{4,5},{5,4},{6,7},{7,6},{8,9},{9,8},{10,11... | collective-permute-start | bytes 460808 | tf_op jit(solution)/shard_map/ppermute | solution.py:25
  53.3 13.6 %collective-permute-start.8 = (bf16[300,256]{1,0:T(8,128)(2,1)S(1)}, bf16[300,256]{1,0:T(8,128)(2,1)S(1)}, u32[]{:S(2)}, u32[]{:S(2)}) collective-permute-start(bf16[300,256]{1,0:T(8,128)(2,1)S(1)} %get-tuple-element.42), channel_id=1, source_target_pairs={{0,1},{1,0},{2,3},{3,2},{4,5},{5,4},{6,7},{7,6},{8,9},{9,8},{10,11... | collective-permute-start | bytes 460808 | tf_op jit(solution)/shard_map/ppermute | solution.py:25
  61.1 6.7 %collective-permute-start.6 = (bf16[2,128,256]{2,1,0:T(8,128)(2,1)S(1)}, bf16[2,128,256]{2,1,0:T(8,128)(2,1)S(1)}, u32[]{:S(2)}, u32[]{:S(2)}) collective-permute-start(bf16[2,128,256]{2,1,0:T(8,128)(2,1)S(1)} %shard_map.79.tile), channel_id=1, source_target_pairs={{0,1},{1,0},{2,3},{3,2},{4,5},{5,4},{6,7},{7,6},{8,9},{9,8},{10,11... | collective-permute-start | bytes 393224 | tf_op jit(solution)/shard_map/ppermute | solution.py:25
  107.9 5.7 %collective-permute-start.9 = (f32[896,128]{1,0:T(8,128)S(1)}, f32[896,128]{1,0:T(8,128)S(1)}, u32[]{:S(2)}, u32[]{:S(2)}) collective-permute-start(f32[896,128]{1,0:T(8,128)S(1)} %bitcast.15), channel_id=1, source_target_pairs={{0,1},{1,0},{2,3},{3,2},{4,5},{5,4},{6,7},{7,6},{8,9},{9,8},{10,11... | collective-permute-start | bytes 1376264 | tf_op jit(solution)/shard_map/ppermute | solution.py:25

commit v4 on v3

--- a/solution.py
+++ b/solution.py
@@ -17,6 +17,7 @@
 PAIR = [(0, 1), (1, 0)]
 Z_MASKS = (1, 2, 7)
 SCRATCH = 16 << 20
+CHUNKS = 4
 HIGHEST = lax.Precision.HIGHEST
 NT = (((1,), (1,)), ((), ()))
 
@@ -62,23 +63,42 @@
     return -(-size // 8) * 8
 
 
-def rows_kernel(device, owners, batch_rows, spectra, kept, sent, *flag, sizes):
+def rows_kernel(device, owners, batch_rows, spectra, kept, sent, *rest, sizes):
+    flag, (lines, listed, arrivals) = rest[:-3], rest[-3:]
     here = device[0]
     core = here & (sizes[3] - 1)
     plane, slots, each, features = kept.shape
+    chunk = features // CHUNKS
+    listing = pltpu.make_async_copy(batch_rows, listed, arrivals.at[CHUNKS])
+    listing.start()
+    loads = []
+    for at in range(CHUNKS):
+        columns = slice(at * chunk, (at + 1) * chunk)
+        load = pltpu.make_async_copy(spectra.at[:, columns], lines.at[:, columns], arrivals.at[at])
+        load.start()
+        loads.append(load)
     if flag:
-        flag[0][0] = jnp.where(owners[0] // 2 != owners[1] // 2, 1, 0)
+        same_chip = owners[0] >> 1 == owners[1] >> 1
+        same_z = place(owners[0], sizes)[1] == place(owners[1], sizes)[1]
+        flag[0][0] = jnp.where(same_chip, 0, jnp.where(same_z, 1, 2))
+    listing.wait()
+    spots = []
     for slot in range(slots):
-        t = slot if slots > 1 else jnp.where(owners[1] // 2 == here // 2, 1, 0)
+        t = slot if slots > 1 else jnp.where(owners[1] >> 1 == here >> 1, 1, 0)
         own = owners[t] == here
-        for rows, out in zip(halves_of(batch_rows, t, core), (kept, sent)):
-            value = lax.dot_general(
-                chosen(rows, spectra.shape[0], own),
-                spectra[...],
-                (((0,), (0,)), ((), ())),
-                preferred_element_type=jnp.float32,
-            )
-            out[:, slot] = value.astype(out.dtype).reshape(plane, each, features)
+        both = jnp.concatenate(halves_of(listed, t, core), axis=1)
+        spots.append(chosen(both, lines.shape[0], own))
+    spots = jnp.concatenate(spots, axis=1)
+    for at in range(CHUNKS):
+        columns = slice(at * chunk, (at + 1) * chunk)
+        loads[at].wait()
+        value = lax.dot_general(
+            spots, lines[:, columns], (((0,), (0,)), ((), ())), preferred_element_type=jnp.float32
+        ).astype(kept.dtype)
+        value = value.reshape(slots, 2, plane, each, chunk)
+        for slot in range(slots):
+            kept[:, slot, :, columns] = value[slot, 0]
+            sent[:, slot, :, columns] = value[slot, 1]
 
 
 def targets_kernel(device, owners, batch_rows, targets, kept, sent, *, sizes):
@@ -104,8 +124,20 @@
         piece[t] = jnp.where(root_z == z, block, jnp.zeros_like(block))
 
 
-def spread_kernel(piece, arrived, out):
-    out[...] = jnp.broadcast_to((piece[...] + arrived[...])[None], out.shape)
+def along_kernel(device, owners, scattered, out, *, sizes):
+    _, z, _, _ = place(device[0], sizes)
+    t = jnp.where(place(owners[1], sizes)[1] == z, 1, 0)
+    root_y, _, root_x, _ = place(owners[t], sizes)
+    out[...] = jnp.broadcast_to(scattered[root_y * sizes[2] + root_x, 0][None], out.shape)
+
+
+def arrived_kernel(owners, along, piece, *, sizes):
+    for t in range(ITERS):
+        piece[t] = along[place(owners[t], sizes)[1]]
+
+
+def spread_kernel(piece, out):
+    out[...] = jnp.broadcast_to(piece[...][None], out.shape)
 
 
 def tile_kernel(batch, own, other, own_norms, other_norms, tile, *, each, factor):
@@ -191,19 +223,22 @@
     trained[...] = coefficients[...] - STEP_RATE / math.sqrt(total) * update
 
 
-def call(kernel, out_shape, operands, scalars=0, out_kinds=None):
+def call(kernel, out_shape, operands, scalars=0, out_kinds=None, in_place=(), scratch=()):
     outs = out_shape if isinstance(out_shape, tuple) else (out_shape,)
     out_kinds = out_kinds or [pltpu.VMEM] * len(outs)
     specs = tuple(pl.BlockSpec(memory_space=kind) for kind in out_kinds)
     kinds = [pltpu.SMEM] * scalars + [pltpu.VMEM] * (len(operands) - scalars)
-    operands = operands[:scalars] + tuple(
-        pltpu.with_memory_space_constraint(value, pltpu.VMEM) for value in operands[scalars:]
-    )
+    kinds = [pltpu.HBM if at in in_place else kind for at, kind in enumerate(kinds)]
+    operands = [
+        value if kind is pltpu.SMEM else pltpu.with_memory_space_constraint(value, kind)
+        for value, kind in zip(operands, kinds)
+    ]
     return pl.pallas_call(
         kernel,
         in_specs=[pl.BlockSpec(memory_space=kind) for kind in kinds],
         out_specs=specs if isinstance(out_shape, tuple) else specs[0],
         out_shape=out_shape,
+        scratch_shapes=scratch,
         compiler_params=pltpu.CompilerParams(vmem_limit_bytes=SCRATCH),
     )(*operands)
 
@@ -220,38 +255,57 @@
     device = lax.axis_index(AXES).reshape(1)
     core = lax.axis_index("core").reshape(1)
     narrow = jnp.bfloat16
+    block = pltpu.VMEM((ITERS, each, features), narrow)
 
     def rows_for(slots):
-        block = pltpu.VMEM((plane, slots, each, features), narrow)
+        blocks = pltpu.VMEM((plane, slots, each, features), narrow)
         flag = (jax.ShapeDtypeStruct((1,), jnp.int32),) if slots == 1 else ()
         return call(
             functools.partial(rows_kernel, sizes=sizes),
-            (block, block) + flag,
+            (blocks, blocks) + flag,
             (device, owners, batch_rows, spectra),
             scalars=2,
             out_kinds=[pltpu.VMEM, pltpu.VMEM] + [pltpu.SMEM] * len(flag),
-        )
-
-    def spread(kept, sent):
-        scattered = exchange(kept + swap(sent), PLANE)
+            in_place=(2, 3),
+            scratch=(
+                pltpu.VMEM(spectra.shape, narrow),
+                pltpu.VMEM(batch_rows.shape, jnp.int32),
+                pltpu.SemaphoreType.DMA((CHUNKS + 1,)),
+            ),
+        )
+
+    def in_steps(kept, sent):
+        piece = call(
+            functools.partial(pick_kernel, sizes=sizes),
+            block,
+            (device, owners, exchange(kept + swap(sent), PLANE)),
+            scalars=2,
+        )
+        for mask in Z_MASKS:
+            piece = piece + lax.ppermute(piece, "z", [(i, i ^ mask) for i in range(sizes[1])])
+        return piece
+
+    def at_once(kept, sent):
+        along = call(
+            functools.partial(along_kernel, sizes=sizes),
+            pltpu.VMEM((sizes[1], each, features), narrow),
+            (device, owners, exchange(kept + swap(sent), PLANE)),
+            scalars=2,
+        )
         return call(
-            functools.partial(pick_kernel, sizes=sizes),
-            pltpu.VMEM((ITERS, each, features), narrow),
-            (device, owners, scattered),
-            scalars=2,
+            functools.partial(arrived_kernel, sizes=sizes),
+            block,
+            (owners, exchange(along, "z")),
+            scalars=1,
         )
 
     kept, sent, apart = rows_for(1)
-    piece = lax.cond(apart[0] != 0, lambda: spread(kept, sent), lambda: spread(*rows_for(2)))
-
-    arrived = None
-    for mask in Z_MASKS:
-        piece = piece if arrived is None else piece + arrived
-        arrived = lax.ppermute(piece, "z", [(i, i ^ mask) for i in range(sizes[1])])
+    piece = lax.switch(
+        apart[0],
+        (lambda: in_steps(*rows_for(2)), lambda: in_steps(kept, sent), lambda: at_once(kept, sent)),
+    )
     spread_out = call(
-        spread_kernel,
-        pltpu.VMEM((plane, ITERS, each, features), narrow),
-        (piece, arrived),
+        spread_kernel, pltpu.VMEM((plane, ITERS, each, features), narrow), (piece,)
     )
     gathered = exchange(spread_out, PLANE).reshape(ITERS * half, features)
 

time: 116 us -> 115 us (level)
  blocking collectives: 54.8 us -> 69.2 us
  starting transfers between devices: 32.9 us -> 19.7 us
  waiting for transfers between devices: 15.7 us -> 13.3 us
  local copies, waits for them, and re-layouts: 2.34 us -> 0.08 us
  Pallas kernels: 8.04 us -> 10.2 us
    all_to_all x4 -> x5, blocking collectives: 54.8 us -> 69.2 us  [exchange(): return lax.all_to_all(blocks, axes, 0, 0, tiled=True)]
    ppermute x3 -> x0, starting transfers between devices: 10.4 us -> none  [body(): arrived = lax.ppermute(piece, 'z', [(i, i ^ mask) for i in range(sizes[1])])]
    ppermute x3 -> x0, waiting for transfers between devices: 5.51 us -> none  [body(): arrived = lax.ppermute(piece, 'z', [(i, i ^ mask) for i in range(sizes[1])])]
    ppermute x6, starting transfers between devices: 18.9 us -> 15.2 us  [swap(): return lax.ppermute(value, 'core', PAIR)]
    all_to_all x1, waiting for transfers between devices: 6.2 us -> 9.36 us  [exchange(): return lax.all_to_all(blocks, axes, 0, 0, tiled=True)]
    unnamed x14 -> x10, local copies, waits for them, and re-layouts: 2.29 us -> 0.03 us
    pallas_call x7 -> x8, Pallas kernels: 8.04 us -> 10.2 us  [call(): pl.pallas_call(kernel, in_specs=[pl.BlockSpec(memory_space=kind) for kind...]
  transfers between devices with their start and end apart: 10 -> 7, of which waited for: 7 -> 4; matrix products, arithmetic and copies ran while one was open for 0% -> 0% of each run, Pallas kernels for 2% -> 2%
where the time goes in v4:
time: 115 us
  blocking collectives  69.2 us (60%)
  starting transfers between devices  19.7 us (17%)
  waiting for transfers between devices  13.3 us (12%)
  Pallas kernels  10.2 us (9%)
  between operations  1.43 us (1%)
    all_to_all x5, blocking collectives, exchange(): return lax.all_to_all(blocks, axes, 0, 0, tiled=True)  69.2 us
    ppermute x6, starting transfers between devices, swap(): return lax.ppermute(value, 'core', PAIR)  15.2 us
    pallas_call x8, Pallas kernels, call(): pl.pallas_call(kernel, in_specs=[pl.BlockSpec(memory_space=kind) for kind...  10.2 us
    all_to_all x1, waiting for transfers between devices, exchange(): return lax.all_to_all(blocks, axes, 0, 0, tiled=True)  9.36 us
    all_to_all x1, starting transfers between devices, exchange(): return lax.all_to_all(blocks, axes, 0, 0, tiled=True)  4.49 us
    ppermute x6, waiting for transfers between devices, swap(): return lax.ppermute(value, 'core', PAIR)  3.97 us
  transfers between devices with their start and end apart: 7, of which 4 were waited for; matrix products, arithmetic and copies ran while one was open for 0% of the time, Pallas kernels for 2%

profile of v4, /device:TPU:1, one launch (start us, length us, event | category | flops | bytes accessed | tf_op | source)
XLA Modules:
  0.0 114.5 jit_solution(3869623885279686752)
XLA Ops:
  0.6 0.0 copy-start.4
  0.6 0.0 copy-start.3
  0.7 3.3 %shard_map.77 = (bf16[16,1,8,2048]{3,2,1,0:T(8,128)(2,1)S(1)}, bf16[16,1,8,2048]{3,2,1,0:T(8,128)(2,1)S(1)}, s32[1]{0:T(128)}) custom-call(s32[1]{0:T(128)} %bitcast.1.device, s32[2]{0:T(128)} %owners.3, s32[2,256]{1,0:T(2,128)} %batch_rows.3, bf16[512,2048]{1,0:T(8,128)(2,1)} %spectra.1), custom_call_target="tpu_custom_call" | custom-call | tf_op jit(solution)/shard_map/pallas_call | solution.py:236
  4.6 0.0 copy-done.4
  4.6 0.0 copy-done.3
  4.6 38.9 %conditional.1 = (bf16[2,8,2048]{2,1,0:T(8,128)(2,1)S(1)}) conditional(s32[]{:T(128)} %bitcast.2, (s32[1]{0:T(128)}, s32[2]{0:T(128)S(1)}, s32[2,256]{1,0:T(2,128)S(1)}, bf16[512,2048]{1,0:T(8,128)(2,1)}) %tuple.24, (bf16[16,1,8,2048]{3,2,1,0:T(8,128)(2,1)S(1)}, bf16[16,1,8,2048]{3,2,1,0:T(8,128)(2,1)S(1)}, s32[1]{0:T(128)}, ...), branch_computations={%region_0.0_spmd, %region_1.0_spmd, %region_2.0_spmd} | conditional | flops 622592 | bytes 10813608 | solution.py:303
  4.6 3.3 %collective-permute-start.8 = (bf16[16,1,8,2048]{3,2,1,0:T(8,128)(2,1)S(1)}, bf16[16,1,8,2048]{3,2,1,0:T(8,128)(2,1)S(1)}, u32[]{:S(2)}, u32[]{:S(2)}) collective-permute-start(bf16[16,1,8,2048]{3,2,1,0:T(8,128)(2,1)S(1)} %get-tuple-element.41), channel_id=1, source_target_pairs={{0,1},{1,0},{2,3},{3,2},{4,5},{5,4},{6,7},{7,6},{8,9},{9,8},{10,11... | collective-permute-start | bytes 1572872 | tf_op jit(solution)/shard_map/cond/branch_2_fun/ppermute | solution.py:26
  7.9 1.5 %collective-permute-done.8 = bf16[16,1,8,2048]{3,2,1,0:T(8,128)(2,1)S(1)} collective-permute-done((bf16[16,1,8,2048]{3,2,1,0:T(8,128)(2,1)S(1)}, bf16[16,1,8,2048]{3,2,1,0:T(8,128)(2,1)S(1)}, u32[]{:S(2)}, u32[]{:S(2)}) %collective-permute-start.8) | collective-permute-done | bytes 524320 | tf_op jit(solution)/shard_map/cond/branch_2_fun/ppermute | solution.py:26
  9.5 0.1 add.52
  9.6 15.6 %all_to_all.38.scattered = bf16[16,1,8,2048]{3,2,1,0:T(8,128)(2,1)S(1)} all-to-all(bf16[16,1,8,2048]{3,2,1,0:T(8,128)(2,1)S(1)} %add.52), channel_id=1, replica_groups=mesh['y'=4,'z'=8,'x'=4,'core'=2] {'y','x'}, dimensions={0} | all-to-all | bytes 1048576 | tf_op jit(solution)/shard_map/cond/branch_2_fun/all_to_all | solution.py:30
  25.2 0.6 branch_2_fun.2
  25.7 17.2 %all_to_all.39.along = bf16[8,8,2048]{2,1,0:T(8,128)(2,1)S(1)} all-to-all(bf16[8,8,2048]{2,1,0:T(8,128)(2,1)S(1)} %branch_2_fun.2), channel_id=1, replica_groups=mesh['y'=4,'z'=8,'x'=4,'core'=2] {'z'}, dimensions={0} | all-to-all | bytes 524288 | tf_op jit(solution)/shard_map/cond/branch_2_fun/all_to_all | solution.py:30
  42.9 0.6 branch_2_fun.3
  43.5 0.0 copy-start
  43.5 0.0 copy-start.1
  43.5 0.0 copy-start.2
  43.5 1.1 shard_map.78
  44.6 4.5 %all-to-all-start.4 = ((bf16[16,2,8,2048]{3,2,1,0:T(8,128)(2,1)}), bf16[16,2,8,2048]{3,2,1,0:T(8,128)(2,1)S(1)}, u32[]{:S(2)}, u32[]{:S(2)}) async-start(bf16[16,2,8,2048]{3,2,1,0:T(8,128)(2,1)} %shard_map.78), calls=%async_computation.4 | async-start | bytes 2097152 | tf_op jit(solution)/shard_map/all_to_all | solution.py:30
  49.1 0.0 copy-done
  49.1 3.0 %collective-permute-start.9 = (bf16[128,2048]{1,0:T(8,128)(2,1)S(1)}, bf16[128,2048]{1,0:T(8,128)(2,1)S(1)}, u32[]{:S(2)}, u32[]{:S(2)}) collective-permute-start(bf16[128,2048]{1,0:T(8,128)(2,1)S(1)} %copy-done), channel_id=1, source_target_pairs={{0,1},{1,0},{2,3},{3,2},{4,5},{5,4},{6,7},{7,6},{8,9},{9,8},{10,11... | collective-permute-start | bytes 1572872 | tf_op jit(solution)/shard_map/ppermute | solution.py:26
  52.1 0.0 copy-done.1
  52.1 0.1 collective-permute-start.11
  52.2 0.0 copy-done.2
  52.2 1.0 shard_map.80
  53.2 0.7 collective-permute-start.12
  53.9 0.2 multiply_reduce_fusion.1
  54.1 0.0 collective-permute-done.9.other
  54.1 0.2 multiply_reduce_fusion
  54.3 9.4 %all-to-all-done.4 = bf16[16,2,8,2048]{3,2,1,0:T(8,128)(2,1)S(1)} async-done(((bf16[16,2,8,2048]{3,2,1,0:T(8,128)(2,1)}), bf16[16,2,8,2048]{3,2,1,0:T(8,128)(2,1)S(1)}, u32[]{:S(2)}, u32[]{:S(2)}) %all-to-all-start.4) | async-done | bytes 1048608 | tf_op jit(solution)/shard_map/all_to_all | solution.py:30
  63.7 0.7 shard_map.79.tile
  64.4 4.1 %collective-permute-start.10 = (bf16[2,128,256]{2,1,0:T(8,128)(2,1)S(1)}, bf16[2,128,256]{2,1,0:T(8,128)(2,1)S(1)}, u32[]{:S(2)}, u32[]{:S(2)}) collective-permute-start(bf16[2,128,256]{2,1,0:T(8,128)(2,1)S(1)} %shard_map.79.tile), channel_id=1, source_target_pairs={{0,1},{1,0},{2,3},{3,2},{4,5},{5,4},{6,7},{7,6},{8,9},{9,8},{10,11... | collective-permute-start | bytes 393224 | tf_op jit(solution)/shard_map/ppermute | solution.py:26
  68.5 0.0 collective-permute-done.11.other
  68.5 0.0 collective-permute-done.12.arrived
  68.5 1.0 collective-permute-done.10.came
  69.4 0.7 shard_map.81
  70.1 12.7 %all_to_all.40 = f32[16,56,128]{2,1,0:T(8,128)S(1)} all-to-all(f32[16,56,128]{2,1,0:T(8,128)S(1)} %bitcast.17), channel_id=1, replica_groups=mesh['y'=4,'z'=8,'x'=4,'core'=2] {'y','x'}, dimensions={0} | all-to-all | bytes 917504 | tf_op jit(solution)/shard_map/all_to_all | solution.py:30
  82.9 11.6 %all_to_all.41 = f32[8,56,128]{2,1,0:T(8,128)S(1)} all-to-all(f32[8,56,128]{2,1,0:T(8,128)S(1)} %broadcast_in_dim.4), channel_id=1, replica_groups=mesh['y'=4,'z'=8,'x'=4,'core'=2] {'z'}, dimensions={0} | all-to-all | bytes 458752 | tf_op jit(solution)/shard_map/all_to_all | solution.py:30
  94.5 12.3 %all_to_all.42 = f32[16,56,128]{2,1,0:T(8,128)S(1)} all-to-all(f32[16,56,128]{2,1,0:T(8,128)S(1)} %broadcast_in_dim.5), channel_id=1, replica_groups=mesh['y'=4,'z'=8,'x'=4,'core'=2] {'y','x'}, dimensions={0} | all-to-all | bytes 917504 | tf_op jit(solution)/shard_map/all_to_all | solution.py:30
  106.7 4.1 %collective-permute-start.13 = (f32[896,128]{1,0:T(8,128)S(1)}, f32[896,128]{1,0:T(8,128)S(1)}, u32[]{:S(2)}, u32[]{:S(2)}) collective-permute-start(f32[896,128]{1,0:T(8,128)S(1)} %bitcast.15), channel_id=1, source_target_pairs={{0,1},{1,0},{2,3},{3,2},{4,5},{5,4},{6,7},{7,6},{8,9},{9,8},{10,11... | collective-permute-start | bytes 1376264 | tf_op jit(solution)/shard_map/ppermute | solution.py:26
  110.8 1.4 %collective-permute-done.13.other = f32[896,128]{1,0:T(8,128)S(1)} collective-permute-done((f32[896,128]{1,0:T(8,128)S(1)}, f32[896,128]{1,0:T(8,128)S(1)}, u32[]{:S(2)}, u32[]{:S(2)}) %collective-permute-start.13) | collective-permute-done | bytes 458784 | tf_op jit(solution)/shard_map/ppermute | solution.py:26
  112.2 2.3 %shard_map.82 = (f32[300,128]{1,0:T(8,128)}, f32[300,2,256]{2,1,0:T(2,128)}) custom-call(s32[1]{0:T(128)} %bitcast.core, f32[896,128]{1,0:T(8,128)S(1)} %bitcast.16, f32[896,128]{1,0:T(8,128)S(1)} %collective-permute-done.13.other, bf16[2,128,256]{2,1,0:T(8,128)(2,1)S(1)} %shard_map.79.tile, bf16[2,128,256]{2,1,0:T(8,128)(2,1)S(1)} %collective-permute-done.10.came, ...), custom_call_target="tpu_custom_call" | custom-call | tf_op jit(solution)/shard_map/pallas_call | solution.py:236
  (6 shorter events, 0.1 us)
Async XLA Ops:
  0.6 3.9 %copy-start.4 = (s32[2]{0:T(128)S(1)}, s32[2]{0:T(128)}, u32[]{:S(2)}) copy-start(s32[2]{0:T(128)} %owners.3) | copy-start | bytes 28
  0.6 3.9 %copy-start.3 = (s32[2,256]{1,0:T(2,128)S(1)}, s32[2,256]{1,0:T(2,128)}, u32[]{:S(2)}) copy-start(s32[2,256]{1,0:T(2,128)} %batch_rows.3) | copy-start | bytes 6148
  4.6 4.8 %collective-permute-start.8 = (bf16[16,1,8,2048]{3,2,1,0:T(8,128)(2,1)S(1)}, bf16[16,1,8,2048]{3,2,1,0:T(8,128)(2,1)S(1)}, u32[]{:S(2)}, u32[]{:S(2)}) collective-permute-start(bf16[16,1,8,2048]{3,2,1,0:T(8,128)(2,1)S(1)} %get-tuple-element.41), channel_id=1, source_target_pairs={{0,1},{1,0},{2,3},{3,2},{4,5},{5,4},{6,7},{7,6},{8,9},{9,8},{10,11... | collective-permute-start | bytes 1572872 | tf_op jit(solution)/shard_map/cond/branch_2_fun/ppermute | solution.py:26
  43.5 5.6 %copy-start = (bf16[128,2048]{1,0:T(8,128)(2,1)S(1)}, bf16[128,2048]{1,0:T(8,128)(2,1)}, u32[]{:S(2)}) copy-start(bf16[128,2048]{1,0:T(8,128)(2,1)} %own.1) | copy-start | bytes 1572868
  43.5 8.6 %copy-start.1 = (f32[128,300]{0,1:T(8,128)S(1)}, f32[128,300]{0,1:T(8,128)}, u32[]{:S(2)}) copy-start(f32[128,300]{0,1:T(8,128)} %param.12) | copy-start | bytes 460804
  43.5 8.7 %copy-start.2 = (bf16[512,300]{0,1:T(8,128)(2,1)S(1)}, bf16[512,300]{0,1:T(8,128)(2,1)}, u32[]{:S(2)}) copy-start(bf16[512,300]{0,1:T(8,128)(2,1)} %param.10) | copy-start | bytes 921604
  44.6 19.1 %all-to-all-start.4 = ((bf16[16,2,8,2048]{3,2,1,0:T(8,128)(2,1)}), bf16[16,2,8,2048]{3,2,1,0:T(8,128)(2,1)S(1)}, u32[]{:S(2)}, u32[]{:S(2)}) async-start(bf16[16,2,8,2048]{3,2,1,0:T(8,128)(2,1)} %shard_map.78), calls=%async_computation.4 | async-start | bytes 2097152 | tf_op jit(solution)/shard_map/all_to_all | solution.py:30
  49.1 5.0 %collective-permute-start.9 = (bf16[128,2048]{1,0:T(8,128)(2,1)S(1)}, bf16[128,2048]{1,0:T(8,128)(2,1)S(1)}, u32[]{:S(2)}, u32[]{:S(2)}) collective-permute-start(bf16[128,2048]{1,0:T(8,128)(2,1)S(1)} %copy-done), channel_id=1, source_target_pairs={{0,1},{1,0},{2,3},{3,2},{4,5},{5,4},{6,7},{7,6},{8,9},{9,8},{10,11... | collective-permute-start | bytes 1572872 | tf_op jit(solution)/shard_map/ppermute | solution.py:26
  52.1 16.4 %collective-permute-start.11 = (f32[300,128]{1,0:T(8,128)S(1)}, f32[300,128]{1,0:T(8,128)S(1)}, u32[]{:S(2)}, u32[]{:S(2)}) collective-permute-start(f32[300,128]{1,0:T(8,128)S(1)} %bitcast.18), channel_id=1, source_target_pairs={{0,1},{1,0},{2,3},{3,2},{4,5},{5,4},{6,7},{7,6},{8,9},{9,8},{10,11... | collective-permute-start | bytes 460808 | tf_op jit(solution)/shard_map/ppermute | solution.py:26
  53.2 15.2 %collective-permute-start.12 = (bf16[300,256]{1,0:T(8,128)(2,1)S(1)}, bf16[300,256]{1,0:T(8,128)(2,1)S(1)}, u32[]{:S(2)}, u32[]{:S(2)}) collective-permute-start(bf16[300,256]{1,0:T(8,128)(2,1)S(1)} %get-tuple-element.55), channel_id=1, source_target_pairs={{0,1},{1,0},{2,3},{3,2},{4,5},{5,4},{6,7},{7,6},{8,9},{9,8},{10,11... | collective-permute-start | bytes 460808 | tf_op jit(solution)/shard_map/ppermute | solution.py:26
  64.4 5.1 %collective-permute-start.10 = (bf16[2,128,256]{2,1,0:T(8,128)(2,1)S(1)}, bf16[2,128,256]{2,1,0:T(8,128)(2,1)S(1)}, u32[]{:S(2)}, u32[]{:S(2)}) collective-permute-start(bf16[2,128,256]{2,1,0:T(8,128)(2,1)S(1)} %shard_map.79.tile), channel_id=1, source_target_pairs={{0,1},{1,0},{2,3},{3,2},{4,5},{5,4},{6,7},{7,6},{8,9},{9,8},{10,11... | collective-permute-start | bytes 393224 | tf_op jit(solution)/shard_map/ppermute | solution.py:26
  106.7 5.5 %collective-permute-start.13 = (f32[896,128]{1,0:T(8,128)S(1)}, f32[896,128]{1,0:T(8,128)S(1)}, u32[]{:S(2)}, u32[]{:S(2)}) collective-permute-start(f32[896,128]{1,0:T(8,128)S(1)} %bitcast.15), channel_id=1, source_target_pairs={{0,1},{1,0},{2,3},{3,2},{4,5},{5,4},{6,7},{7,6},{8,9},{9,8},{10,11... | collective-permute-start | bytes 1376264 | tf_op jit(solution)/shard_map/ppermute | solution.py:26

commit v5 on v4

v5 whole, which is shorter than its diff:
```python
import functools
import math

import jax
import jax.numpy as jnp
from jax import lax
from jax.experimental import pallas as pl
from jax.experimental.pallas import tpu as pltpu
from jax.sharding import Mesh
from jax.sharding import PartitionSpec as P

ITERS = 2
AXES = ("y", "z", "x", "core")
PLANE = ("y", "x")
EPSILON = 1e-06
STEP_RATE = 0.2
SCRATCH = 16 << 20
CHUNKS = 4
GROUP = 4
HIGHEST = lax.Precision.HIGHEST
NT = (((1,), (1,)), ((), ()))


def exchange(blocks, axes):
    return lax.all_to_all(blocks, axes, 0, 0, tiled=True)


def place(device, sizes):
    bits = [size.bit_length() - 1 for size in sizes]
    core = device & (sizes[3] - 1)
    x = device >> bits[3] & (sizes[2] - 1)
    z = device >> (bits[3] + bits[2]) & (sizes[1] - 1)
    return device >> (bits[3] + bits[2] + bits[1]), z, x, core


def chosen(rows, held, own):
    spots = lax.broadcasted_iota(jnp.int32, (held, rows.shape[1]), 0) == rows
    return jnp.where(spots & own, 1.0, 0.0).astype(jnp.bfloat16)


def halves_of(batch_rows, t, core):
    rows = batch_rows[pl.ds(t, 1), :] if not isinstance(t, int) else batch_rows[t : t + 1, :]
    half = rows.shape[1] // 2
    first, second = rows[:, :half], rows[:, half:]
    return jnp.where(core == 0, first, second), jnp.where(core == 0, second, first)


def copies(value, axes):
    size = lax.axis_size(axes)
    return exchange(jnp.broadcast_to(value[None], (size, *value.shape)), axes)


def squares(value):
    return jnp.sum(jnp.square(value.astype(jnp.float32)), axis=1)


def aligned(size):
    return -(-size // 8) * 8


def rows_kernel(device, owners, batch_rows, spectra, kept, sent, *rest, sizes):
    flag, (lines, listed, arrivals) = rest[:-3], rest[-3:]
    here = device[0]
    core = here & (sizes[3] - 1)
    plane, slots, each, features = kept.shape
    chunk = features // CHUNKS
    listing = pltpu.make_async_copy(batch_rows, listed, arrivals.at[CHUNKS])
    listing.start()
    loads = []
    for at in range(CHUNKS):
        columns = slice(at * chunk, (at + 1) * chunk)
        load = pltpu.make_async_copy(spectra.at[:, columns], lines.at[:, columns], arrivals.at[at])
        load.start()
        loads.append(load)
    if flag:
        flag[0][0] = jnp.where(owners[0] >> 1 == owners[1] >> 1, 0, 1)
    listing.wait()
    spots = []
    for slot in range(slots):
        t = slot if slots > 1 else jnp.where(owners[1] >> 1 == here >> 1, 1, 0)
        own = owners[t] == here
        both = jnp.concatenate(halves_of(listed, t, core), axis=1)
        spots.append(chosen(both, lines.shape[0], own))
    spots = jnp.concatenate(spots, axis=1)
    for at in range(CHUNKS):
        columns = slice(at * chunk, (at + 1) * chunk)
        loads[at].wait()
        value = lax.dot_general(
            spots, lines[:, columns], (((0,), (0,)), ((), ())), preferred_element_type=jnp.float32
        ).astype(kept.dtype)
        value = value.reshape(slots, 2, plane, each, chunk)
        for slot in range(slots):
            kept[:, slot, :, columns] = value[slot, 0]
            sent[:, slot, :, columns] = value[slot, 1]


def targets_kernel(device, owners, batch_rows, targets, near, across, *, sizes):
    here = device[0]
    core = here & (sizes[3] - 1)
    batch_of = place(here, sizes)[1] & 1
    half = batch_rows.shape[1] // 2
    for t, out in ((batch_of, near), (1 - batch_of, across)):
        for at, rows in enumerate(halves_of(batch_rows, t, core)):
            out[:, at * half : (at + 1) * half] = jnp.dot(
                targets[...],
                chosen(rows, targets.shape[1], owners[t] == here),
                preferred_element_type=jnp.float32,
            ).astype(out.dtype)


def along_kernel(owners, scattered, out, *, sizes):
    slots = scattered.shape[1]
    for t in range(ITERS):
        root_y, _, root_x, _ = place(owners[t], sizes)
        block = scattered[root_y * sizes[2] + root_x, t if slots > 1 else 0]
        for z in range(t, sizes[1], ITERS):
            out[z] = block


def spread_kernel(device, owners, along, out, *, sizes):
    t = place(device[0], sizes)[1] & 1
    out[...] = jnp.broadcast_to(along[place(owners[t], sizes)[1]][None], out.shape)


def tile_kernel(member, batch, *rest, factor):
    centers, norms, (tile, turned) = rest[:GROUP], rest[GROUP : 2 * GROUP], rest[2 * GROUP :]
    lines = batch[...]
    lengths = jnp.sqrt(
        jnp.sum(jnp.square(lines.astype(jnp.float32)), axis=1, keepdims=True) + EPSILON
    )
    for at in range(GROUP):
        dots = lax.dot_general(lines, centers[at][...], NT, preferred_element_type=jnp.float32)
        scaled = dots / (lengths * norms[at][...]) * factor
        value = (scaled + scaled * scaled * scaled / 3.0).astype(tile.dtype)
        turned[at] = value
        tile[member[0] ^ at] = value


def partial_kernel(turned, *rest, root_scale):
    coefficients, (near, came, lines) = rest[:GROUP], rest[GROUP:]
    outs = lines.shape[0]
    total = None
    for at in range(GROUP):
        term = lax.dot_general(
            coefficients[at][...],
            turned[at].astype(jnp.float32),
            NT,
            precision=HIGHEST,
            preferred_element_type=jnp.float32,
        )
        total = term if total is None else total + term
    held = near[...].astype(jnp.float32) + came[...].astype(jnp.float32)
    lines[...] = total / root_scale - held


def join_kernel(member, partial, tile, came, lines):
    outs, count = partial.shape
    step = aligned(outs)
    first = member[0] < 2
    gram = None
    for at in range(GROUP):
        mine, theirs = tile[at], came[at]
        term = lax.dot_general(
            jnp.where(first, mine, theirs),
            jnp.where(first, theirs, mine),
            NT,
            preferred_element_type=jnp.float32,
        )
        gram = term if gram is None else gram + term
    lines[:outs] = partial[...]
    lines[outs:step] = jnp.zeros((step - outs, count), jnp.float32)
    lines[step : step + count] = gram
    lines[step + count :] = jnp.zeros((lines.shape[0] - step - count, count), jnp.float32)


def finish_kernel(member, mine, other, *rest, total):
    tiles, (coefficients, trained, residuals, kept) = rest[:GROUP], rest[GROUP:]
    outs, _ = coefficients.shape
    blocks, _, height, count = mine.shape
    step = aligned(outs)
    is_first = member[0] & 1 == 0

    def lines_of(t):
        own = mine[:, t].reshape(blocks * height, count)
        sent = other[:, t].reshape(blocks * height, count)
        return jnp.where(is_first, own, sent), jnp.where(is_first, sent, own)

    early, late = lines_of(0), lines_of(1)
    quarters = [value[step : step + count] for value in (*early, *late)]
    gram = jnp.concatenate(
        [
            jnp.concatenate([quarters[0], quarters[3]], axis=1),
            jnp.concatenate([quarters[2], quarters[1]], axis=1),
        ],
        axis=0,
    )
    first = jnp.concatenate([value[:outs] for value in early], axis=1)
    second = jnp.concatenate([value[:outs] for value in late], axis=1)
    second = second - STEP_RATE / total * jnp.dot(
        first, gram, precision=HIGHEST, preferred_element_type=jnp.float32
    )
    for t, residual in enumerate((first, second)):
        residuals[:, t, :] = residual
        for at in range(2):
            kept[2 * t + at] = residual[:, at * count : (at + 1) * count]
    update = None
    for at in range(GROUP):
        term = jnp.dot(
            kept[member[0] ^ at],
            tiles[at][...].astype(jnp.float32),
            precision=HIGHEST,
            preferred_element_type=jnp.float32,
        )
        update = term if update is None else update + term
    trained[...] = coefficients[...] - STEP_RATE / math.sqrt(total) * update


def call(kernel, out_shape, operands, scalars=0, out_kinds=None, in_place=(), scratch=()):
    outs = out_shape if isinstance(out_shape, tuple) else (out_shape,)
    out_kinds = out_kinds or [pltpu.VMEM] * len(outs)
    specs = tuple(pl.BlockSpec(memory_space=kind) for kind in out_kinds)
    kinds = [pltpu.SMEM] * scalars + [pltpu.VMEM] * (len(operands) - scalars)
    kinds = [pltpu.HBM if at in in_place else kind for at, kind in enumerate(kinds)]
    operands = [
        value if kind is pltpu.SMEM else pltpu.with_memory_space_constraint(value, kind)
        for value, kind in zip(operands, kinds)
    ]
    return pl.pallas_call(
        kernel,
        in_specs=[pl.BlockSpec(memory_space=kind) for kind in kinds],
        out_specs=specs if isinstance(out_shape, tuple) else specs[0],
        out_shape=out_shape,
        scratch_shapes=scratch,
        compiler_params=pltpu.CompilerParams(vmem_limit_bytes=SCRATCH),
    )(*operands)


def body(spectra, targets, centers, coefficients, owners, batch_rows):
    width, features = centers.shape
    outs = coefficients.shape[1]
    batch = batch_rows.shape[1]
    half = batch // 2
    total = width * lax.axis_size(AXES)
    sizes = tuple(lax.axis_size(name) for name in AXES)
    plane = sizes[0] * sizes[2]
    each = half // plane
    device = lax.axis_index(AXES).reshape(1)
    narrow = jnp.bfloat16
    z_size, core_size = sizes[1], sizes[3]
    member = ((lax.axis_index("z") & 1) * core_size + lax.axis_index("core")).reshape(1)

    def move(value, target):
        pairs = []
        for z in range(z_size):
            for c in range(core_size):
                to = target((z & 1) * core_size + c)
                pairs.append((z * core_size + c, (z - (z & 1) + to // 2) * core_size + to % 2))
        return lax.ppermute(value, ("z", "core"), pairs)

    def by(value, mask):
        return move(value, lambda at: at ^ mask)

    def rows_for(slots):
        blocks = pltpu.VMEM((plane, slots, each, features), narrow)
        flag = (jax.ShapeDtypeStruct((1,), jnp.int32),) if slots == 1 else ()
        return call(
            functools.partial(rows_kernel, sizes=sizes),
            (blocks, blocks) + flag,
            (device, owners, batch_rows, spectra),
            scalars=2,
            out_kinds=[pltpu.VMEM, pltpu.VMEM] + [pltpu.SMEM] * len(flag),
            in_place=(2, 3),
            scratch=(
                pltpu.VMEM(spectra.shape, narrow),
                pltpu.VMEM(batch_rows.shape, jnp.int32),
                pltpu.SemaphoreType.DMA((CHUNKS + 1,)),
            ),
        )

    def scatter(kept, sent):
        return call(
            functools.partial(along_kernel, sizes=sizes),
            pltpu.VMEM((z_size, each, features), narrow),
            (owners, exchange(kept + by(sent, 1), PLANE)),
            scalars=1,
        )

    kept, sent, apart = rows_for(1)
    along = lax.cond(apart[0] != 0, lambda: scatter(kept, sent), lambda: scatter(*rows_for(2)))
    spread_out = call(
        functools.partial(spread_kernel, sizes=sizes),
        pltpu.VMEM((plane, each, features), narrow),
        (device, owners, exchange(along, "z")),
        scalars=2,
    )
    gathered = exchange(spread_out, PLANE).reshape(half, features)

    shown = pltpu.VMEM((outs, batch), narrow)
    near, across = call(
        functools.partial(targets_kernel, sizes=sizes),
        (shown, shown),
        (device, owners, batch_rows, targets.T),
        scalars=2,
    )
    near = near + by(across, 2)
    came_targets = by(near[:, half:], 1)

    turned = coefficients.T
    both_centers = [centers, by(centers, 2)]
    both_coefficients = [turned, by(turned, 2)]
    all_centers = [both_centers[0], by(both_centers[0], 1), both_centers[1], by(both_centers[1], 1)]
    all_coefficients = [
        both_coefficients[0],
        by(both_coefficients[0], 1),
        both_coefficients[1],
        by(both_coefficients[1], 1),
    ]
    norms = [jnp.sqrt(squares(value) + EPSILON).reshape(1, -1) for value in all_centers]

    square = pltpu.VMEM((GROUP, half, width), narrow)
    tile, turned_tile = call(
        functools.partial(tile_kernel, factor=math.sqrt(features)),
        (square, square),
        (member, gathered, *all_centers, *norms),
        scalars=1,
    )
    came = move(tile, lambda at: at ^ 2 if at >= 2 else at ^ 3)
    partial = call(
        functools.partial(partial_kernel, root_scale=math.sqrt(total)),
        pltpu.VMEM((outs, half), jnp.float32),
        (turned_tile, *all_coefficients, near[:, :half], came_targets),
    )
    height = -(-(aligned(outs) + half) // (8 * plane)) * 8
    lines = call(
        join_kernel,
        pltpu.VMEM((plane * height, half), jnp.float32),
        (member, partial, tile, came),
        scalars=1,
    )
    tiles = [turned_tile[0]] + [by(turned_tile[at], at) for at in range(1, GROUP)]
    own = exchange(lines.reshape(plane, height, half), PLANE).sum(axis=0)
    own = copies(own, "z").reshape(z_size // 2, 2, height, half).sum(axis=0)
    whole = copies(own, PLANE)
    trained, residuals = call(
        functools.partial(finish_kernel, total=total),
        (
            jax.ShapeDtypeStruct((outs, width), jnp.float32),
            jax.ShapeDtypeStruct((outs, ITERS, batch), jnp.float32),
        ),
        (member, whole, by(whole, 1), *tiles, turned),
        scalars=1,
        scratch=(pltpu.VMEM((GROUP, outs, half), jnp.float32),),
    )
    return trained.T, jnp.transpose(residuals, (1, 2, 0))


def solution(mesh):
    torus = Mesh(mesh.devices.reshape(4, 8, 4, 2), AXES)
    return jax.shard_map(
        body,
        mesh=torus,
        in_specs=(P(AXES, None), P(AXES, None), P(AXES, None), P(AXES, None), P(), P()),
        out_specs=(P(AXES, None), P()),
        check_vma=False,
    )
```

time: 115 us -> 120 us (1.043)
  blocking collectives: 69.2 us -> 53.1 us
  starting transfers between devices: 19.7 us -> 35.5 us
  waiting for transfers between devices: 13.3 us -> 17.5 us
    all_to_all x5 -> x4, blocking collectives: 69.2 us -> 53.1 us  [exchange(): return lax.all_to_all(blocks, axes, 0, 0, tiled=True)]
    ppermute x6 -> x14, starting transfers between devices: 15.2 us -> 24.7 us  [move(): return lax.ppermute(value, ('z', 'core'), pairs)]
    ppermute x6 -> x14, waiting for transfers between devices: 3.97 us -> 11 us  [move(): return lax.ppermute(value, ('z', 'core'), pairs)]
    all_to_all x1 -> x2, starting transfers between devices: 4.49 us -> 10.9 us  [exchange(): return lax.all_to_all(blocks, axes, 0, 0, tiled=True)]
    all_to_all x1 -> x2, waiting for transfers between devices: 9.36 us -> 6.53 us  [exchange(): return lax.all_to_all(blocks, axes, 0, 0, tiled=True)]
  transfers between devices with their start and end apart: 7 -> 16, of which waited for: 4 -> 8; matrix products, arithmetic and copies ran while one was open for 0% -> 1% of each run, Pallas kernels for 2% -> 7%
where the time goes in v5:
time: 120 us
  blocking collectives  53.1 us (44%)
  starting transfers between devices  35.5 us (30%)
  waiting for transfers between devices  17.5 us (15%)
  Pallas kernels  10.9 us (9%)
  between operations  1.5 us (1%)
    all_to_all x4, blocking collectives, exchange(): return lax.all_to_all(blocks, axes, 0, 0, tiled=True)  53.1 us
    ppermute x14, starting transfers between devices, move(): return lax.ppermute(value, ('z', 'core'), pairs)  24.7 us
    ppermute x14, waiting for transfers between devices, move(): return lax.ppermute(value, ('z', 'core'), pairs)  11 us
    all_to_all x2, starting transfers between devices, exchange(): return lax.all_to_all(blocks, axes, 0, 0, tiled=True)  10.9 us
    pallas_call x8, Pallas kernels, call(): pl.pallas_call(kernel, in_specs=[pl.BlockSpec(memory_space=kind) for kind...  10.9 us
    all_to_all x2, waiting for transfers between devices, exchange(): return lax.all_to_all(blocks, axes, 0, 0, tiled=True)  6.53 us
  transfers between devices with their start and end apart: 16, of which 8 were waited for; matrix products, arithmetic and copies ran while one was open for 1% of the time, Pallas kernels for 7%

profile of v5, /device:TPU:1, one launch (start us, length us, event | category | flops | bytes accessed | tf_op | source)
XLA Modules:
  0.0 119.6 jit_solution(9586953620731698242)
XLA Ops:
  0.6 2.5 %collective-permute-start.3 = (bf16[128,2048]{1,0:T(8,128)(2,1)}, bf16[128,2048]{1,0:T(8,128)(2,1)S(1)}, u32[]{:S(2)}, u32[]{:S(2)}) collective-permute-start(bf16[128,2048]{1,0:T(8,128)(2,1)} %rest_0_.1), channel_id=1, source_target_pairs={{0,8},{1,9},{8,0},{9,1},{16,24},{17,25},{24,16},{25,17},{32,40},{3... | collective-permute-start | bytes 1572872 | tf_op jit(solution)/shard_map/ppermute | solution.py:258
  3.2 3.2 %shard_map.77 = (bf16[16,1,8,2048]{3,2,1,0:T(8,128)(2,1)S(1)}, bf16[16,1,8,2048]{3,2,1,0:T(8,128)(2,1)S(1)}, s32[1]{0:T(128)}) custom-call(s32[1]{0:T(128)} %bitcast.1.device, s32[2]{0:T(128)} %owners.5, s32[2,256]{1,0:T(2,128)} %batch_rows.3, bf16[512,2048]{1,0:T(8,128)(2,1)} %spectra.1), custom_call_target="tpu_custom_call" | custom-call | tf_op jit(solution)/shard_map/pallas_call | solution.py:228
  7.1 0.0 copy-start
  7.1 0.0 copy-start.1
  7.1 0.0 copy-start.2
  7.1 21.3 %conditional.1 = (bf16[8,8,2048]{2,1,0:T(8,128)(2,1)}) conditional(s32[]{:T(128)} %bitcast.2, (s32[1]{0:T(128)}, s32[2]{0:T(128)S(1)}, s32[2,256]{1,0:T(2,128)S(1)}, bf16[512,2048]{1,0:T(8,128)(2,1)}) %tuple.24, (bf16[16,1,8,2048]{3,2,1,0:T(8,128)(2,1)S(1)}, bf16[16,1,8,2048]{3,2,1,0:T(8,128)(2,1)S(1)}, s32[2]{0:T(128)S(1)}) %tuple.25), branch_computations={%region_0.0_spmd, %region_1.0_spmd} | conditional | flops 524288 | bytes 9437232 | solution.py:289
  7.1 1.0 collective-permute-start.1
  8.2 1.5 %collective-permute-done.1 = bf16[16,1,8,2048]{3,2,1,0:T(8,128)(2,1)S(1)} collective-permute-done((bf16[16,1,8,2048]{3,2,1,0:T(8,128)(2,1)S(1)}, bf16[16,1,8,2048]{3,2,1,0:T(8,128)(2,1)S(1)}, u32[]{:S(2)}, u32[]{:S(2)}) %collective-permute-start.1) | collective-permute-done | bytes 524320 | tf_op jit(solution)/shard_map/cond/branch_1_fun/ppermute | solution.py:258
  9.7 0.1 add.55
  9.8 17.3 %all_to_all.34.scattered = bf16[16,1,8,2048]{3,2,1,0:T(8,128)(2,1)S(1)} all-to-all(bf16[16,1,8,2048]{3,2,1,0:T(8,128)(2,1)S(1)} %add.55), channel_id=1, replica_groups=mesh['y'=4,'z'=8,'x'=4,'core'=2] {'y','x'}, dimensions={0} | all-to-all | bytes 1048576 | tf_op jit(solution)/shard_map/cond/branch_1_fun/all_to_all | solution.py:25
  27.1 1.3 %branch_1_fun.1 = bf16[8,8,2048]{2,1,0:T(8,128)(2,1)} custom-call(s32[2]{0:T(128)S(1)} %get-tuple-element.23.owners, bf16[16,1,8,2048]{3,2,1,0:T(8,128)(2,1)S(1)} %all_to_all.34.scattered), custom_call_target="tpu_custom_call" | custom-call | tf_op jit(solution)/shard_map/cond/branch_1_fun/pallas_call | solution.py:228
  28.4 7.3 %all-to-all-start.2 = ((bf16[8,8,2048]{2,1,0:T(8,128)(2,1)}), bf16[8,8,2048]{2,1,0:T(8,128)(2,1)S(1)}, u32[]{:S(2)}, u32[]{:S(2)}) async-start(bf16[8,8,2048]{2,1,0:T(8,128)(2,1)} %get-tuple-element.52), calls=%async_computation.2 | async-start | bytes 524288 | tf_op jit(solution)/shard_map/all_to_all | solution.py:25
  35.7 2.1 %collective-permute-start.2 = (bf16[128,2048]{1,0:T(8,128)(2,1)S(1)}, bf16[128,2048]{1,0:T(8,128)(2,1)S(1)}, u32[]{:S(2)}, u32[]{:S(2)}) collective-permute-start(bf16[128,2048]{1,0:T(8,128)(2,1)S(1)} %copy-done), channel_id=1, source_target_pairs={{0,1},{1,0},{8,9},{9,8},{16,17},{17,16},{24,25},{25,24},{32,33},{3... | collective-permute-start | bytes 1572872 | tf_op jit(solution)/shard_map/ppermute | solution.py:258
  37.8 0.1 collective-permute-start.5
  37.9 1.6 %collective-permute-start.6 = (f32[300,128]{1,0:T(8,128)S(1)}, f32[300,128]{1,0:T(8,128)S(1)}, u32[]{:S(2)}, u32[]{:S(2)}) collective-permute-start(f32[300,128]{1,0:T(8,128)S(1)} %bitcast.29), channel_id=1, source_target_pairs={{0,8},{1,9},{8,0},{9,1},{16,24},{17,25},{24,16},{25,17},{32,40},{3... | collective-permute-start | bytes 460808 | tf_op jit(solution)/shard_map/ppermute | solution.py:258
  39.6 1.0 shard_map.80
  40.6 0.1 collective-permute-start.8
  40.7 0.2 multiply_reduce_fusion.3
  40.9 4.4 %collective-permute-done.6.rest_2_ = f32[300,128]{1,0:T(8,128)S(1)} collective-permute-done((f32[300,128]{1,0:T(8,128)S(1)}, f32[300,128]{1,0:T(8,128)S(1)}, u32[]{:S(2)}, u32[]{:S(2)}) %collective-permute-start.6) | collective-permute-done | bytes 153632 | tf_op jit(solution)/shard_map/ppermute | solution.py:258
  45.3 4.4 %collective-permute-start.7 = (f32[300,128]{1,0:T(8,128)S(1)}, f32[300,128]{1,0:T(8,128)S(1)}, u32[]{:S(2)}, u32[]{:S(2)}) collective-permute-start(f32[300,128]{1,0:T(8,128)S(1)} %collective-permute-done.6.rest_2_), channel_id=1, source_target_pairs={{0,1},{1,0},{8,9},{9,8},{16,17},{17,16},{24,25},{25,24},{32,33},{3... | collective-permute-start | bytes 460808 | tf_op jit(solution)/shard_map/ppermute | solution.py:258
  49.8 0.0 all-to-all-done.2.along
  49.8 1.4 %shard_map.78 = bf16[16,8,2048]{2,1,0:T(8,128)(2,1)} custom-call(s32[1]{0:T(128)} %bitcast.1.device, s32[2]{0:T(128)S(1)} %copy-done.4, bf16[8,8,2048]{2,1,0:T(8,128)(2,1)S(1)} %all-to-all-done.2.along), custom_call_target="tpu_custom_call" | custom-call | tf_op jit(solution)/shard_map/pallas_call | solution.py:228
  51.2 3.6 %all-to-all-start.3 = ((bf16[16,8,2048]{2,1,0:T(8,128)(2,1)}), bf16[16,8,2048]{2,1,0:T(8,128)(2,1)S(1)}, u32[]{:S(2)}, u32[]{:S(2)}) async-start(bf16[16,8,2048]{2,1,0:T(8,128)(2,1)} %shard_map.78), calls=%async_computation.3 | async-start | bytes 1048576 | tf_op jit(solution)/shard_map/all_to_all | solution.py:25
  54.8 1.8 %collective-permute-start.4 = (bf16[128,2048]{1,0:T(8,128)(2,1)S(1)}, bf16[128,2048]{1,0:T(8,128)(2,1)S(1)}, u32[]{:S(2)}, u32[]{:S(2)}) collective-permute-start(bf16[128,2048]{1,0:T(8,128)(2,1)S(1)} %collective-permute-done.3.rest_2_), channel_id=1, source_target_pairs={{0,1},{1,0},{8,9},{9,8},{16,17},{17,16},{24,25},{25,24},{32,33},{3... | collective-permute-start | bytes 1572872 | tf_op jit(solution)/shard_map/ppermute | solution.py:258
  56.6 0.2 multiply_reduce_fusion.1
  56.8 0.2 multiply_reduce_fusion.2
  57.0 1.1 collective-permute-done.4.rest_3_
  58.1 0.2 multiply_reduce_fusion
  58.3 6.5 %all-to-all-done.3 = bf16[16,8,2048]{2,1,0:T(8,128)(2,1)S(1)} async-done(((bf16[16,8,2048]{2,1,0:T(8,128)(2,1)}), bf16[16,8,2048]{2,1,0:T(8,128)(2,1)S(1)}, u32[]{:S(2)}, u32[]{:S(2)}) %all-to-all-start.3) | async-done | bytes 524320 | tf_op jit(solution)/shard_map/all_to_all | solution.py:25
  64.8 0.7 shard_map.79
  65.6 3.4 %collective-permute-start.10 = (bf16[4,128,128]{2,1,0:T(8,128)(2,1)S(1)}, bf16[4,128,128]{2,1,0:T(8,128)(2,1)S(1)}, u32[]{:S(2)}, u32[]{:S(2)}) collective-permute-start(bf16[4,128,128]{2,1,0:T(8,128)(2,1)S(1)} %get-tuple-element.43.tile), channel_id=1, source_target_pairs={{0,9},{1,8},{8,0},{9,1},{16,25},{17,24},{24,16},{25,17},{32,41},{3... | collective-permute-start | bytes 393224 | tf_op jit(solution)/shard_map/ppermute | solution.py:258
  69.0 0.3 collective-permute-start.9
  69.3 0.0 collective-permute-done.5.rest_1_
  69.3 1.2 %collective-permute-done.9.rest_5_ = bf16[300,128]{1,0:T(8,128)(2,1)S(1)} collective-permute-done((bf16[300,128]{1,0:T(8,128)(2,1)S(1)}, bf16[300,128]{1,0:T(8,128)(2,1)S(1)}, u32[]{:S(2)}, u32[]{:S(2)}) %collective-permute-start.9) | collective-permute-done | bytes 76832 | tf_op jit(solution)/shard_map/ppermute | solution.py:258
  70.5 0.7 shard_map.81.partial
  71.2 0.4 collective-permute-done.10.came
  71.6 0.2 shard_map.82
  71.8 10.3 %all_to_all.35 = f32[16,32,128]{2,1,0:T(8,128)S(1)} all-to-all(f32[16,32,128]{2,1,0:T(8,128)S(1)} %bitcast.27), channel_id=1, replica_groups=mesh['y'=4,'z'=8,'x'=4,'core'=2] {'y','x'}, dimensions={0} | all-to-all | bytes 524288 | tf_op jit(solution)/shard_map/all_to_all | solution.py:25
  82.2 13.6 %all_to_all.36 = f32[8,32,128]{2,1,0:T(8,128)S(1)} all-to-all(f32[8,32,128]{2,1,0:T(8,128)S(1)} %broadcast_in_dim.4), channel_id=1, replica_groups=mesh['y'=4,'z'=8,'x'=4,'core'=2] {'z'}, dimensions={0} | all-to-all | bytes 262144 | tf_op jit(solution)/shard_map/all_to_all | solution.py:25
  95.8 0.1 broadcast_in_dim.5
  95.9 11.9 %all_to_all.37.mine = f32[16,2,32,128]{3,2,1,0:T(8,128)S(1)} all-to-all(f32[16,2,32,128]{3,2,1,0:T(8,128)S(1)} %broadcast_in_dim.5), channel_id=1, replica_groups=mesh['y'=4,'z'=8,'x'=4,'core'=2] {'y','x'}, dimensions={0} | all-to-all | bytes 1048576 | tf_op jit(solution)/shard_map/all_to_all | solution.py:25
  107.7 5.0 %collective-permute-start.11 = (f32[16,2,32,128]{3,2,1,0:T(8,128)S(1)}, f32[16,2,32,128]{3,2,1,0:T(8,128)S(1)}, u32[]{:S(2)}, u32[]{:S(2)}) collective-permute-start(f32[16,2,32,128]{3,2,1,0:T(8,128)S(1)} %all_to_all.37.mine), channel_id=1, source_target_pairs={{0,1},{1,0},{8,9},{9,8},{16,17},{17,16},{24,25},{25,24},{32,33},{3... | collective-permute-start | bytes 1572872 | tf_op jit(solution)/shard_map/ppermute | solution.py:258
  112.8 0.1 collective-permute-start.12
  112.9 0.4 collective-permute-start.13
  113.2 1.8 %collective-permute-start.14 = (bf16[128,128]{1,0:T(8,128)(2,1)S(1)}, bf16[128,128]{1,0:T(8,128)(2,1)S(1)}, u32[]{:S(2)}, u32[]{:S(2)}) collective-permute-start(bf16[128,128]{1,0:T(8,128)(2,1)S(1)} %get-tuple-element.48), channel_id=1, source_target_pairs={{0,9},{1,8},{8,1},{9,0},{16,25},{17,24},{24,17},{25,16},{32,41},{3... | collective-permute-start | bytes 98312 | tf_op jit(solution)/shard_map/ppermute | solution.py:258
  115.0 0.7 collective-permute-done.13.rest_2_
  115.7 1.6 %collective-permute-done.14.rest_3_ = bf16[128,128]{1,0:T(8,128)(2,1)S(1)} collective-permute-done((bf16[128,128]{1,0:T(8,128)(2,1)S(1)}, bf16[128,128]{1,0:T(8,128)(2,1)S(1)}, u32[]{:S(2)}, u32[]{:S(2)}) %collective-permute-start.14) | collective-permute-done | bytes 32800 | tf_op jit(solution)/shard_map/ppermute | solution.py:258
  117.3 2.3 %shard_map.83 = (f32[300,128]{1,0:T(8,128)}, f32[300,2,256]{2,1,0:T(2,128)}) custom-call(s32[1]{0:T(128)} %bitcast.member, f32[16,2,32,128]{3,2,1,0:T(8,128)S(1)} %all_to_all.37.mine, f32[16,2,32,128]{3,2,1,0:T(8,128)S(1)} %collective-permute-done.11.other, bf16[128,128]{1,0:T(8,128)(2,1)S(1)} %get-tuple-element.51.rest_0_, ...), custom_call_target="tpu_custom_call" | custom-call | tf_op jit(solution)/shard_map/pallas_call | solution.py:228
  (23 shorter events, 0.2 us)
Async XLA Ops:
  0.6 6.4 %copy-start.4 = (s32[2]{0:T(128)S(1)}, s32[2]{0:T(128)}, u32[]{:S(2)}) copy-start(s32[2]{0:T(128)} %owners.5) | copy-start | bytes 28
  0.6 6.4 %copy-start.3 = (s32[2,256]{1,0:T(2,128)S(1)}, s32[2,256]{1,0:T(2,128)}, u32[]{:S(2)}) copy-start(s32[2,256]{1,0:T(2,128)} %batch_rows.3) | copy-start | bytes 6148
  0.6 54.1 %collective-permute-start.3 = (bf16[128,2048]{1,0:T(8,128)(2,1)}, bf16[128,2048]{1,0:T(8,128)(2,1)S(1)}, u32[]{:S(2)}, u32[]{:S(2)}) collective-permute-start(bf16[128,2048]{1,0:T(8,128)(2,1)} %rest_0_.1), channel_id=1, source_target_pairs={{0,8},{1,9},{8,0},{9,1},{16,24},{17,25},{24,16},{25,17},{32,40},{3... | collective-permute-start | bytes 1572872 | tf_op jit(solution)/shard_map/ppermute | solution.py:258
  7.1 28.6 %copy-start = (bf16[128,2048]{1,0:T(8,128)(2,1)S(1)}, bf16[128,2048]{1,0:T(8,128)(2,1)}, u32[]{:S(2)}) copy-start(bf16[128,2048]{1,0:T(8,128)(2,1)} %rest_0_.1) | copy-start | bytes 1572868
  7.1 30.7 %copy-start.1 = (f32[128,300]{0,1:T(8,128)S(1)}, f32[128,300]{0,1:T(8,128)}, u32[]{:S(2)}) copy-start(f32[128,300]{0,1:T(8,128)} %param.11) | copy-start | bytes 460804
  7.1 32.5 %copy-start.2 = (bf16[512,300]{0,1:T(8,128)(2,1)S(1)}, bf16[512,300]{0,1:T(8,128)(2,1)}, u32[]{:S(2)}) copy-start(bf16[512,300]{0,1:T(8,128)(2,1)} %param.9) | copy-start | bytes 921604
  7.1 2.6 %collective-permute-start.1 = (bf16[16,1,8,2048]{3,2,1,0:T(8,128)(2,1)S(1)}, bf16[16,1,8,2048]{3,2,1,0:T(8,128)(2,1)S(1)}, u32[]{:S(2)}, u32[]{:S(2)}) collective-permute-start(bf16[16,1,8,2048]{3,2,1,0:T(8,128)(2,1)S(1)} %get-tuple-element.25), channel_id=1, source_target_pairs={{0,1},{1,0},{8,9},{9,8},{16,17},{17,16},{24,25},{25,24},{32,33},{3... | collective-permute-start | bytes 1572872 | tf_op jit(solution)/shard_map/cond/branch_1_fun/ppermute | solution.py:258
  28.4 21.4 %all-to-all-start.2 = ((bf16[8,8,2048]{2,1,0:T(8,128)(2,1)}), bf16[8,8,2048]{2,1,0:T(8,128)(2,1)S(1)}, u32[]{:S(2)}, u32[]{:S(2)}) async-start(bf16[8,8,2048]{2,1,0:T(8,128)(2,1)} %get-tuple-element.52), calls=%async_computation.2 | async-start | bytes 524288 | tf_op jit(solution)/shard_map/all_to_all | solution.py:25
  35.7 21.1 %collective-permute-start.2 = (bf16[128,2048]{1,0:T(8,128)(2,1)S(1)}, bf16[128,2048]{1,0:T(8,128)(2,1)S(1)}, u32[]{:S(2)}, u32[]{:S(2)}) collective-permute-start(bf16[128,2048]{1,0:T(8,128)(2,1)S(1)} %copy-done), channel_id=1, source_target_pairs={{0,1},{1,0},{8,9},{9,8},{16,17},{17,16},{24,25},{25,24},{32,33},{3... | collective-permute-start | bytes 1572872 | tf_op jit(solution)/shard_map/ppermute | solution.py:258
  37.8 31.4 %collective-permute-start.5 = (f32[300,128]{1,0:T(8,128)S(1)}, f32[300,128]{1,0:T(8,128)S(1)}, u32[]{:S(2)}, u32[]{:S(2)}) collective-permute-start(f32[300,128]{1,0:T(8,128)S(1)} %bitcast.28), channel_id=1, source_target_pairs={{0,1},{1,0},{8,9},{9,8},{16,17},{17,16},{24,25},{25,24},{32,33},{3... | collective-permute-start | bytes 460808 | tf_op jit(solution)/shard_map/ppermute | solution.py:258
  37.9 7.3 %collective-permute-start.6 = (f32[300,128]{1,0:T(8,128)S(1)}, f32[300,128]{1,0:T(8,128)S(1)}, u32[]{:S(2)}, u32[]{:S(2)}) collective-permute-start(f32[300,128]{1,0:T(8,128)S(1)} %bitcast.29), channel_id=1, source_target_pairs={{0,8},{1,9},{8,0},{9,1},{16,24},{17,25},{24,16},{25,17},{32,40},{3... | collective-permute-start | bytes 460808 | tf_op jit(solution)/shard_map/ppermute | solution.py:258
  40.6 9.1 %collective-permute-start.8 = (bf16[300,256]{1,0:T(8,128)(2,1)S(1)}, bf16[300,256]{1,0:T(8,128)(2,1)S(1)}, u32[]{:S(2)}, u32[]{:S(2)}) collective-permute-start(bf16[300,256]{1,0:T(8,128)(2,1)S(1)} %get-tuple-element.42), channel_id=1, source_target_pairs={{0,8},{1,9},{8,0},{9,1},{16,24},{17,25},{24,16},{25,17},{32,40},{3... | collective-permute-start | bytes 460808 | tf_op jit(solution)/shard_map/ppermute | solution.py:258
  45.3 25.2 %collective-permute-start.7 = (f32[300,128]{1,0:T(8,128)S(1)}, f32[300,128]{1,0:T(8,128)S(1)}, u32[]{:S(2)}, u32[]{:S(2)}) collective-permute-start(f32[300,128]{1,0:T(8,128)S(1)} %collective-permute-done.6.rest_2_), channel_id=1, source_target_pairs={{0,1},{1,0},{8,9},{9,8},{16,17},{17,16},{24,25},{25,24},{32,33},{3... | collective-permute-start | bytes 460808 | tf_op jit(solution)/shard_map/ppermute | solution.py:258
  51.2 13.7 %all-to-all-start.3 = ((bf16[16,8,2048]{2,1,0:T(8,128)(2,1)}), bf16[16,8,2048]{2,1,0:T(8,128)(2,1)S(1)}, u32[]{:S(2)}, u32[]{:S(2)}) async-start(bf16[16,8,2048]{2,1,0:T(8,128)(2,1)} %shard_map.78), calls=%async_computation.3 | async-start | bytes 1048576 | tf_op jit(solution)/shard_map/all_to_all | solution.py:25
  54.8 3.3 %collective-permute-start.4 = (bf16[128,2048]{1,0:T(8,128)(2,1)S(1)}, bf16[128,2048]{1,0:T(8,128)(2,1)S(1)}, u32[]{:S(2)}, u32[]{:S(2)}) collective-permute-start(bf16[128,2048]{1,0:T(8,128)(2,1)S(1)} %collective-permute-done.3.rest_2_), channel_id=1, source_target_pairs={{0,1},{1,0},{8,9},{9,8},{16,17},{17,16},{24,25},{25,24},{32,33},{3... | collective-permute-start | bytes 1572872 | tf_op jit(solution)/shard_map/ppermute | solution.py:258
  65.6 6.0 %collective-permute-start.10 = (bf16[4,128,128]{2,1,0:T(8,128)(2,1)S(1)}, bf16[4,128,128]{2,1,0:T(8,128)(2,1)S(1)}, u32[]{:S(2)}, u32[]{:S(2)}) collective-permute-start(bf16[4,128,128]{2,1,0:T(8,128)(2,1)S(1)} %get-tuple-element.43.tile), channel_id=1, source_target_pairs={{0,9},{1,8},{8,0},{9,1},{16,25},{17,24},{24,16},{25,17},{32,41},{3... | collective-permute-start | bytes 393224 | tf_op jit(solution)/shard_map/ppermute | solution.py:258
  69.0 1.5 %collective-permute-start.9 = (bf16[300,128]{1,0:T(8,128)(2,1)S(1)}, bf16[300,128]{1,0:T(8,128)(2,1)S(1)}, u32[]{:S(2)}, u32[]{:S(2)}) collective-permute-start(bf16[300,128]{1,0:T(8,128)(2,1)S(1)} %get-tuple-element.46), channel_id=1, source_target_pairs={{0,1},{1,0},{8,9},{9,8},{16,17},{17,16},{24,25},{25,24},{32,33},{3... | collective-permute-start | bytes 230408 | tf_op jit(solution)/shard_map/ppermute | solution.py:258
  107.7 9.5 %collective-permute-start.11 = (f32[16,2,32,128]{3,2,1,0:T(8,128)S(1)}, f32[16,2,32,128]{3,2,1,0:T(8,128)S(1)}, u32[]{:S(2)}, u32[]{:S(2)}) collective-permute-start(f32[16,2,32,128]{3,2,1,0:T(8,128)S(1)} %all_to_all.37.mine), channel_id=1, source_target_pairs={{0,1},{1,0},{8,9},{9,8},{16,17},{17,16},{24,25},{25,24},{32,33},{3... | collective-permute-start | bytes 1572872 | tf_op jit(solution)/shard_map/ppermute | solution.py:258
  112.8 2.2 %collective-permute-start.12 = (bf16[128,128]{1,0:T(8,128)(2,1)S(1)}, bf16[128,128]{1,0:T(8,128)(2,1)S(1)}, u32[]{:S(2)}, u32[]{:S(2)}) collective-permute-start(bf16[128,128]{1,0:T(8,128)(2,1)S(1)} %get-tuple-element.50), channel_id=1, source_target_pairs={{0,1},{1,0},{8,9},{9,8},{16,17},{17,16},{24,25},{25,24},{32,33},{3... | collective-permute-start | bytes 98312 | tf_op jit(solution)/shard_map/ppermute | solution.py:258
  112.9 2.9 %collective-permute-start.13 = (bf16[128,128]{1,0:T(8,128)(2,1)S(1)}, bf16[128,128]{1,0:T(8,128)(2,1)S(1)}, u32[]{:S(2)}, u32[]{:S(2)}) collective-permute-start(bf16[128,128]{1,0:T(8,128)(2,1)S(1)} %get-tuple-element.49), channel_id=1, source_target_pairs={{0,8},{1,9},{8,0},{9,1},{16,24},{17,25},{24,16},{25,17},{32,40},{3... | collective-permute-start | bytes 98312 | tf_op jit(solution)/shard_map/ppermute | solution.py:258
  113.2 4.0 %collective-permute-start.14 = (bf16[128,128]{1,0:T(8,128)(2,1)S(1)}, bf16[128,128]{1,0:T(8,128)(2,1)S(1)}, u32[]{:S(2)}, u32[]{:S(2)}) collective-permute-start(bf16[128,128]{1,0:T(8,128)(2,1)S(1)} %get-tuple-element.48), channel_id=1, source_target_pairs={{0,9},{1,8},{8,1},{9,0},{16,25},{17,24},{24,17},{25,16},{32,41},{3... | collective-permute-start | bytes 98312 | tf_op jit(solution)/shard_map/ppermute | solution.py:258

commit v6 on v5

--- a/solution.py
+++ b/solution.py
@@ -285,12 +285,15 @@
             scalars=1,
         )
 
+    def reach(kept, sent):
+        return exchange(scatter(kept, sent), "z")
+
     kept, sent, apart = rows_for(1)
-    along = lax.cond(apart[0] != 0, lambda: scatter(kept, sent), lambda: scatter(*rows_for(2)))
+    along = lax.cond(apart[0] != 0, lambda: reach(kept, sent), lambda: reach(*rows_for(2)))
     spread_out = call(
         functools.partial(spread_kernel, sizes=sizes),
         pltpu.VMEM((plane, each, features), narrow),
-        (device, owners, exchange(along, "z")),
+        (device, owners, along),
         scalars=2,
     )
     gathered = exchange(spread_out, PLANE).reshape(half, features)
@@ -317,6 +320,9 @@
     ]
     norms = [jnp.sqrt(squares(value) + EPSILON).reshape(1, -1) for value in all_centers]
 
+    gathered, all_centers, all_coefficients, near, came_targets, norms = lax.optimization_barrier(
+        (gathered, all_centers, all_coefficients, near, came_targets, norms)
+    )
     square = pltpu.VMEM((GROUP, half, width), narrow)
     tile, turned_tile = call(
         functools.partial(tile_kernel, factor=math.sqrt(features)),
@@ -339,6 +345,7 @@
     )
     tiles = [turned_tile[0]] + [by(turned_tile[at], at) for at in range(1, GROUP)]
     own = exchange(lines.reshape(plane, height, half), PLANE).sum(axis=0)
+    own, tiles = lax.optimization_barrier((own, tiles))
     own = copies(own, "z").reshape(z_size // 2, 2, height, half).sum(axis=0)
     whole = copies(own, PLANE)
     trained, residuals = call(

time: 120 us -> 117 us (0.975)
  starting transfers between devices: 35.5 us -> 30.1 us
  blocking collectives: 53.1 us -> 57.5 us
  waiting for transfers between devices: 17.5 us -> 15.4 us
    ppermute x14, starting transfers between devices: 24.7 us -> 18.2 us  [move(): return lax.ppermute(value, ('z', 'core'), pairs)]
    all_to_all x4, blocking collectives: 53.1 us -> 57.5 us  [exchange(): return lax.all_to_all(blocks, axes, 0, 0, tiled=True)]
    all_to_all x2, waiting for transfers between devices: 6.53 us -> 4.45 us  [exchange(): return lax.all_to_all(blocks, axes, 0, 0, tiled=True)]
  transfers between devices with their start and end apart: 16 -> 16, of which waited for: 8 -> 6; matrix products, arithmetic and copies ran while one was open for 1% -> 1% of each run, Pallas kernels for 7% -> 6%
where the time goes in v6:
time: 117 us
  blocking collectives  57.5 us (49%)
  starting transfers between devices  30.1 us (26%)
  waiting for transfers between devices  15.4 us (13%)
  Pallas kernels  10.8 us (9%)
  between operations  1.55 us (1%)
    all_to_all x4, blocking collectives, exchange(): return lax.all_to_all(blocks, axes, 0, 0, tiled=True)  57.5 us
    ppermute x14, starting transfers between devices, move(): return lax.ppermute(value, ('z', 'core'), pairs)  18.2 us
    all_to_all x2, starting transfers between devices, exchange(): return lax.all_to_all(blocks, axes, 0, 0, tiled=True)  11.9 us
    ppermute x14, waiting for transfers between devices, move(): return lax.ppermute(value, ('z', 'core'), pairs)  11 us
    pallas_call x8, Pallas kernels, call(): pl.pallas_call(kernel, in_specs=[pl.BlockSpec(memory_space=kind) for kind...  10.8 us
    all_to_all x2, waiting for transfers between devices, exchange(): return lax.all_to_all(blocks, axes, 0, 0, tiled=True)  4.45 us
  transfers between devices with their start and end apart: 16, of which 6 were waited for; matrix products, arithmetic and copies ran while one was open for 1% of the time, Pallas kernels for 6%

profile of v6, /device:TPU:1, one launch (start us, length us, event | category | flops | bytes accessed | tf_op | source)
XLA Modules:
  0.0 116.6 jit_solution(15256499620504029915)
XLA Ops:
  0.6 2.5 %collective-permute-start.3 = (bf16[128,2048]{1,0:T(8,128)(2,1)}, bf16[128,2048]{1,0:T(8,128)(2,1)S(1)}, u32[]{:S(2)}, u32[]{:S(2)}) collective-permute-start(bf16[128,2048]{1,0:T(8,128)(2,1)} %rest_0_), channel_id=1, source_target_pairs={{0,8},{1,9},{8,0},{9,1},{16,24},{17,25},{24,16},{25,17},{32,40},{3... | collective-permute-start | bytes 1572872 | tf_op jit(solution)/shard_map/ppermute | solution.py:258
  3.2 1.0 collective-permute-start.2
  4.1 0.0 collective-permute-start.5
  4.2 1.5 %collective-permute-start.6 = (f32[300,128]{1,0:T(8,128)}, f32[300,128]{1,0:T(8,128)S(1)}, u32[]{:S(2)}, u32[]{:S(2)}) collective-permute-start(f32[300,128]{1,0:T(8,128)} %bitcast.28), channel_id=1, source_target_pairs={{0,8},{1,9},{8,0},{9,1},{16,24},{17,25},{24,16},{25,17},{32,40},{3... | collective-permute-start | bytes 460808 | tf_op jit(solution)/shard_map/ppermute | solution.py:258
  5.7 3.2 %shard_map.77 = (bf16[16,1,8,2048]{3,2,1,0:T(8,128)(2,1)S(1)}, bf16[16,1,8,2048]{3,2,1,0:T(8,128)(2,1)S(1)}, s32[1]{0:T(128)}) custom-call(s32[1]{0:T(128)} %bitcast.1.device, s32[2]{0:T(128)} %owners.5, s32[2,256]{1,0:T(2,128)} %batch_rows.3, bf16[512,2048]{1,0:T(8,128)(2,1)} %spectra.1), custom_call_target="tpu_custom_call" | custom-call | tf_op jit(solution)/shard_map/pallas_call | solution.py:228
  9.6 0.0 copy-start.2
  9.6 35.9 %conditional.1 = (bf16[8,8,2048]{2,1,0:T(8,128)(2,1)S(1)}) conditional(s32[]{:T(128)} %bitcast.2, (s32[1]{0:T(128)}, s32[2]{0:T(128)S(1)}, s32[2,256]{1,0:T(2,128)S(1)}, bf16[512,2048]{1,0:T(8,128)(2,1)}) %tuple.27, (bf16[16,1,8,2048]{3,2,1,0:T(8,128)(2,1)S(1)}, bf16[16,1,8,2048]{3,2,1,0:T(8,128)(2,1)S(1)}, s32[2]{0:T(128)S(1)}) %tuple.28), branch_computations={%region_0.0_spmd, %region_1.0_spmd} | conditional | flops 524288 | bytes 9961520 | solution.py:292
  9.6 0.9 collective-permute-start.1
  10.5 1.5 %collective-permute-done.1 = bf16[16,1,8,2048]{3,2,1,0:T(8,128)(2,1)S(1)} collective-permute-done((bf16[16,1,8,2048]{3,2,1,0:T(8,128)(2,1)S(1)}, bf16[16,1,8,2048]{3,2,1,0:T(8,128)(2,1)S(1)}, u32[]{:S(2)}, u32[]{:S(2)}) %collective-permute-start.1) | collective-permute-done | bytes 524320 | tf_op jit(solution)/shard_map/cond/branch_1_fun/ppermute | solution.py:258
  12.0 0.1 add.55
  12.2 15.6 %all_to_all.38.scattered = bf16[16,1,8,2048]{3,2,1,0:T(8,128)(2,1)S(1)} all-to-all(bf16[16,1,8,2048]{3,2,1,0:T(8,128)(2,1)S(1)} %add.55), channel_id=1, replica_groups=mesh['y'=4,'z'=8,'x'=4,'core'=2] {'y','x'}, dimensions={0} | all-to-all | bytes 1048576 | tf_op jit(solution)/shard_map/cond/branch_1_fun/all_to_all | solution.py:25
  27.7 0.6 branch_1_fun.1
  28.3 17.2 %all_to_all.39 = bf16[8,8,2048]{2,1,0:T(8,128)(2,1)S(1)} all-to-all(bf16[8,8,2048]{2,1,0:T(8,128)(2,1)S(1)} %branch_1_fun.1), channel_id=1, replica_groups=mesh['y'=4,'z'=8,'x'=4,'core'=2] {'z'}, dimensions={0} | all-to-all | bytes 524288 | tf_op jit(solution)/shard_map/cond/branch_1_fun/all_to_all | solution.py:25
  45.5 1.4 %shard_map.78 = bf16[16,8,2048]{2,1,0:T(8,128)(2,1)} custom-call(s32[1]{0:T(128)} %bitcast.1.device, s32[2]{0:T(128)S(1)} %copy-done.6, bf16[8,8,2048]{2,1,0:T(8,128)(2,1)S(1)} %get-tuple-element.90.along), custom_call_target="tpu_custom_call" | custom-call | tf_op jit(solution)/shard_map/pallas_call | solution.py:228
  46.9 4.5 %all-to-all-start.4 = ((bf16[16,8,2048]{2,1,0:T(8,128)(2,1)}), bf16[16,8,2048]{2,1,0:T(8,128)(2,1)S(1)}, u32[]{:S(2)}, u32[]{:S(2)}) async-start(bf16[16,8,2048]{2,1,0:T(8,128)(2,1)} %shard_map.78), calls=%async_computation.4 | async-start | bytes 1048576 | tf_op jit(solution)/shard_map/all_to_all | solution.py:25
  51.4 1.0 shard_map.79
  52.4 0.1 collective-permute-start.8
  52.5 0.2 multiply_reduce_fusion.3
  52.7 3.9 %collective-permute-done.8 = bf16[300,256]{1,0:T(8,128)(2,1)S(1)} collective-permute-done((bf16[300,256]{1,0:T(8,128)(2,1)S(1)}, bf16[300,256]{1,0:T(8,128)(2,1)S(1)}, u32[]{:S(2)}, u32[]{:S(2)}) %collective-permute-start.8) | collective-permute-done | bytes 153632 | tf_op jit(solution)/shard_map/ppermute | solution.py:258
  56.6 0.0 copy-start.4
  56.6 0.0 copy-start.1
  56.7 4.1 %collective-permute-start.9 = (bf16[300,128]{1,0:T(8,128)(2,1)S(1)}, bf16[300,128]{1,0:T(8,128)(2,1)S(1)}, u32[]{:S(2)}, u32[]{:S(2)}) collective-permute-start(bf16[300,128]{1,0:T(8,128)(2,1)S(1)} %slice.24), channel_id=1, source_target_pairs={{0,1},{1,0},{8,9},{9,8},{16,17},{17,16},{24,25},{25,24},{32,33},{3... | collective-permute-start | bytes 230408 | tf_op jit(solution)/shard_map/ppermute | solution.py:258
  60.8 0.5 collective-permute-start.7
  61.4 0.1 collective-permute-start.4
  61.4 0.2 multiply_reduce_fusion.1
  61.6 0.2 multiply_reduce_fusion.2
  61.8 1.4 %collective-permute-done.4.rest_3_ = bf16[128,2048]{1,0:T(8,128)(2,1)S(1)} collective-permute-done((bf16[128,2048]{1,0:T(8,128)(2,1)S(1)}, bf16[128,2048]{1,0:T(8,128)(2,1)S(1)}, u32[]{:S(2)}, u32[]{:S(2)}) %collective-permute-start.4) | collective-permute-done | bytes 524320 | tf_op jit(solution)/shard_map/ppermute | solution.py:258
  63.3 0.2 multiply_reduce_fusion
  63.5 0.0 collective-permute-done.7.rest_3_
  63.5 0.0 all-to-all-done.4
  63.5 0.0 copy-start.5
  63.5 0.7 shard_map.80
  64.3 1.3 %collective-permute-start.10 = (bf16[4,128,128]{2,1,0:T(8,128)(2,1)S(1)}, bf16[4,128,128]{2,1,0:T(8,128)(2,1)S(1)}, u32[]{:S(2)}, u32[]{:S(2)}) collective-permute-start(bf16[4,128,128]{2,1,0:T(8,128)(2,1)S(1)} %get-tuple-element.78.tile), channel_id=1, source_target_pairs={{0,9},{1,8},{8,0},{9,1},{16,25},{17,24},{24,16},{25,17},{32,41},{3... | collective-permute-start | bytes 393224 | tf_op jit(solution)/shard_map/ppermute | solution.py:258
  65.6 0.7 shard_map.81.partial
  66.3 2.6 %collective-permute-done.10.came = bf16[4,128,128]{2,1,0:T(8,128)(2,1)S(1)} collective-permute-done((bf16[4,128,128]{2,1,0:T(8,128)(2,1)S(1)}, bf16[4,128,128]{2,1,0:T(8,128)(2,1)S(1)}, u32[]{:S(2)}, u32[]{:S(2)}) %collective-permute-start.10) | collective-permute-done | bytes 131104 | tf_op jit(solution)/shard_map/ppermute | solution.py:258
  68.9 0.9 shard_map.82
  69.8 7.4 %all-to-all-start.5 = ((f32[16,32,128]{2,1,0:T(8,128)}), f32[16,32,128]{2,1,0:T(8,128)S(1)}, u32[]{:S(2)}, u32[]{:S(2)}) async-start(f32[16,32,128]{2,1,0:T(8,128)} %bitcast.10), calls=%async_computation.5 | async-start | bytes 524288 | tf_op jit(solution)/shard_map/all_to_all | solution.py:25
  77.2 1.4 %collective-permute-start.11 = (bf16[128,128]{1,0:T(8,128)(2,1)S(1)}, bf16[128,128]{1,0:T(8,128)(2,1)S(1)}, u32[]{:S(2)}, u32[]{:S(2)}) collective-permute-start(bf16[128,128]{1,0:T(8,128)(2,1)S(1)} %get-tuple-element.88), channel_id=1, source_target_pairs={{0,1},{1,0},{8,9},{9,8},{16,17},{17,16},{24,25},{25,24},{32,33},{3... | collective-permute-start | bytes 98312 | tf_op jit(solution)/shard_map/ppermute | solution.py:258
  78.7 0.0 collective-permute-start.12
  78.7 1.7 %collective-permute-start.13 = (bf16[128,128]{1,0:T(8,128)(2,1)S(1)}, bf16[128,128]{1,0:T(8,128)(2,1)S(1)}, u32[]{:S(2)}, u32[]{:S(2)}) collective-permute-start(bf16[128,128]{1,0:T(8,128)(2,1)S(1)} %get-tuple-element.86), channel_id=1, source_target_pairs={{0,9},{1,8},{8,1},{9,0},{16,25},{17,24},{24,17},{25,16},{32,41},{3... | collective-permute-start | bytes 98312 | tf_op jit(solution)/shard_map/ppermute | solution.py:258
  80.4 4.4 %all-to-all-done.5 = f32[16,32,128]{2,1,0:T(8,128)S(1)} async-done(((f32[16,32,128]{2,1,0:T(8,128)}), f32[16,32,128]{2,1,0:T(8,128)S(1)}, u32[]{:S(2)}, u32[]{:S(2)}) %all-to-all-start.5) | async-done | bytes 262176 | tf_op jit(solution)/shard_map/all_to_all | solution.py:25
  84.9 0.0 collective-permute-done.11.rest_1_
  84.9 10.5 %all_to_all.40 = f32[8,32,128]{2,1,0:T(8,128)S(1)} all-to-all(f32[8,32,128]{2,1,0:T(8,128)S(1)} %broadcast_in_dim.4), channel_id=1, replica_groups=mesh['y'=4,'z'=8,'x'=4,'core'=2] {'z'}, dimensions={0} | all-to-all | bytes 262144 | tf_op jit(solution)/shard_map/all_to_all | solution.py:25
  95.5 0.1 broadcast_in_dim.5
  95.5 14.2 %all_to_all.41.mine = f32[16,2,32,128]{3,2,1,0:T(8,128)S(1)} all-to-all(f32[16,2,32,128]{3,2,1,0:T(8,128)S(1)} %broadcast_in_dim.5), channel_id=1, replica_groups=mesh['y'=4,'z'=8,'x'=4,'core'=2] {'y','x'}, dimensions={0} | all-to-all | bytes 1048576 | tf_op jit(solution)/shard_map/all_to_all | solution.py:25
  109.8 2.9 %collective-permute-start.14 = (f32[16,2,32,128]{3,2,1,0:T(8,128)S(1)}, f32[16,2,32,128]{3,2,1,0:T(8,128)S(1)}, u32[]{:S(2)}, u32[]{:S(2)}) collective-permute-start(f32[16,2,32,128]{3,2,1,0:T(8,128)S(1)} %all_to_all.41.mine), channel_id=1, source_target_pairs={{0,1},{1,0},{8,9},{9,8},{16,17},{17,16},{24,25},{25,24},{32,33},{3... | collective-permute-start | bytes 1572872 | tf_op jit(solution)/shard_map/ppermute | solution.py:258
  112.7 1.5 %collective-permute-done.14.other = f32[16,2,32,128]{3,2,1,0:T(8,128)S(1)} collective-permute-done((f32[16,2,32,128]{3,2,1,0:T(8,128)S(1)}, f32[16,2,32,128]{3,2,1,0:T(8,128)S(1)}, u32[]{:S(2)}, u32[]{:S(2)}) %collective-permute-start.14) | collective-permute-done | bytes 524320 | tf_op jit(solution)/shard_map/ppermute | solution.py:258
  114.2 2.3 %shard_map.83 = (f32[300,128]{1,0:T(8,128)}, f32[300,2,256]{2,1,0:T(2,128)}) custom-call(s32[1]{0:T(128)} %bitcast.member, f32[16,2,32,128]{3,2,1,0:T(8,128)S(1)} %all_to_all.41.mine, f32[16,2,32,128]{3,2,1,0:T(8,128)S(1)} %collective-permute-done.14.other, bf16[128,128]{1,0:T(8,128)(2,1)S(1)} %get-tuple-element.80.rest_0_, ...), custom_call_target="tpu_custom_call" | custom-call | tf_op jit(solution)/shard_map/pallas_call | solution.py:228
  (28 shorter events, 0.2 us)
Async XLA Ops:
  0.6 8.9 %copy-start.6 = (s32[2]{0:T(128)S(1)}, s32[2]{0:T(128)}, u32[]{:S(2)}) copy-start(s32[2]{0:T(128)} %owners.5) | copy-start | bytes 28
  0.6 8.9 %copy-start.3 = (s32[2,256]{1,0:T(2,128)S(1)}, s32[2,256]{1,0:T(2,128)}, u32[]{:S(2)}) copy-start(s32[2,256]{1,0:T(2,128)} %batch_rows.3) | copy-start | bytes 6148
  0.6 60.7 %collective-permute-start.3 = (bf16[128,2048]{1,0:T(8,128)(2,1)}, bf16[128,2048]{1,0:T(8,128)(2,1)S(1)}, u32[]{:S(2)}, u32[]{:S(2)}) collective-permute-start(bf16[128,2048]{1,0:T(8,128)(2,1)} %rest_0_), channel_id=1, source_target_pairs={{0,8},{1,9},{8,0},{9,1},{16,24},{17,25},{24,16},{25,17},{32,40},{3... | collective-permute-start | bytes 1572872 | tf_op jit(solution)/shard_map/ppermute | solution.py:258
  3.2 58.4 %collective-permute-start.2 = (bf16[128,2048]{1,0:T(8,128)(2,1)}, bf16[128,2048]{1,0:T(8,128)(2,1)S(1)}, u32[]{:S(2)}, u32[]{:S(2)}) collective-permute-start(bf16[128,2048]{1,0:T(8,128)(2,1)} %rest_0_), channel_id=1, source_target_pairs={{0,1},{1,0},{8,9},{9,8},{16,17},{17,16},{24,25},{25,24},{32,33},{3... | collective-permute-start | bytes 1572872 | tf_op jit(solution)/shard_map/ppermute | solution.py:258
  4.1 59.3 %collective-permute-start.5 = (f32[300,128]{1,0:T(8,128)}, f32[300,128]{1,0:T(8,128)S(1)}, u32[]{:S(2)}, u32[]{:S(2)}) collective-permute-start(f32[300,128]{1,0:T(8,128)} %bitcast.27), channel_id=1, source_target_pairs={{0,1},{1,0},{8,9},{9,8},{16,17},{17,16},{24,25},{25,24},{32,33},{3... | collective-permute-start | bytes 460808 | tf_op jit(solution)/shard_map/ppermute | solution.py:258
  4.2 56.7 %collective-permute-start.6 = (f32[300,128]{1,0:T(8,128)}, f32[300,128]{1,0:T(8,128)S(1)}, u32[]{:S(2)}, u32[]{:S(2)}) collective-permute-start(f32[300,128]{1,0:T(8,128)} %bitcast.28), channel_id=1, source_target_pairs={{0,8},{1,9},{8,0},{9,1},{16,24},{17,25},{24,16},{25,17},{32,40},{3... | collective-permute-start | bytes 460808 | tf_op jit(solution)/shard_map/ppermute | solution.py:258
  9.6 41.8 %copy-start.2 = (bf16[512,300]{0,1:T(8,128)(2,1)S(1)}, bf16[512,300]{0,1:T(8,128)(2,1)}, u32[]{:S(2)}) copy-start(bf16[512,300]{0,1:T(8,128)(2,1)} %param.9) | copy-start | bytes 921604
  9.6 2.4 %collective-permute-start.1 = (bf16[16,1,8,2048]{3,2,1,0:T(8,128)(2,1)S(1)}, bf16[16,1,8,2048]{3,2,1,0:T(8,128)(2,1)S(1)}, u32[]{:S(2)}, u32[]{:S(2)}) collective-permute-start(bf16[16,1,8,2048]{3,2,1,0:T(8,128)(2,1)S(1)} %get-tuple-element.25), channel_id=1, source_target_pairs={{0,1},{1,0},{8,9},{9,8},{16,17},{17,16},{24,25},{25,24},{32,33},{3... | collective-permute-start | bytes 1572872 | tf_op jit(solution)/shard_map/cond/branch_1_fun/ppermute | solution.py:258
  45.5 7.0 %copy-start = (bf16[128,2048]{1,0:T(8,128)(2,1)S(1)}, bf16[128,2048]{1,0:T(8,128)(2,1)}, u32[]{:S(2)}) copy-start(bf16[128,2048]{1,0:T(8,128)(2,1)} %rest_0_) | copy-start | bytes 1572868
  46.9 16.6 %all-to-all-start.4 = ((bf16[16,8,2048]{2,1,0:T(8,128)(2,1)}), bf16[16,8,2048]{2,1,0:T(8,128)(2,1)S(1)}, u32[]{:S(2)}, u32[]{:S(2)}) async-start(bf16[16,8,2048]{2,1,0:T(8,128)(2,1)} %shard_map.78), calls=%async_computation.4 | async-start | bytes 1048576 | tf_op jit(solution)/shard_map/all_to_all | solution.py:25
  52.4 4.2 %collective-permute-start.8 = (bf16[300,256]{1,0:T(8,128)(2,1)S(1)}, bf16[300,256]{1,0:T(8,128)(2,1)S(1)}, u32[]{:S(2)}, u32[]{:S(2)}) collective-permute-start(bf16[300,256]{1,0:T(8,128)(2,1)S(1)} %get-tuple-element.61), channel_id=1, source_target_pairs={{0,8},{1,9},{8,0},{9,1},{16,24},{17,25},{24,16},{25,17},{32,40},{3... | collective-permute-start | bytes 460808 | tf_op jit(solution)/shard_map/ppermute | solution.py:258
  56.6 4.2 %copy-start.4 = (bf16[300,256]{1,0:T(8,128)(2,1)}, bf16[300,256]{1,0:T(8,128)(2,1)S(1)}, u32[]{:S(2)}) copy-start(bf16[300,256]{1,0:T(8,128)(2,1)S(1)} %add.69) | copy-start | bytes 460804
  56.6 8.9 %copy-start.1 = (f32[128,300]{0,1:T(8,128)S(1)}, f32[128,300]{0,1:T(8,128)}, u32[]{:S(2)}) copy-start(f32[128,300]{0,1:T(8,128)} %param.11) | copy-start | bytes 460804
  56.7 6.8 %collective-permute-start.9 = (bf16[300,128]{1,0:T(8,128)(2,1)S(1)}, bf16[300,128]{1,0:T(8,128)(2,1)S(1)}, u32[]{:S(2)}, u32[]{:S(2)}) collective-permute-start(bf16[300,128]{1,0:T(8,128)(2,1)S(1)} %slice.24), channel_id=1, source_target_pairs={{0,1},{1,0},{8,9},{9,8},{16,17},{17,16},{24,25},{25,24},{32,33},{3... | collective-permute-start | bytes 230408 | tf_op jit(solution)/shard_map/ppermute | solution.py:258
  60.8 2.7 %collective-permute-start.7 = (f32[300,128]{1,0:T(8,128)S(1)}, f32[300,128]{1,0:T(8,128)S(1)}, u32[]{:S(2)}, u32[]{:S(2)}) collective-permute-start(f32[300,128]{1,0:T(8,128)S(1)} %collective-permute-done.6.rest_2_), channel_id=1, source_target_pairs={{0,1},{1,0},{8,9},{9,8},{16,17},{17,16},{24,25},{25,24},{32,33},{3... | collective-permute-start | bytes 460808 | tf_op jit(solution)/shard_map/ppermute | solution.py:258
  61.4 1.9 %collective-permute-start.4 = (bf16[128,2048]{1,0:T(8,128)(2,1)S(1)}, bf16[128,2048]{1,0:T(8,128)(2,1)S(1)}, u32[]{:S(2)}, u32[]{:S(2)}) collective-permute-start(bf16[128,2048]{1,0:T(8,128)(2,1)S(1)} %collective-permute-done.3.rest_2_), channel_id=1, source_target_pairs={{0,1},{1,0},{8,9},{9,8},{16,17},{17,16},{24,25},{25,24},{32,33},{3... | collective-permute-start | bytes 1572872 | tf_op jit(solution)/shard_map/ppermute | solution.py:258
  63.5 2.1 %copy-start.5 = (bf16[300,256]{1,0:T(8,128)(2,1)S(1)}, bf16[300,256]{1,0:T(8,128)(2,1)}, u32[]{:S(2)}) copy-start(bf16[300,256]{1,0:T(8,128)(2,1)} %copy-done.4) | copy-start | bytes 460804
  64.3 4.6 %collective-permute-start.10 = (bf16[4,128,128]{2,1,0:T(8,128)(2,1)S(1)}, bf16[4,128,128]{2,1,0:T(8,128)(2,1)S(1)}, u32[]{:S(2)}, u32[]{:S(2)}) collective-permute-start(bf16[4,128,128]{2,1,0:T(8,128)(2,1)S(1)} %get-tuple-element.78.tile), channel_id=1, source_target_pairs={{0,9},{1,8},{8,0},{9,1},{16,25},{17,24},{24,16},{25,17},{32,41},{3... | collective-permute-start | bytes 393224 | tf_op jit(solution)/shard_map/ppermute | solution.py:258
  69.8 15.1 %all-to-all-start.5 = ((f32[16,32,128]{2,1,0:T(8,128)}), f32[16,32,128]{2,1,0:T(8,128)S(1)}, u32[]{:S(2)}, u32[]{:S(2)}) async-start(f32[16,32,128]{2,1,0:T(8,128)} %bitcast.10), calls=%async_computation.5 | async-start | bytes 524288 | tf_op jit(solution)/shard_map/all_to_all | solution.py:25
  77.2 7.6 %collective-permute-start.11 = (bf16[128,128]{1,0:T(8,128)(2,1)S(1)}, bf16[128,128]{1,0:T(8,128)(2,1)S(1)}, u32[]{:S(2)}, u32[]{:S(2)}) collective-permute-start(bf16[128,128]{1,0:T(8,128)(2,1)S(1)} %get-tuple-element.88), channel_id=1, source_target_pairs={{0,1},{1,0},{8,9},{9,8},{16,17},{17,16},{24,25},{25,24},{32,33},{3... | collective-permute-start | bytes 98312 | tf_op jit(solution)/shard_map/ppermute | solution.py:258
  78.7 6.2 %collective-permute-start.12 = (bf16[128,128]{1,0:T(8,128)(2,1)S(1)}, bf16[128,128]{1,0:T(8,128)(2,1)S(1)}, u32[]{:S(2)}, u32[]{:S(2)}) collective-permute-start(bf16[128,128]{1,0:T(8,128)(2,1)S(1)} %get-tuple-element.87), channel_id=1, source_target_pairs={{0,8},{1,9},{8,0},{9,1},{16,24},{17,25},{24,16},{25,17},{32,40},{3... | collective-permute-start | bytes 98312 | tf_op jit(solution)/shard_map/ppermute | solution.py:258
  78.7 6.2 %collective-permute-start.13 = (bf16[128,128]{1,0:T(8,128)(2,1)S(1)}, bf16[128,128]{1,0:T(8,128)(2,1)S(1)}, u32[]{:S(2)}, u32[]{:S(2)}) collective-permute-start(bf16[128,128]{1,0:T(8,128)(2,1)S(1)} %get-tuple-element.86), channel_id=1, source_target_pairs={{0,9},{1,8},{8,1},{9,0},{16,25},{17,24},{24,17},{25,16},{32,41},{3... | collective-permute-start | bytes 98312 | tf_op jit(solution)/shard_map/ppermute | solution.py:258
  109.8 4.5 %collective-permute-start.14 = (f32[16,2,32,128]{3,2,1,0:T(8,128)S(1)}, f32[16,2,32,128]{3,2,1,0:T(8,128)S(1)}, u32[]{:S(2)}, u32[]{:S(2)}) collective-permute-start(f32[16,2,32,128]{3,2,1,0:T(8,128)S(1)} %all_to_all.41.mine), channel_id=1, source_target_pairs={{0,1},{1,0},{8,9},{9,8},{16,17},{17,16},{24,25},{25,24},{32,33},{3... | collective-permute-start | bytes 1572872 | tf_op jit(solution)/shard_map/ppermute | solution.py:258

commit v7 on v4

--- a/solution.py
+++ b/solution.py
@@ -20,6 +20,7 @@
 CHUNKS = 4
 HIGHEST = lax.Precision.HIGHEST
 NT = (((1,), (1,)), ((), ()))
+NN = (((1,), (0,)), ((), ()))
 
 
 def swap(value):
@@ -69,36 +70,50 @@
     core = here & (sizes[3] - 1)
     plane, slots, each, features = kept.shape
     chunk = features // CHUNKS
-    listing = pltpu.make_async_copy(batch_rows, listed, arrivals.at[CHUNKS])
-    listing.start()
-    loads = []
-    for at in range(CHUNKS):
-        columns = slice(at * chunk, (at + 1) * chunk)
-        load = pltpu.make_async_copy(spectra.at[:, columns], lines.at[:, columns], arrivals.at[at])
-        load.start()
-        loads.append(load)
+    later = owners[1] >> 1 == here >> 1
+    involved = later | (owners[0] >> 1 == here >> 1)
     if flag:
         same_chip = owners[0] >> 1 == owners[1] >> 1
         same_z = place(owners[0], sizes)[1] == place(owners[1], sizes)[1]
         flag[0][0] = jnp.where(same_chip, 0, jnp.where(same_z, 1, 2))
-    listing.wait()
-    spots = []
-    for slot in range(slots):
-        t = slot if slots > 1 else jnp.where(owners[1] >> 1 == here >> 1, 1, 0)
-        own = owners[t] == here
-        both = jnp.concatenate(halves_of(listed, t, core), axis=1)
-        spots.append(chosen(both, lines.shape[0], own))
-    spots = jnp.concatenate(spots, axis=1)
-    for at in range(CHUNKS):
-        columns = slice(at * chunk, (at + 1) * chunk)
-        loads[at].wait()
-        value = lax.dot_general(
-            spots, lines[:, columns], (((0,), (0,)), ((), ())), preferred_element_type=jnp.float32
-        ).astype(kept.dtype)
-        value = value.reshape(slots, 2, plane, each, chunk)
+
+    @pl.when(jnp.logical_not(involved))
+    def _():
+        kept[...] = jnp.zeros_like(kept)
+        sent[...] = jnp.zeros_like(sent)
+
+    @pl.when(involved)
+    def _():
+        listing = pltpu.make_async_copy(batch_rows, listed, arrivals.at[CHUNKS])
+        listing.start()
+        loads = []
+        for at in range(CHUNKS):
+            columns = slice(at * chunk, (at + 1) * chunk)
+            load = pltpu.make_async_copy(
+                spectra.at[:, columns], lines.at[:, columns], arrivals.at[at]
+            )
+            load.start()
+            loads.append(load)
+        listing.wait()
+        spots = []
         for slot in range(slots):
-            kept[:, slot, :, columns] = value[slot, 0]
-            sent[:, slot, :, columns] = value[slot, 1]
+            t = slot if slots > 1 else jnp.where(later, 1, 0)
+            both = jnp.concatenate(halves_of(listed, t, core), axis=1)
+            spots.append(chosen(both, lines.shape[0], owners[t] == here))
+        spots = jnp.concatenate(spots, axis=1)
+        for at in range(CHUNKS):
+            columns = slice(at * chunk, (at + 1) * chunk)
+            loads[at].wait()
+            value = lax.dot_general(
+                spots,
+                lines[:, columns],
+                (((0,), (0,)), ((), ())),
+                preferred_element_type=jnp.float32,
+            ).astype(kept.dtype)
+            value = value.reshape(slots, 2, plane, each, chunk)
+            for slot in range(slots):
+                kept[:, slot, :, columns] = value[slot, 0]
+                sent[:, slot, :, columns] = value[slot, 1]
 
 
 def targets_kernel(device, owners, batch_rows, targets, kept, sent, *, sizes):
@@ -131,13 +146,32 @@
     out[...] = jnp.broadcast_to(scattered[root_y * sizes[2] + root_x, 0][None], out.shape)
 
 
-def arrived_kernel(owners, along, piece, *, sizes):
+def spread_kernel(owners, along, out, *, sizes):
+    plane, _, each, features = out.shape
     for t in range(ITERS):
-        piece[t] = along[place(owners[t], sizes)[1]]
-
-
-def spread_kernel(piece, out):
-    out[...] = jnp.broadcast_to(piece[...][None], out.shape)
+        block = along[place(owners[t], sizes)[1]]
+        out[:, t] = jnp.broadcast_to(block[None], (plane, each, features))
+
+
+def spread_steps_kernel(piece, arrived, out):
+    out[...] = jnp.broadcast_to((piece[...] + arrived[...])[None], out.shape)
+
+
+def pieces_of(value):
+    pieces = []
+    for _ in range(3):
+        piece = value.astype(jnp.bfloat16)
+        pieces.append(piece)
+        value = value - piece.astype(jnp.float32)
+    return pieces
+
+
+def wide_dot(pieces, value, dims):
+    total = None
+    for piece in reversed(pieces):
+        term = lax.dot_general(piece, value, dims, preferred_element_type=jnp.float32)
+        total = term if total is None else total + term
+    return total
 
 
 def tile_kernel(batch, own, other, own_norms, other_norms, tile, *, each, factor):
@@ -164,19 +198,10 @@
     step = aligned(outs)
     lines[...] = jnp.zeros_like(lines)
     held = kept[...].astype(jnp.float32) + arrived[...].astype(jnp.float32)
+    own_pieces, other_pieces = pieces_of(own[...]), pieces_of(other[...])
     for t in range(ITERS):
-        total = lax.dot_general(
-            own[...],
-            tile[t, :, :width].astype(jnp.float32),
-            NT,
-            precision=HIGHEST,
-            preferred_element_type=jnp.float32,
-        ) + lax.dot_general(
-            other[...],
-            tile[t, :, width:].astype(jnp.float32),
-            NT,
-            precision=HIGHEST,
-            preferred_element_type=jnp.float32,
+        total = wide_dot(own_pieces, tile[t, :, :width], NT) + wide_dot(
+            other_pieces, tile[t, :, width:], NT
         )
         lines[t * step : t * step + outs, :] = (
             total / root_scale - held[:, t * count : (t + 1) * count]
@@ -213,12 +238,11 @@
     update = None
     for t, residual in enumerate((first, second)):
         residuals[:, t, :] = residual
-        kept = tile[t, :, :width].astype(jnp.float32)
-        sent = came[t, :, width:].astype(jnp.float32)
+        kept, sent = tile[t, :, :width], came[t, :, width:]
         rows = jnp.concatenate(
             [jnp.where(is_first, kept, sent), jnp.where(is_first, sent, kept)], axis=0
         )
-        term = jnp.dot(residual, rows, precision=HIGHEST, preferred_element_type=jnp.float32)
+        term = wide_dot(pieces_of(residual), rows, NN)
         update = term if update is None else update + term
     trained[...] = coefficients[...] - STEP_RATE / math.sqrt(total) * update
 
@@ -256,10 +280,11 @@
     core = lax.axis_index("core").reshape(1)
     narrow = jnp.bfloat16
     block = pltpu.VMEM((ITERS, each, features), narrow)
+    whole_block = jax.ShapeDtypeStruct((plane, ITERS, each, features), narrow)
 
     def rows_for(slots):
         blocks = pltpu.VMEM((plane, slots, each, features), narrow)
-        flag = (jax.ShapeDtypeStruct((1,), jnp.int32),) if slots == 1 else ()
+        flag = (pltpu.SMEM((1,), jnp.int32),) if slots == 1 else ()
         return call(
             functools.partial(rows_kernel, sizes=sizes),
             (blocks, blocks) + flag,
@@ -281,9 +306,11 @@
             (device, owners, exchange(kept + swap(sent), PLANE)),
             scalars=2,
         )
+        arrived = None
         for mask in Z_MASKS:
-            piece = piece + lax.ppermute(piece, "z", [(i, i ^ mask) for i in range(sizes[1])])
-        return piece
+            piece = piece if arrived is None else piece + arrived
+            arrived = lax.ppermute(piece, "z", [(i, i ^ mask) for i in range(sizes[1])])
+        return call(spread_steps_kernel, whole_block, (piece, arrived))
 
     def at_once(kept, sent):
         along = call(
@@ -293,19 +320,16 @@
             scalars=2,
         )
         return call(
-            functools.partial(arrived_kernel, sizes=sizes),
-            block,
+            functools.partial(spread_kernel, sizes=sizes),
+            whole_block,
             (owners, exchange(along, "z")),
             scalars=1,
         )
 
     kept, sent, apart = rows_for(1)
-    piece = lax.switch(
+    spread_out = lax.switch(
         apart[0],
         (lambda: in_steps(*rows_for(2)), lambda: in_steps(kept, sent), lambda: at_once(kept, sent)),
-    )
-    spread_out = call(
-        spread_kernel, pltpu.VMEM((plane, ITERS, each, features), narrow), (piece,)
     )
     gathered = exchange(spread_out, PLANE).reshape(ITERS * half, features)
 

time: 115 us -> 111 us (0.965)
  Pallas kernels: 10.2 us -> 7.24 us
    pallas_call x8 -> x7, Pallas kernels: 10.2 us -> 7.24 us  [call(): pl.pallas_call(kernel, in_specs=[pl.BlockSpec(memory_space=kind) for kind...]
where the time goes in v7:
time: 111 us
  blocking collectives  69.2 us (62%)
  starting transfers between devices  19.8 us (18%)
  waiting for transfers between devices  13.3 us (12%)
  Pallas kernels  7.24 us (7%)
    all_to_all x5, blocking collectives, exchange(): return lax.all_to_all(blocks, axes, 0, 0, tiled=True)  69.2 us
    ppermute x6, starting transfers between devices, swap(): return lax.ppermute(value, 'core', PAIR)  15.2 us
    all_to_all x1, waiting for transfers between devices, exchange(): return lax.all_to_all(blocks, axes, 0, 0, tiled=True)  9.36 us
    pallas_call x7, Pallas kernels, call(): pl.pallas_call(kernel, in_specs=[pl.BlockSpec(memory_space=kind) for kind...  7.24 us
    all_to_all x1, starting transfers between devices, exchange(): return lax.all_to_all(blocks, axes, 0, 0, tiled=True)  4.62 us
    ppermute x6, waiting for transfers between devices, swap(): return lax.ppermute(value, 'core', PAIR)  3.97 us
  transfers between devices with their start and end apart: 7, of which 4 were waited for; matrix products, arithmetic and copies ran while one was open for 0% of the time, Pallas kernels for 2%

profile of v7, /device:TPU:1, one launch (start us, length us, event | category | flops | bytes accessed | tf_op | source)
XLA Modules:
  0.0 111.0 jit_solution(2977010023360617311)
XLA Ops:
  0.6 0.0 copy-start.4
  0.6 0.0 copy-start.3
  0.7 0.8 shard_map.77
  1.5 0.0 copy-done.4
  1.5 0.0 copy-done.3
  1.5 39.9 %conditional.1 = (bf16[16,2,8,2048]{3,2,1,0:T(8,128)(2,1)}) conditional(s32[]{:T(128)} %bitcast.2, (s32[1]{0:T(128)}, s32[2]{0:T(128)S(1)}, s32[2,256]{1,0:T(2,128)S(1)}, bf16[512,2048]{1,0:T(8,128)(2,1)}) %tuple.24, (bf16[16,1,8,2048]{3,2,1,0:T(8,128)(2,1)S(1)}, bf16[16,1,8,2048]{3,2,1,0:T(8,128)(2,1)S(1)}, s32[1]{0:T(128)}, ...), branch_computations={%region_0.0_spmd, %region_1.0_spmd, %region_2.0_spmd} | conditional | flops 589824 | bytes 10617000 | solution.py:330
  1.6 3.3 %collective-permute-start.8 = (bf16[16,1,8,2048]{3,2,1,0:T(8,128)(2,1)S(1)}, bf16[16,1,8,2048]{3,2,1,0:T(8,128)(2,1)S(1)}, u32[]{:S(2)}, u32[]{:S(2)}) collective-permute-start(bf16[16,1,8,2048]{3,2,1,0:T(8,128)(2,1)S(1)} %get-tuple-element.41), channel_id=1, source_target_pairs={{0,1},{1,0},{2,3},{3,2},{4,5},{5,4},{6,7},{7,6},{8,9},{9,8},{10,11... | collective-permute-start | bytes 1572872 | tf_op jit(solution)/shard_map/cond/branch_2_fun/ppermute | solution.py:27
  4.8 1.5 %collective-permute-done.8 = bf16[16,1,8,2048]{3,2,1,0:T(8,128)(2,1)S(1)} collective-permute-done((bf16[16,1,8,2048]{3,2,1,0:T(8,128)(2,1)S(1)}, bf16[16,1,8,2048]{3,2,1,0:T(8,128)(2,1)S(1)}, u32[]{:S(2)}, u32[]{:S(2)}) %collective-permute-start.8) | collective-permute-done | bytes 524320 | tf_op jit(solution)/shard_map/cond/branch_2_fun/ppermute | solution.py:27
  6.4 0.1 add.46
  6.5 15.6 %all_to_all.38.scattered = bf16[16,1,8,2048]{3,2,1,0:T(8,128)(2,1)S(1)} all-to-all(bf16[16,1,8,2048]{3,2,1,0:T(8,128)(2,1)S(1)} %add.46), channel_id=1, replica_groups=mesh['y'=4,'z'=8,'x'=4,'core'=2] {'y','x'}, dimensions={0} | all-to-all | bytes 1048576 | tf_op jit(solution)/shard_map/cond/branch_2_fun/all_to_all | solution.py:31
  22.1 0.6 branch_2_fun.2
  22.7 17.2 %all_to_all.39.along = bf16[8,8,2048]{2,1,0:T(8,128)(2,1)S(1)} all-to-all(bf16[8,8,2048]{2,1,0:T(8,128)(2,1)S(1)} %branch_2_fun.2), channel_id=1, replica_groups=mesh['y'=4,'z'=8,'x'=4,'core'=2] {'z'}, dimensions={0} | all-to-all | bytes 524288 | tf_op jit(solution)/shard_map/cond/branch_2_fun/all_to_all | solution.py:31
  39.8 1.6 %branch_2_fun.3 = bf16[16,2,8,2048]{3,2,1,0:T(8,128)(2,1)} custom-call(s32[2]{0:T(128)S(1)} %get-tuple-element.38.owners, bf16[8,8,2048]{2,1,0:T(8,128)(2,1)S(1)} %all_to_all.39.along), custom_call_target="tpu_custom_call" | custom-call | tf_op jit(solution)/shard_map/cond/branch_2_fun/pallas_call | solution.py:260
  41.5 0.0 copy-start
  41.5 0.0 copy-start.1
  41.5 0.0 copy-start.2
  41.5 4.6 %all-to-all-start.4 = ((bf16[16,2,8,2048]{3,2,1,0:T(8,128)(2,1)}), bf16[16,2,8,2048]{3,2,1,0:T(8,128)(2,1)S(1)}, u32[]{:S(2)}, u32[]{:S(2)}) async-start(bf16[16,2,8,2048]{3,2,1,0:T(8,128)(2,1)} %get-tuple-element.58), calls=%async_computation.4 | async-start | bytes 2097152 | tf_op jit(solution)/shard_map/all_to_all | solution.py:31
  46.1 0.0 copy-done
  46.1 3.0 %collective-permute-start.9 = (bf16[128,2048]{1,0:T(8,128)(2,1)S(1)}, bf16[128,2048]{1,0:T(8,128)(2,1)S(1)}, u32[]{:S(2)}, u32[]{:S(2)}) collective-permute-start(bf16[128,2048]{1,0:T(8,128)(2,1)S(1)} %copy-done), channel_id=1, source_target_pairs={{0,1},{1,0},{2,3},{3,2},{4,5},{5,4},{6,7},{7,6},{8,9},{9,8},{10,11... | collective-permute-start | bytes 1572872 | tf_op jit(solution)/shard_map/ppermute | solution.py:27
  49.1 0.0 copy-done.1
  49.1 0.1 collective-permute-start.11
  49.2 0.0 copy-done.2
  49.2 1.0 shard_map.79
  50.2 0.7 collective-permute-start.12
  50.9 0.2 multiply_reduce_fusion.1
  51.1 0.0 collective-permute-done.9.other
  51.1 0.2 multiply_reduce_fusion
  51.3 9.4 %all-to-all-done.4 = bf16[16,2,8,2048]{3,2,1,0:T(8,128)(2,1)S(1)} async-done(((bf16[16,2,8,2048]{3,2,1,0:T(8,128)(2,1)}), bf16[16,2,8,2048]{3,2,1,0:T(8,128)(2,1)S(1)}, u32[]{:S(2)}, u32[]{:S(2)}) %all-to-all-start.4) | async-done | bytes 1048608 | tf_op jit(solution)/shard_map/all_to_all | solution.py:31
  60.7 0.7 shard_map.78.tile
  61.4 4.0 %collective-permute-start.10 = (bf16[2,128,256]{2,1,0:T(8,128)(2,1)S(1)}, bf16[2,128,256]{2,1,0:T(8,128)(2,1)S(1)}, u32[]{:S(2)}, u32[]{:S(2)}) collective-permute-start(bf16[2,128,256]{2,1,0:T(8,128)(2,1)S(1)} %shard_map.78.tile), channel_id=1, source_target_pairs={{0,1},{1,0},{2,3},{3,2},{4,5},{5,4},{6,7},{7,6},{8,9},{9,8},{10,11... | collective-permute-start | bytes 393224 | tf_op jit(solution)/shard_map/ppermute | solution.py:27
  65.5 0.0 collective-permute-done.11.other
  65.5 0.0 collective-permute-done.12.arrived
  65.5 1.0 collective-permute-done.10.came
  66.4 0.7 shard_map.80
  67.1 12.7 %all_to_all.40 = f32[16,56,128]{2,1,0:T(8,128)S(1)} all-to-all(f32[16,56,128]{2,1,0:T(8,128)S(1)} %bitcast.17), channel_id=1, replica_groups=mesh['y'=4,'z'=8,'x'=4,'core'=2] {'y','x'}, dimensions={0} | all-to-all | bytes 917504 | tf_op jit(solution)/shard_map/all_to_all | solution.py:31
  79.9 11.5 %all_to_all.41 = f32[8,56,128]{2,1,0:T(8,128)S(1)} all-to-all(f32[8,56,128]{2,1,0:T(8,128)S(1)} %broadcast_in_dim.4), channel_id=1, replica_groups=mesh['y'=4,'z'=8,'x'=4,'core'=2] {'z'}, dimensions={0} | all-to-all | bytes 458752 | tf_op jit(solution)/shard_map/all_to_all | solution.py:31
  91.5 12.3 %all_to_all.42 = f32[16,56,128]{2,1,0:T(8,128)S(1)} all-to-all(f32[16,56,128]{2,1,0:T(8,128)S(1)} %broadcast_in_dim.5), channel_id=1, replica_groups=mesh['y'=4,'z'=8,'x'=4,'core'=2] {'y','x'}, dimensions={0} | all-to-all | bytes 917504 | tf_op jit(solution)/shard_map/all_to_all | solution.py:31
  103.7 4.1 %collective-permute-start.13 = (f32[896,128]{1,0:T(8,128)S(1)}, f32[896,128]{1,0:T(8,128)S(1)}, u32[]{:S(2)}, u32[]{:S(2)}) collective-permute-start(f32[896,128]{1,0:T(8,128)S(1)} %bitcast.15), channel_id=1, source_target_pairs={{0,1},{1,0},{2,3},{3,2},{4,5},{5,4},{6,7},{7,6},{8,9},{9,8},{10,11... | collective-permute-start | bytes 1376264 | tf_op jit(solution)/shard_map/ppermute | solution.py:27
  107.8 1.4 %collective-permute-done.13.other = f32[896,128]{1,0:T(8,128)S(1)} collective-permute-done((f32[896,128]{1,0:T(8,128)S(1)}, f32[896,128]{1,0:T(8,128)S(1)}, u32[]{:S(2)}, u32[]{:S(2)}) %collective-permute-start.13) | collective-permute-done | bytes 458784 | tf_op jit(solution)/shard_map/ppermute | solution.py:27
  109.2 1.8 %shard_map.81 = (f32[300,128]{1,0:T(8,128)}, f32[300,2,256]{2,1,0:T(2,128)}) custom-call(s32[1]{0:T(128)} %bitcast.core, f32[896,128]{1,0:T(8,128)S(1)} %bitcast.16, f32[896,128]{1,0:T(8,128)S(1)} %collective-permute-done.13.other, bf16[2,128,256]{2,1,0:T(8,128)(2,1)S(1)} %shard_map.78.tile, bf16[2,128,256]{2,1,0:T(8,128)(2,1)S(1)} %collective-permute-done.10.came, ...), custom_call_target="tpu_custom_call" | custom-call | tf_op jit(solution)/shard_map/pallas_call | solution.py:260
  (6 shorter events, 0.1 us)
Async XLA Ops:
  0.6 0.9 copy-start.4
  0.6 0.9 copy-start.3
  1.6 4.8 %collective-permute-start.8 = (bf16[16,1,8,2048]{3,2,1,0:T(8,128)(2,1)S(1)}, bf16[16,1,8,2048]{3,2,1,0:T(8,128)(2,1)S(1)}, u32[]{:S(2)}, u32[]{:S(2)}) collective-permute-start(bf16[16,1,8,2048]{3,2,1,0:T(8,128)(2,1)S(1)} %get-tuple-element.41), channel_id=1, source_target_pairs={{0,1},{1,0},{2,3},{3,2},{4,5},{5,4},{6,7},{7,6},{8,9},{9,8},{10,11... | collective-permute-start | bytes 1572872 | tf_op jit(solution)/shard_map/cond/branch_2_fun/ppermute | solution.py:27
  41.5 4.6 %copy-start = (bf16[128,2048]{1,0:T(8,128)(2,1)S(1)}, bf16[128,2048]{1,0:T(8,128)(2,1)}, u32[]{:S(2)}) copy-start(bf16[128,2048]{1,0:T(8,128)(2,1)} %own.1) | copy-start | bytes 1572868
  41.5 7.6 %copy-start.1 = (f32[128,300]{0,1:T(8,128)S(1)}, f32[128,300]{0,1:T(8,128)}, u32[]{:S(2)}) copy-start(f32[128,300]{0,1:T(8,128)} %param.12) | copy-start | bytes 460804
  41.5 7.7 %copy-start.2 = (bf16[512,300]{0,1:T(8,128)(2,1)S(1)}, bf16[512,300]{0,1:T(8,128)(2,1)}, u32[]{:S(2)}) copy-start(bf16[512,300]{0,1:T(8,128)(2,1)} %param.10) | copy-start | bytes 921604
  41.5 19.2 %all-to-all-start.4 = ((bf16[16,2,8,2048]{3,2,1,0:T(8,128)(2,1)}), bf16[16,2,8,2048]{3,2,1,0:T(8,128)(2,1)S(1)}, u32[]{:S(2)}, u32[]{:S(2)}) async-start(bf16[16,2,8,2048]{3,2,1,0:T(8,128)(2,1)} %get-tuple-element.58), calls=%async_computation.4 | async-start | bytes 2097152 | tf_op jit(solution)/shard_map/all_to_all | solution.py:31
  46.1 5.0 %collective-permute-start.9 = (bf16[128,2048]{1,0:T(8,128)(2,1)S(1)}, bf16[128,2048]{1,0:T(8,128)(2,1)S(1)}, u32[]{:S(2)}, u32[]{:S(2)}) collective-permute-start(bf16[128,2048]{1,0:T(8,128)(2,1)S(1)} %copy-done), channel_id=1, source_target_pairs={{0,1},{1,0},{2,3},{3,2},{4,5},{5,4},{6,7},{7,6},{8,9},{9,8},{10,11... | collective-permute-start | bytes 1572872 | tf_op jit(solution)/shard_map/ppermute | solution.py:27
  49.1 16.4 %collective-permute-start.11 = (f32[300,128]{1,0:T(8,128)S(1)}, f32[300,128]{1,0:T(8,128)S(1)}, u32[]{:S(2)}, u32[]{:S(2)}) collective-permute-start(f32[300,128]{1,0:T(8,128)S(1)} %bitcast.18), channel_id=1, source_target_pairs={{0,1},{1,0},{2,3},{3,2},{4,5},{5,4},{6,7},{7,6},{8,9},{9,8},{10,11... | collective-permute-start | bytes 460808 | tf_op jit(solution)/shard_map/ppermute | solution.py:27
  50.2 15.2 %collective-permute-start.12 = (bf16[300,256]{1,0:T(8,128)(2,1)S(1)}, bf16[300,256]{1,0:T(8,128)(2,1)S(1)}, u32[]{:S(2)}, u32[]{:S(2)}) collective-permute-start(bf16[300,256]{1,0:T(8,128)(2,1)S(1)} %get-tuple-element.55), channel_id=1, source_target_pairs={{0,1},{1,0},{2,3},{3,2},{4,5},{5,4},{6,7},{7,6},{8,9},{9,8},{10,11... | collective-permute-start | bytes 460808 | tf_op jit(solution)/shard_map/ppermute | solution.py:27
  61.4 5.0 %collective-permute-start.10 = (bf16[2,128,256]{2,1,0:T(8,128)(2,1)S(1)}, bf16[2,128,256]{2,1,0:T(8,128)(2,1)S(1)}, u32[]{:S(2)}, u32[]{:S(2)}) collective-permute-start(bf16[2,128,256]{2,1,0:T(8,128)(2,1)S(1)} %shard_map.78.tile), channel_id=1, source_target_pairs={{0,1},{1,0},{2,3},{3,2},{4,5},{5,4},{6,7},{7,6},{8,9},{9,8},{10,11... | collective-permute-start | bytes 393224 | tf_op jit(solution)/shard_map/ppermute | solution.py:27
  103.7 5.5 %collective-permute-start.13 = (f32[896,128]{1,0:T(8,128)S(1)}, f32[896,128]{1,0:T(8,128)S(1)}, u32[]{:S(2)}, u32[]{:S(2)}) collective-permute-start(f32[896,128]{1,0:T(8,128)S(1)} %bitcast.15), channel_id=1, source_target_pairs={{0,1},{1,0},{2,3},{3,2},{4,5},{5,4},{6,7},{7,6},{8,9},{9,8},{10,11... | collective-permute-start | bytes 1376264 | tf_op jit(solution)/shard_map/ppermute | solution.py:27

commit v8 on v6

--- a/solution.py
+++ b/solution.py
@@ -19,6 +19,7 @@
 GROUP = 4
 HIGHEST = lax.Precision.HIGHEST
 NT = (((1,), (1,)), ((), ()))
+NN = (((1,), (0,)), ((), ()))
 
 
 def exchange(blocks, axes):
@@ -58,54 +59,70 @@
     return -(-size // 8) * 8
 
 
-def rows_kernel(device, owners, batch_rows, spectra, kept, sent, *rest, sizes):
-    flag, (lines, listed, arrivals) = rest[:-3], rest[-3:]
+def rows_kernel(device, owners, batch_rows, spectra, targets, kept, sent, *rest, sizes):
+    extra, (lines, shown, listed, arrivals) = rest[:-4], rest[-4:]
     here = device[0]
     core = here & (sizes[3] - 1)
     plane, slots, each, features = kept.shape
     chunk = features // CHUNKS
-    listing = pltpu.make_async_copy(batch_rows, listed, arrivals.at[CHUNKS])
-    listing.start()
-    loads = []
-    for at in range(CHUNKS):
-        columns = slice(at * chunk, (at + 1) * chunk)
-        load = pltpu.make_async_copy(spectra.at[:, columns], lines.at[:, columns], arrivals.at[at])
-        load.start()
-        loads.append(load)
-    if flag:
-        flag[0][0] = jnp.where(owners[0] >> 1 == owners[1] >> 1, 0, 1)
-    listing.wait()
-    spots = []
-    for slot in range(slots):
-        t = slot if slots > 1 else jnp.where(owners[1] >> 1 == here >> 1, 1, 0)
-        own = owners[t] == here
-        both = jnp.concatenate(halves_of(listed, t, core), axis=1)
-        spots.append(chosen(both, lines.shape[0], own))
-    spots = jnp.concatenate(spots, axis=1)
-    for at in range(CHUNKS):
-        columns = slice(at * chunk, (at + 1) * chunk)
-        loads[at].wait()
-        value = lax.dot_general(
-            spots, lines[:, columns], (((0,), (0,)), ((), ())), preferred_element_type=jnp.float32
-        ).astype(kept.dtype)
-        value = value.reshape(slots, 2, plane, each, chunk)
+    later = owners[1] >> 1 == here >> 1
+    involved = later | (owners[0] >> 1 == here >> 1)
+    if extra:
+        near, across, flag = extra
+        flag[0] = jnp.where(owners[0] >> 1 == owners[1] >> 1, 0, 1)
+
+    @pl.when(jnp.logical_not(involved))
+    def _():
+        kept[...] = jnp.zeros_like(kept)
+        sent[...] = jnp.zeros_like(sent)
+        for out in extra[:2]:
+            out[...] = jnp.zeros_like(out)
+
+    @pl.when(involved)
+    def _():
+        listing = pltpu.make_async_copy(batch_rows, listed, arrivals.at[CHUNKS])
+        listing.start()
+        loads = []
+        for at in range(CHUNKS):
+            columns = slice(at * chunk, (at + 1) * chunk)
+            load = pltpu.make_async_copy(
+                spectra.at[:, columns], lines.at[:, columns], arrivals.at[at]
+            )
+            load.start()
+            loads.append(load)
+        if extra:
+            showing = pltpu.make_async_copy(targets, shown, arrivals.at[CHUNKS + 1])
+            showing.start()
+        listing.wait()
+        spots = []
         for slot in range(slots):
-            kept[:, slot, :, columns] = value[slot, 0]
-            sent[:, slot, :, columns] = value[slot, 1]
-
-
-def targets_kernel(device, owners, batch_rows, targets, near, across, *, sizes):
-    here = device[0]
-    core = here & (sizes[3] - 1)
-    batch_of = place(here, sizes)[1] & 1
-    half = batch_rows.shape[1] // 2
-    for t, out in ((batch_of, near), (1 - batch_of, across)):
-        for at, rows in enumerate(halves_of(batch_rows, t, core)):
-            out[:, at * half : (at + 1) * half] = jnp.dot(
-                targets[...],
-                chosen(rows, targets.shape[1], owners[t] == here),
+            t = slot if slots > 1 else jnp.where(later, 1, 0)
+            both = jnp.concatenate(halves_of(listed, t, core), axis=1)
+            spots.append(chosen(both, lines.shape[0], owners[t] == here))
+        spots = jnp.concatenate(spots, axis=1)
+        for at in range(CHUNKS):
+            columns = slice(at * chunk, (at + 1) * chunk)
+            loads[at].wait()
+            value = lax.dot_general(
+                spots,
+                lines[:, columns],
+                (((0,), (0,)), ((), ())),
                 preferred_element_type=jnp.float32,
-            ).astype(out.dtype)
+            ).astype(kept.dtype)
+            value = value.reshape(slots, 2, plane, each, chunk)
+            for slot in range(slots):
+                kept[:, slot, :, columns] = value[slot, 0]
+                sent[:, slot, :, columns] = value[slot, 1]
+        if extra:
+            showing.wait()
+            batch_of = place(here, sizes)[1] & 1
+            for t, out in ((batch_of, near), (1 - batch_of, across)):
+                both = jnp.concatenate(halves_of(listed, t, core), axis=1)
+                out[...] = jnp.dot(
+                    shown[...],
+                    chosen(both, lines.shape[0], owners[t] == here),
+                    preferred_element_type=jnp.float32,
+                ).astype(out.dtype)
 
 
 def along_kernel(owners, scattered, out, *, sizes):
@@ -122,8 +139,25 @@
     out[...] = jnp.broadcast_to(along[place(owners[t], sizes)[1]][None], out.shape)
 
 
+def pieces_of(value):
+    pieces = []
+    for _ in range(3):
+        piece = value.astype(jnp.bfloat16)
+        pieces.append(piece)
+        value = value - piece.astype(jnp.float32)
+    return pieces
+
+
+def wide_dot(pieces, value, dims):
+    total = None
+    for piece in reversed(pieces):
+        term = lax.dot_general(piece, value, dims, preferred_element_type=jnp.float32)
+        total = term if total is None else total + term
+    return total
+
+
 def tile_kernel(member, batch, *rest, factor):
-    centers, norms, (tile, turned) = rest[:GROUP], rest[GROUP : 2 * GROUP], rest[2 * GROUP :]
+    centers, norms, (tile, turned, side) = rest[:GROUP], rest[GROUP : 2 * GROUP], rest[2 * GROUP :]
     lines = batch[...]
     lengths = jnp.sqrt(
         jnp.sum(jnp.square(lines.astype(jnp.float32)), axis=1, keepdims=True) + EPSILON
@@ -134,6 +168,7 @@
         value = (scaled + scaled * scaled * scaled / 3.0).astype(tile.dtype)
         turned[at] = value
         tile[member[0] ^ at] = value
+    side[...] = jnp.where(member[0] < 2, turned[2], turned[3])
 
 
 def partial_kernel(turned, *rest, root_scale):
@@ -141,13 +176,7 @@
     outs = lines.shape[0]
     total = None
     for at in range(GROUP):
-        term = lax.dot_general(
-            coefficients[at][...],
-            turned[at].astype(jnp.float32),
-            NT,
-            precision=HIGHEST,
-            preferred_element_type=jnp.float32,
-        )
+        term = wide_dot(pieces_of(coefficients[at][...]), turned[at], NT)
         total = term if total is None else total + term
     held = near[...].astype(jnp.float32) + came[...].astype(jnp.float32)
     lines[...] = total / root_scale - held
@@ -173,8 +202,9 @@
     lines[step + count :] = jnp.zeros((lines.shape[0] - step - count, count), jnp.float32)
 
 
-def finish_kernel(member, mine, other, *rest, total):
-    tiles, (coefficients, trained, residuals, kept) = rest[:GROUP], rest[GROUP:]
+def finish_kernel(
+    member, mine, other, tile, came, paired, beside, coefficients, trained, residuals, kept, *, total
+):
     outs, _ = coefficients.shape
     blocks, _, height, count = mine.shape
     step = aligned(outs)
@@ -203,14 +233,16 @@
         residuals[:, t, :] = residual
         for at in range(2):
             kept[2 * t + at] = residual[:, at * count : (at + 1) * count]
+    given, even = came[member[0]], member[0] < 2
+    tiles = (
+        tile[0],
+        paired[...],
+        jnp.where(even, given, beside[...]),
+        jnp.where(even, beside[...], given),
+    )
     update = None
     for at in range(GROUP):
-        term = jnp.dot(
-            kept[member[0] ^ at],
-            tiles[at][...].astype(jnp.float32),
-            precision=HIGHEST,
-            preferred_element_type=jnp.float32,
-        )
+        term = wide_dot(pieces_of(kept[member[0] ^ at]), tiles[at], NN)
         update = term if update is None else update + term
     trained[...] = coefficients[...] - STEP_RATE / math.sqrt(total) * update
 
@@ -260,20 +292,24 @@
     def by(value, mask):
         return move(value, lambda at: at ^ mask)
 
+    turned = coefficients.T
+    shown = pltpu.VMEM((outs, batch), narrow)
+
     def rows_for(slots):
         blocks = pltpu.VMEM((plane, slots, each, features), narrow)
-        flag = (jax.ShapeDtypeStruct((1,), jnp.int32),) if slots == 1 else ()
+        extra = (shown, shown, pltpu.SMEM((1,), jnp.int32)) if slots == 1 else ()
         return call(
             functools.partial(rows_kernel, sizes=sizes),
-            (blocks, blocks) + flag,
-            (device, owners, batch_rows, spectra),
+            (blocks, blocks) + extra,
+            (device, owners, batch_rows, spectra, targets.T),
             scalars=2,
-            out_kinds=[pltpu.VMEM, pltpu.VMEM] + [pltpu.SMEM] * len(flag),
-            in_place=(2, 3),
+            out_kinds=[pltpu.VMEM] * (2 + len(extra[:2])) + [pltpu.SMEM] * len(extra[2:]),
+            in_place=(2, 3, 4),
             scratch=(
                 pltpu.VMEM(spectra.shape, narrow),
+                pltpu.VMEM(targets.shape[::-1], narrow),
                 pltpu.VMEM(batch_rows.shape, jnp.int32),
-                pltpu.SemaphoreType.DMA((CHUNKS + 1,)),
+                pltpu.SemaphoreType.DMA((CHUNKS + 2,)),
             ),
         )
 
@@ -288,7 +324,7 @@
     def reach(kept, sent):
         return exchange(scatter(kept, sent), "z")
 
-    kept, sent, apart = rows_for(1)
+    kept, sent, near, across, apart = rows_for(1)
     along = lax.cond(apart[0] != 0, lambda: reach(kept, sent), lambda: reach(*rows_for(2)))
     spread_out = call(
         functools.partial(spread_kernel, sizes=sizes),
@@ -296,19 +332,11 @@
         (device, owners, along),
         scalars=2,
     )
+    near = near + by(across, 2)
+    near, turned, spread_out = lax.optimization_barrier((near, turned, spread_out))
+    came_targets = by(near[:, half:], 1)
     gathered = exchange(spread_out, PLANE).reshape(half, features)
 
-    shown = pltpu.VMEM((outs, batch), narrow)
-    near, across = call(
-        functools.partial(targets_kernel, sizes=sizes),
-        (shown, shown),
-        (device, owners, batch_rows, targets.T),
-        scalars=2,
-    )
-    near = near + by(across, 2)
-    came_targets = by(near[:, half:], 1)
-
-    turned = coefficients.T
     both_centers = [centers, by(centers, 2)]
     both_coefficients = [turned, by(turned, 2)]
     all_centers = [both_centers[0], by(both_centers[0], 1), both_centers[1], by(both_centers[1], 1)]
@@ -324,9 +352,9 @@
         (gathered, all_centers, all_coefficients, near, came_targets, norms)
     )
     square = pltpu.VMEM((GROUP, half, width), narrow)
-    tile, turned_tile = call(
+    tile, turned_tile, side = call(
         functools.partial(tile_kernel, factor=math.sqrt(features)),
-        (square, square),
+        (square, square, pltpu.VMEM((half, width), narrow)),
         (member, gathered, *all_centers, *norms),
         scalars=1,
     )
@@ -343,9 +371,10 @@
         (member, partial, tile, came),
         scalars=1,
     )
-    tiles = [turned_tile[0]] + [by(turned_tile[at], at) for at in range(1, GROUP)]
+    paired = by(turned_tile[1], 1)
+    beside = move(side, lambda at: at ^ 2 if at < 2 else at ^ 3)
+    lines, paired, beside = lax.optimization_barrier((lines, paired, beside))
     own = exchange(lines.reshape(plane, height, half), PLANE).sum(axis=0)
-    own, tiles = lax.optimization_barrier((own, tiles))
     own = copies(own, "z").reshape(z_size // 2, 2, height, half).sum(axis=0)
     whole = copies(own, PLANE)
     trained, residuals = call(
@@ -354,7 +383,7 @@
             jax.ShapeDtypeStruct((outs, width), jnp.float32),
             jax.ShapeDtypeStruct((outs, ITERS, batch), jnp.float32),
         ),
-        (member, whole, by(whole, 1), *tiles, turned),
+        (member, whole, by(whole, 1), turned_tile, came, paired, beside, turned),
         scalars=1,
         scratch=(pltpu.VMEM((GROUP, outs, half), jnp.float32),),
     )

time: 117 us -> 113 us (0.966)
  blocking collectives: 57.5 us -> 67.1 us
  starting transfers between devices: 30.1 us -> 21.8 us
  Pallas kernels: 10.8 us -> 6.72 us
    all_to_all x4 -> x5, blocking collectives: 57.5 us -> 67.1 us  [exchange(): return lax.all_to_all(blocks, axes, 0, 0, tiled=True)]
    all_to_all x2 -> x1, starting transfers between devices: 11.9 us -> 3.57 us  [exchange(): return lax.all_to_all(blocks, axes, 0, 0, tiled=True)]
    pallas_call x8 -> x7, Pallas kernels: 10.8 us -> 6.72 us  [call(): pl.pallas_call(kernel, in_specs=[pl.BlockSpec(memory_space=kind) for kind...]
    ppermute x14 -> x13, waiting for transfers between devices: 11 us -> 7.01 us  [move(): return lax.ppermute(value, ('z', 'core'), pairs)]
    all_to_all x2 -> x1, waiting for transfers between devices: 4.45 us -> 7.98 us  [exchange(): return lax.all_to_all(blocks, axes, 0, 0, tiled=True)]
    ppermute x14 -> x13, starting transfers between devices: 18.2 us -> 18.2 us  [move(): return lax.ppermute(value, ('z', 'core'), pairs)]
  transfers between devices with their start and end apart: 16 -> 14, of which waited for: 6 -> 6; matrix products, arithmetic and copies ran while one was open for 1% -> 1% of each run, Pallas kernels for 6% -> 3%
where the time goes in v8:
time: 113 us; the launch traced here: 112 us
  blocking collectives  67.1 us (59%)
  starting transfers between devices  21.8 us (19%)
  waiting for transfers between devices  15 us (13%)
  Pallas kernels  6.72 us (6%)
    all_to_all x5, blocking collectives, exchange(): return lax.all_to_all(blocks, axes, 0, 0, tiled=True)  67.1 us
    ppermute x13, starting transfers between devices, move(): return lax.ppermute(value, ('z', 'core'), pairs)  18.2 us
    all_to_all x1, waiting for transfers between devices, exchange(): return lax.all_to_all(blocks, axes, 0, 0, tiled=True)  7.98 us
    ppermute x13, waiting for transfers between devices, move(): return lax.ppermute(value, ('z', 'core'), pairs)  7.01 us
    pallas_call x7, Pallas kernels, call(): pl.pallas_call(kernel, in_specs=[pl.BlockSpec(memory_space=kind) for kind...  6.72 us
    all_to_all x1, starting transfers between devices, exchange(): return lax.all_to_all(blocks, axes, 0, 0, tiled=True)  3.57 us
  transfers between devices with their start and end apart: 14, of which 6 were waited for; matrix products, arithmetic and copies ran while one was open for 1% of the time, Pallas kernels for 3%

profile of v8, /device:TPU:1, one launch (start us, length us, event | category | flops | bytes accessed | tf_op | source)
XLA Modules:
  0.0 112.4 jit_solution(398545732897330911)
XLA Ops:
  0.6 2.5 %collective-permute-start.4 = (bf16[128,2048]{1,0:T(8,128)(2,1)}, bf16[128,2048]{1,0:T(8,128)(2,1)S(1)}, u32[]{:S(2)}, u32[]{:S(2)}) collective-permute-start(bf16[128,2048]{1,0:T(8,128)(2,1)} %rest_0_), channel_id=1, source_target_pairs={{0,8},{1,9},{8,0},{9,1},{16,24},{17,25},{24,16},{25,17},{32,40},{3... | collective-permute-start | bytes 1572872 | tf_op jit(solution)/shard_map/ppermute | solution.py:290
  3.2 1.0 collective-permute-start.3
  4.1 0.8 shard_map.77
  5.0 1.6 %collective-permute-start.2 = (bf16[300,256]{1,0:T(8,128)(2,1)S(1)}, bf16[300,256]{1,0:T(8,128)(2,1)S(1)}, u32[]{:S(2)}, u32[]{:S(2)}) collective-permute-start(bf16[300,256]{1,0:T(8,128)(2,1)S(1)} %get-tuple-element.63), channel_id=1, source_target_pairs={{0,8},{1,9},{8,0},{9,1},{16,24},{17,25},{24,16},{25,17},{32,40},{3... | collective-permute-start | bytes 460808 | tf_op jit(solution)/shard_map/ppermute | solution.py:290
  6.6 36.3 %conditional.1 = (bf16[8,8,2048]{2,1,0:T(8,128)(2,1)S(1)}) conditional(s32[]{:T(128)} %bitcast.5, (bf16[512,300]{0,1:T(8,128)(2,1)}, s32[1]{0:T(128)}, s32[2]{0:T(128)S(1)}, s32[2,256]{1,0:T(2,128)}, bf16[512,2048]{1,0:T(8,128)(2,1)}) %tuple.25, (bf16[16,1,8,2048]{3,2,1,0:T(8,128)(2,1)S(1)}, bf16[16,1,8,2048]{3,2,1,0:T(8,128)(2,1)S(1)}, ...), branch_computations={%region_0.0_spmd, %region_1.0_spmd} | conditional | flops 524288 | bytes 9961520 | solution.py:328
  6.6 0.3 collective-permute-start.1
  6.9 1.6 %collective-permute-done.1 = bf16[16,1,8,2048]{3,2,1,0:T(8,128)(2,1)S(1)} collective-permute-done((bf16[16,1,8,2048]{3,2,1,0:T(8,128)(2,1)S(1)}, bf16[16,1,8,2048]{3,2,1,0:T(8,128)(2,1)S(1)}, u32[]{:S(2)}, u32[]{:S(2)}) %collective-permute-start.1) | collective-permute-done | bytes 524320 | tf_op jit(solution)/shard_map/cond/branch_1_fun/ppermute | solution.py:290
  8.5 0.1 add.55
  8.6 16.1 %all_to_all.38.scattered = bf16[16,1,8,2048]{3,2,1,0:T(8,128)(2,1)S(1)} all-to-all(bf16[16,1,8,2048]{3,2,1,0:T(8,128)(2,1)S(1)} %add.55), channel_id=1, replica_groups=mesh['y'=4,'z'=8,'x'=4,'core'=2] {'y','x'}, dimensions={0} | all-to-all | bytes 1048576 | tf_op jit(solution)/shard_map/cond/branch_1_fun/all_to_all | solution.py:26
  24.7 0.6 branch_1_fun.1
  25.3 17.6 %all_to_all.39 = bf16[8,8,2048]{2,1,0:T(8,128)(2,1)S(1)} all-to-all(bf16[8,8,2048]{2,1,0:T(8,128)(2,1)S(1)} %branch_1_fun.1), channel_id=1, replica_groups=mesh['y'=4,'z'=8,'x'=4,'core'=2] {'z'}, dimensions={0} | all-to-all | bytes 524288 | tf_op jit(solution)/shard_map/cond/branch_1_fun/all_to_all | solution.py:26
  42.9 1.4 %shard_map.78 = bf16[16,8,2048]{2,1,0:T(8,128)(2,1)} custom-call(s32[1]{0:T(128)} %bitcast.2.device, s32[2]{0:T(128)S(1)} %copy-done.4, bf16[8,8,2048]{2,1,0:T(8,128)(2,1)S(1)} %get-tuple-element.93.along), custom_call_target="tpu_custom_call" | custom-call | tf_op jit(solution)/shard_map/pallas_call | solution.py:260
  44.3 0.2 multiply_reduce_fusion.3
  44.5 0.0 collective-permute-done.2
  44.6 0.0 copy-start.2
  44.6 0.3 collective-permute-start.7
  44.9 4.0 %collective-permute-start.6 = (f32[300,128]{1,0:T(8,128)S(1)}, f32[300,128]{1,0:T(8,128)S(1)}, u32[]{:S(2)}, u32[]{:S(2)}) collective-permute-start(f32[300,128]{1,0:T(8,128)S(1)} %bitcast.24), channel_id=1, source_target_pairs={{0,1},{1,0},{8,9},{9,8},{16,17},{17,16},{24,25},{25,24},{32,33},{3... | collective-permute-start | bytes 460808 | tf_op jit(solution)/shard_map/ppermute | solution.py:290
  48.8 3.6 %all-to-all-start.4 = ((bf16[16,8,2048]{2,1,0:T(8,128)(2,1)}), bf16[16,8,2048]{2,1,0:T(8,128)(2,1)S(1)}, u32[]{:S(2)}, u32[]{:S(2)}) async-start(bf16[16,8,2048]{2,1,0:T(8,128)(2,1)} %shard_map.78), calls=%async_computation.4 | async-start | bytes 1048576 | tf_op jit(solution)/shard_map/all_to_all | solution.py:26
  52.4 0.1 collective-permute-start.9
  52.6 0.0 collective-permute-done.7.rest_2_
  52.6 0.9 collective-permute-start.8
  53.5 0.0 collective-permute-done.4.rest_2_
  53.5 0.0 collective-permute-start.5
  53.5 0.2 multiply_reduce_fusion.1
  53.7 0.0 collective-permute-done.3.rest_1_
  53.7 0.2 multiply_reduce_fusion.2
  53.9 1.5 %collective-permute-done.5.rest_3_ = bf16[128,2048]{1,0:T(8,128)(2,1)S(1)} collective-permute-done((bf16[128,2048]{1,0:T(8,128)(2,1)S(1)}, bf16[128,2048]{1,0:T(8,128)(2,1)S(1)}, u32[]{:S(2)}, u32[]{:S(2)}) %collective-permute-start.5) | collective-permute-done | bytes 524320 | tf_op jit(solution)/shard_map/ppermute | solution.py:290
  55.4 0.2 multiply_reduce_fusion
  55.6 0.0 collective-permute-done.9.rest_5_
  55.6 0.0 collective-permute-done.6.rest_1_
  55.6 0.0 collective-permute-done.8.rest_3_
  55.6 8.0 %all-to-all-done.4 = bf16[16,8,2048]{2,1,0:T(8,128)(2,1)S(1)} async-done(((bf16[16,8,2048]{2,1,0:T(8,128)(2,1)}), bf16[16,8,2048]{2,1,0:T(8,128)(2,1)S(1)}, u32[]{:S(2)}, u32[]{:S(2)}) %all-to-all-start.4) | async-done | bytes 524320 | tf_op jit(solution)/shard_map/all_to_all | solution.py:26
  63.6 0.8 shard_map.79
  64.4 2.4 %collective-permute-start.10 = (bf16[4,128,128]{2,1,0:T(8,128)(2,1)S(1)}, bf16[4,128,128]{2,1,0:T(8,128)(2,1)S(1)}, u32[]{:S(2)}, u32[]{:S(2)}) collective-permute-start(bf16[4,128,128]{2,1,0:T(8,128)(2,1)S(1)} %get-tuple-element.86.tile), channel_id=1, source_target_pairs={{0,9},{1,8},{8,0},{9,1},{16,25},{17,24},{24,16},{25,17},{32,41},{3... | collective-permute-start | bytes 393224 | tf_op jit(solution)/shard_map/ppermute | solution.py:290
  66.8 0.0 collective-permute-start.11
  66.8 0.7 collective-permute-start.12
  67.5 0.7 shard_map.80.partial
  68.1 1.7 %collective-permute-done.10.came = bf16[4,128,128]{2,1,0:T(8,128)(2,1)S(1)} collective-permute-done((bf16[4,128,128]{2,1,0:T(8,128)(2,1)S(1)}, bf16[4,128,128]{2,1,0:T(8,128)(2,1)S(1)}, u32[]{:S(2)}, u32[]{:S(2)}) %collective-permute-start.10) | collective-permute-done | bytes 131104 | tf_op jit(solution)/shard_map/ppermute | solution.py:290
  69.9 0.2 shard_map.81
  70.1 0.0 collective-permute-done.11.paired
  70.1 0.6 collective-permute-done.12.beside
  70.7 10.7 %all_to_all.40 = f32[16,32,128]{2,1,0:T(8,128)S(1)} all-to-all(f32[16,32,128]{2,1,0:T(8,128)S(1)} %bitcast.22), channel_id=1, replica_groups=mesh['y'=4,'z'=8,'x'=4,'core'=2] {'y','x'}, dimensions={0} | all-to-all | bytes 524288 | tf_op jit(solution)/shard_map/all_to_all | solution.py:26
  81.4 11.1 %all_to_all.41 = f32[8,32,128]{2,1,0:T(8,128)S(1)} all-to-all(f32[8,32,128]{2,1,0:T(8,128)S(1)} %broadcast_in_dim.4), channel_id=1, replica_groups=mesh['y'=4,'z'=8,'x'=4,'core'=2] {'z'}, dimensions={0} | all-to-all | bytes 262144 | tf_op jit(solution)/shard_map/all_to_all | solution.py:26
  92.5 0.1 broadcast_in_dim.5
  92.6 11.6 %all_to_all.42.mine = f32[16,2,32,128]{3,2,1,0:T(8,128)S(1)} all-to-all(f32[16,2,32,128]{3,2,1,0:T(8,128)S(1)} %broadcast_in_dim.5), channel_id=1, replica_groups=mesh['y'=4,'z'=8,'x'=4,'core'=2] {'y','x'}, dimensions={0} | all-to-all | bytes 1048576 | tf_op jit(solution)/shard_map/all_to_all | solution.py:26
  104.2 4.4 %collective-permute-start.13 = (f32[16,2,32,128]{3,2,1,0:T(8,128)S(1)}, f32[16,2,32,128]{3,2,1,0:T(8,128)S(1)}, u32[]{:S(2)}, u32[]{:S(2)}) collective-permute-start(f32[16,2,32,128]{3,2,1,0:T(8,128)S(1)} %all_to_all.42.mine), channel_id=1, source_target_pairs={{0,1},{1,0},{8,9},{9,8},{16,17},{17,16},{24,25},{25,24},{32,33},{3... | collective-permute-start | bytes 1572872 | tf_op jit(solution)/shard_map/ppermute | solution.py:290
  108.6 1.5 %collective-permute-done.13.other = f32[16,2,32,128]{3,2,1,0:T(8,128)S(1)} collective-permute-done((f32[16,2,32,128]{3,2,1,0:T(8,128)S(1)}, f32[16,2,32,128]{3,2,1,0:T(8,128)S(1)}, u32[]{:S(2)}, u32[]{:S(2)}) %collective-permute-start.13) | collective-permute-done | bytes 524320 | tf_op jit(solution)/shard_map/ppermute | solution.py:290
  110.1 2.3 %shard_map.82 = (f32[300,128]{1,0:T(8,128)}, f32[300,2,256]{2,1,0:T(2,128)}) custom-call(s32[1]{0:T(128)} %bitcast.1.member, f32[16,2,32,128]{3,2,1,0:T(8,128)S(1)} %all_to_all.42.mine, f32[16,2,32,128]{3,2,1,0:T(8,128)S(1)} %collective-permute-done.13.other, bf16[4,128,128]{2,1,0:T(8,128)(2,1)S(1)} %get-tuple-element.79.turned.tile, ...), custom_call_target="tpu_custom_call" | custom-call | tf_op jit(solution)/shard_map/pallas_call | solution.py:260
  (20 shorter events, 0.2 us)
Async XLA Ops:
  0.6 6.0 %copy-start.4 = (s32[2]{0:T(128)S(1)}, s32[2]{0:T(128)}, u32[]{:S(2)}) copy-start(s32[2]{0:T(128)} %owners.3) | copy-start | bytes 28
  0.6 52.9 %collective-permute-start.4 = (bf16[128,2048]{1,0:T(8,128)(2,1)}, bf16[128,2048]{1,0:T(8,128)(2,1)S(1)}, u32[]{:S(2)}, u32[]{:S(2)}) collective-permute-start(bf16[128,2048]{1,0:T(8,128)(2,1)} %rest_0_), channel_id=1, source_target_pairs={{0,8},{1,9},{8,0},{9,1},{16,24},{17,25},{24,16},{25,17},{32,40},{3... | collective-permute-start | bytes 1572872 | tf_op jit(solution)/shard_map/ppermute | solution.py:290
  3.2 50.5 %collective-permute-start.3 = (bf16[128,2048]{1,0:T(8,128)(2,1)}, bf16[128,2048]{1,0:T(8,128)(2,1)S(1)}, u32[]{:S(2)}, u32[]{:S(2)}) collective-permute-start(bf16[128,2048]{1,0:T(8,128)(2,1)} %rest_0_), channel_id=1, source_target_pairs={{0,1},{1,0},{8,9},{9,8},{16,17},{17,16},{24,25},{25,24},{32,33},{3... | collective-permute-start | bytes 1572872 | tf_op jit(solution)/shard_map/ppermute | solution.py:290
  5.0 39.5 %collective-permute-start.2 = (bf16[300,256]{1,0:T(8,128)(2,1)S(1)}, bf16[300,256]{1,0:T(8,128)(2,1)S(1)}, u32[]{:S(2)}, u32[]{:S(2)}) collective-permute-start(bf16[300,256]{1,0:T(8,128)(2,1)S(1)} %get-tuple-element.63), channel_id=1, source_target_pairs={{0,8},{1,9},{8,0},{9,1},{16,24},{17,25},{24,16},{25,17},{32,40},{3... | collective-permute-start | bytes 460808 | tf_op jit(solution)/shard_map/ppermute | solution.py:290
  6.6 37.7 %copy-start = (bf16[128,2048]{1,0:T(8,128)(2,1)S(1)}, bf16[128,2048]{1,0:T(8,128)(2,1)}, u32[]{:S(2)}) copy-start(bf16[128,2048]{1,0:T(8,128)(2,1)} %rest_0_) | copy-start | bytes 1572868
  6.6 38.0 %copy-start.1 = (f32[128,300]{0,1:T(8,128)S(1)}, f32[128,300]{0,1:T(8,128)}, u32[]{:S(2)}) copy-start(f32[128,300]{0,1:T(8,128)} %param.11) | copy-start | bytes 460804
  6.6 1.9 %collective-permute-start.1 = (bf16[16,1,8,2048]{3,2,1,0:T(8,128)(2,1)S(1)}, bf16[16,1,8,2048]{3,2,1,0:T(8,128)(2,1)S(1)}, u32[]{:S(2)}, u32[]{:S(2)}) collective-permute-start(bf16[16,1,8,2048]{3,2,1,0:T(8,128)(2,1)S(1)} %get-tuple-element.28), channel_id=1, source_target_pairs={{0,1},{1,0},{8,9},{9,8},{16,17},{17,16},{24,25},{25,24},{32,33},{3... | collective-permute-start | bytes 1572872 | tf_op jit(solution)/shard_map/cond/branch_1_fun/ppermute | solution.py:290
  44.6 7.9 %copy-start.2 = (bf16[300,256]{1,0:T(8,128)(2,1)}, bf16[300,256]{1,0:T(8,128)(2,1)S(1)}, u32[]{:S(2)}) copy-start(bf16[300,256]{1,0:T(8,128)(2,1)S(1)} %add.69) | copy-start | bytes 460804
  44.6 8.0 %collective-permute-start.7 = (f32[300,128]{1,0:T(8,128)S(1)}, f32[300,128]{1,0:T(8,128)S(1)}, u32[]{:S(2)}, u32[]{:S(2)}) collective-permute-start(f32[300,128]{1,0:T(8,128)S(1)} %bitcast.23), channel_id=1, source_target_pairs={{0,8},{1,9},{8,0},{9,1},{16,24},{17,25},{24,16},{25,17},{32,40},{3... | collective-permute-start | bytes 460808 | tf_op jit(solution)/shard_map/ppermute | solution.py:290
  44.9 10.8 %collective-permute-start.6 = (f32[300,128]{1,0:T(8,128)S(1)}, f32[300,128]{1,0:T(8,128)S(1)}, u32[]{:S(2)}, u32[]{:S(2)}) collective-permute-start(f32[300,128]{1,0:T(8,128)S(1)} %bitcast.24), channel_id=1, source_target_pairs={{0,1},{1,0},{8,9},{9,8},{16,17},{17,16},{24,25},{25,24},{32,33},{3... | collective-permute-start | bytes 460808 | tf_op jit(solution)/shard_map/ppermute | solution.py:290
  48.8 14.8 %all-to-all-start.4 = ((bf16[16,8,2048]{2,1,0:T(8,128)(2,1)}), bf16[16,8,2048]{2,1,0:T(8,128)(2,1)S(1)}, u32[]{:S(2)}, u32[]{:S(2)}) async-start(bf16[16,8,2048]{2,1,0:T(8,128)(2,1)} %shard_map.78), calls=%async_computation.4 | async-start | bytes 1048576 | tf_op jit(solution)/shard_map/all_to_all | solution.py:26
  52.4 3.2 %collective-permute-start.9 = (bf16[300,128]{1,0:T(8,128)(2,1)S(1)}, bf16[300,128]{1,0:T(8,128)(2,1)S(1)}, u32[]{:S(2)}, u32[]{:S(2)}) collective-permute-start(bf16[300,128]{1,0:T(8,128)(2,1)S(1)} %slice.9), channel_id=1, source_target_pairs={{0,1},{1,0},{8,9},{9,8},{16,17},{17,16},{24,25},{25,24},{32,33},{3... | collective-permute-start | bytes 230408 | tf_op jit(solution)/shard_map/ppermute | solution.py:290
  52.6 3.0 %collective-permute-start.8 = (f32[300,128]{1,0:T(8,128)S(1)}, f32[300,128]{1,0:T(8,128)S(1)}, u32[]{:S(2)}, u32[]{:S(2)}) collective-permute-start(f32[300,128]{1,0:T(8,128)S(1)} %collective-permute-done.7.rest_2_), channel_id=1, source_target_pairs={{0,1},{1,0},{8,9},{9,8},{16,17},{17,16},{24,25},{25,24},{32,33},{3... | collective-permute-start | bytes 460808 | tf_op jit(solution)/shard_map/ppermute | solution.py:290
  53.5 1.9 %collective-permute-start.5 = (bf16[128,2048]{1,0:T(8,128)(2,1)S(1)}, bf16[128,2048]{1,0:T(8,128)(2,1)S(1)}, u32[]{:S(2)}, u32[]{:S(2)}) collective-permute-start(bf16[128,2048]{1,0:T(8,128)(2,1)S(1)} %collective-permute-done.4.rest_2_), channel_id=1, source_target_pairs={{0,1},{1,0},{8,9},{9,8},{16,17},{17,16},{24,25},{25,24},{32,33},{3... | collective-permute-start | bytes 1572872 | tf_op jit(solution)/shard_map/ppermute | solution.py:290
  63.6 3.8 %copy-start.3 = (bf16[300,256]{1,0:T(8,128)(2,1)S(1)}, bf16[300,256]{1,0:T(8,128)(2,1)}, u32[]{:S(2)}) copy-start(bf16[300,256]{1,0:T(8,128)(2,1)} %copy-done.2) | copy-start | bytes 460804
  64.4 5.5 %collective-permute-start.10 = (bf16[4,128,128]{2,1,0:T(8,128)(2,1)S(1)}, bf16[4,128,128]{2,1,0:T(8,128)(2,1)S(1)}, u32[]{:S(2)}, u32[]{:S(2)}) collective-permute-start(bf16[4,128,128]{2,1,0:T(8,128)(2,1)S(1)} %get-tuple-element.86.tile), channel_id=1, source_target_pairs={{0,9},{1,8},{8,0},{9,1},{16,25},{17,24},{24,16},{25,17},{32,41},{3... | collective-permute-start | bytes 393224 | tf_op jit(solution)/shard_map/ppermute | solution.py:290
  66.8 3.3 %collective-permute-start.11 = (bf16[128,128]{1,0:T(8,128)(2,1)S(1)}, bf16[128,128]{1,0:T(8,128)(2,1)S(1)}, u32[]{:S(2)}, u32[]{:S(2)}) collective-permute-start(bf16[128,128]{1,0:T(8,128)(2,1)S(1)} %slice_bitcast_fusion), channel_id=1, source_target_pairs={{0,1},{1,0},{8,9},{9,8},{16,17},{17,16},{24,25},{25,24},{32,33},{3... | collective-permute-start | bytes 98312 | tf_op jit(solution)/shard_map/ppermute | solution.py:290
  66.8 3.9 %collective-permute-start.12 = (bf16[128,128]{1,0:T(8,128)(2,1)S(1)}, bf16[128,128]{1,0:T(8,128)(2,1)S(1)}, u32[]{:S(2)}, u32[]{:S(2)}) collective-permute-start(bf16[128,128]{1,0:T(8,128)(2,1)S(1)} %get-tuple-element.87), channel_id=1, source_target_pairs={{0,8},{1,9},{8,1},{9,0},{16,24},{17,25},{24,17},{25,16},{32,40},{3... | collective-permute-start | bytes 98312 | tf_op jit(solution)/shard_map/ppermute | solution.py:290
  104.2 5.9 %collective-permute-start.13 = (f32[16,2,32,128]{3,2,1,0:T(8,128)S(1)}, f32[16,2,32,128]{3,2,1,0:T(8,128)S(1)}, u32[]{:S(2)}, u32[]{:S(2)}) collective-permute-start(f32[16,2,32,128]{3,2,1,0:T(8,128)S(1)} %all_to_all.42.mine), channel_id=1, source_target_pairs={{0,1},{1,0},{8,9},{9,8},{16,17},{17,16},{24,25},{25,24},{32,33},{3... | collective-permute-start | bytes 1572872 | tf_op jit(solution)/shard_map/ppermute | solution.py:290

commit v9 on v8

--- a/solution.py
+++ b/solution.py
@@ -8,6 +8,7 @@
 from jax.experimental.pallas import tpu as pltpu
 from jax.sharding import Mesh
 from jax.sharding import PartitionSpec as P
+
 
 ITERS = 2
 AXES = ("y", "z", "x", "core")
@@ -73,8 +74,6 @@
 
     @pl.when(jnp.logical_not(involved))
     def _():
-        kept[...] = jnp.zeros_like(kept)
-        sent[...] = jnp.zeros_like(sent)
         for out in extra[:2]:
             out[...] = jnp.zeros_like(out)
 
@@ -173,7 +172,6 @@
 
 def partial_kernel(turned, *rest, root_scale):
     coefficients, (near, came, lines) = rest[:GROUP], rest[GROUP:]
-    outs = lines.shape[0]
     total = None
     for at in range(GROUP):
         term = wide_dot(pieces_of(coefficients[at][...]), turned[at], NT)
@@ -203,7 +201,7 @@
 
 
 def finish_kernel(
-    member, mine, other, tile, came, paired, beside, coefficients, trained, residuals, kept, *, total
+    member, mine, other, tile, came, paired, beside, coefficients, trained, residuals, tiles, *, total
 ):
     outs, _ = coefficients.shape
     blocks, _, height, count = mine.shape
@@ -229,20 +227,16 @@
     second = second - STEP_RATE / total * jnp.dot(
         first, gram, precision=HIGHEST, preferred_element_type=jnp.float32
     )
+    given, even = came[member[0]], member[0] < 2
+    tiles[member[0]] = tile[0]
+    tiles[member[0] ^ 1] = paired[...]
+    tiles[member[0] ^ 2] = jnp.where(even, given, beside[...])
+    tiles[member[0] ^ 3] = jnp.where(even, beside[...], given)
+    update = None
     for t, residual in enumerate((first, second)):
         residuals[:, t, :] = residual
-        for at in range(2):
-            kept[2 * t + at] = residual[:, at * count : (at + 1) * count]
-    given, even = came[member[0]], member[0] < 2
-    tiles = (
-        tile[0],
-        paired[...],
-        jnp.where(even, given, beside[...]),
-        jnp.where(even, beside[...], given),
-    )
-    update = None
-    for at in range(GROUP):
-        term = wide_dot(pieces_of(kept[member[0] ^ at]), tiles[at], NN)
+        rows = tiles[2 * t : 2 * t + 2].reshape(2 * count, -1)
+        term = wide_dot(pieces_of(residual), rows, NN)
         update = term if update is None else update + term
     trained[...] = coefficients[...] - STEP_RATE / math.sqrt(total) * update
 
@@ -332,17 +326,18 @@
         (device, owners, along),
         scalars=2,
     )
+    across, turned, spread_out = lax.optimization_barrier((across, turned, spread_out))
+    gathered = exchange(spread_out, PLANE).reshape(half, features)
     near = near + by(across, 2)
-    near, turned, spread_out = lax.optimization_barrier((near, turned, spread_out))
     came_targets = by(near[:, half:], 1)
-    gathered = exchange(spread_out, PLANE).reshape(half, features)
 
     both_centers = [centers, by(centers, 2)]
     both_coefficients = [turned, by(turned, 2)]
+    pair_coefficients = by(both_coefficients[0], 1)
     all_centers = [both_centers[0], by(both_centers[0], 1), both_centers[1], by(both_centers[1], 1)]
     all_coefficients = [
         both_coefficients[0],
-        by(both_coefficients[0], 1),
+        pair_coefficients,
         both_coefficients[1],
         by(both_coefficients[1], 1),
     ]
@@ -385,7 +380,7 @@
         ),
         (member, whole, by(whole, 1), turned_tile, came, paired, beside, turned),
         scalars=1,
-        scratch=(pltpu.VMEM((GROUP, outs, half), jnp.float32),),
+        scratch=(pltpu.VMEM((GROUP, half, width), narrow),),
     )
     return trained.T, jnp.transpose(residuals, (1, 2, 0))
 

time: 113 us -> 111 us (0.982)
  waiting for transfers between devices: 15 us -> 12.8 us
    all_to_all x1, waiting for transfers between devices: 7.98 us -> 1.64 us  [exchange(): return lax.all_to_all(blocks, axes, 0, 0, tiled=True)]
    ppermute x13, waiting for transfers between devices: 7.01 us -> 11.1 us  [move(): return lax.ppermute(value, ('z', 'core'), pairs)]
  transfers between devices with their start and end apart: 14 -> 14, of which waited for: 6 -> 7; matrix products, arithmetic and copies ran while one was open for 1% -> 1% of each run, Pallas kernels for 3% -> 3%
where the time goes in v9:
time: 111 us
  blocking collectives  68.1 us (61%)
  starting transfers between devices  21.8 us (20%)
  waiting for transfers between devices  12.8 us (12%)
  Pallas kernels  6.1 us (5%)
    all_to_all x5, blocking collectives, exchange(): return lax.all_to_all(blocks, axes, 0, 0, tiled=True)  68.1 us
    ppermute x13, starting transfers between devices, move(): return lax.ppermute(value, ('z', 'core'), pairs)  18.2 us
    ppermute x13, waiting for transfers between devices, move(): return lax.ppermute(value, ('z', 'core'), pairs)  11.1 us
    pallas_call x7, Pallas kernels, call(): pl.pallas_call(kernel, in_specs=[pl.BlockSpec(memory_space=kind) for kind...  6.1 us
    all_to_all x1, starting transfers between devices, exchange(): return lax.all_to_all(blocks, axes, 0, 0, tiled=True)  3.57 us
  transfers between devices with their start and end apart: 14, of which 7 were waited for; matrix products, arithmetic and copies ran while one was open for 1% of the time, Pallas kernels for 3%

profile of v9, /device:TPU:1, one launch (start us, length us, event | category | flops | bytes accessed | tf_op | source)
XLA Modules:
  0.0 110.6 jit_solution(7122853298028671458)
XLA Ops:
  0.6 2.5 %collective-permute-start.3 = (bf16[128,2048]{1,0:T(8,128)(2,1)}, bf16[128,2048]{1,0:T(8,128)(2,1)S(1)}, u32[]{:S(2)}, u32[]{:S(2)}) collective-permute-start(bf16[128,2048]{1,0:T(8,128)(2,1)} %rest_0_), channel_id=1, source_target_pairs={{0,8},{1,9},{8,0},{9,1},{16,24},{17,25},{24,16},{25,17},{32,40},{3... | collective-permute-start | bytes 1572872 | tf_op jit(solution)/shard_map/ppermute | solution.py:284
  3.2 1.0 collective-permute-start.2
  4.1 0.7 shard_map.77
  4.9 0.0 copy-start.1
  4.9 36.7 %conditional.1 = (bf16[8,8,2048]{2,1,0:T(8,128)(2,1)S(1)}) conditional(s32[]{:T(128)} %bitcast.5, (bf16[512,300]{0,1:T(8,128)(2,1)}, s32[1]{0:T(128)}, s32[2]{0:T(128)S(1)}, s32[2,256]{1,0:T(2,128)}, bf16[512,2048]{1,0:T(8,128)(2,1)}) %tuple.25, (bf16[16,1,8,2048]{3,2,1,0:T(8,128)(2,1)S(1)}, bf16[16,1,8,2048]{3,2,1,0:T(8,128)(2,1)S(1)}, ...), branch_computations={%region_0.0_spmd, %region_1.0_spmd} | conditional | flops 524288 | bytes 9961520 | solution.py:322
  4.9 0.1 collective-permute-start.1
  5.0 1.9 %collective-permute-done.1 = bf16[16,1,8,2048]{3,2,1,0:T(8,128)(2,1)S(1)} collective-permute-done((bf16[16,1,8,2048]{3,2,1,0:T(8,128)(2,1)S(1)}, bf16[16,1,8,2048]{3,2,1,0:T(8,128)(2,1)S(1)}, u32[]{:S(2)}, u32[]{:S(2)}) %collective-permute-start.1) | collective-permute-done | bytes 524320 | tf_op jit(solution)/shard_map/cond/branch_1_fun/ppermute | solution.py:284
  6.9 0.1 add.55
  7.1 17.5 %all_to_all.38.scattered = bf16[16,1,8,2048]{3,2,1,0:T(8,128)(2,1)S(1)} all-to-all(bf16[16,1,8,2048]{3,2,1,0:T(8,128)(2,1)S(1)} %add.55), channel_id=1, replica_groups=mesh['y'=4,'z'=8,'x'=4,'core'=2] {'y','x'}, dimensions={0} | all-to-all | bytes 1048576 | tf_op jit(solution)/shard_map/cond/branch_1_fun/all_to_all | solution.py:27
  24.5 0.6 branch_1_fun.1
  25.1 16.5 %all_to_all.39 = bf16[8,8,2048]{2,1,0:T(8,128)(2,1)S(1)} all-to-all(bf16[8,8,2048]{2,1,0:T(8,128)(2,1)S(1)} %branch_1_fun.1), channel_id=1, replica_groups=mesh['y'=4,'z'=8,'x'=4,'core'=2] {'z'}, dimensions={0} | all-to-all | bytes 524288 | tf_op jit(solution)/shard_map/cond/branch_1_fun/all_to_all | solution.py:27
  41.6 1.4 %shard_map.78 = bf16[16,8,2048]{2,1,0:T(8,128)(2,1)} custom-call(s32[1]{0:T(128)} %bitcast.2.device, s32[2]{0:T(128)S(1)} %copy-done.4, bf16[8,8,2048]{2,1,0:T(8,128)(2,1)S(1)} %get-tuple-element.93.along), custom_call_target="tpu_custom_call" | custom-call | tf_op jit(solution)/shard_map/pallas_call | solution.py:254
  43.0 3.4 %collective-permute-start.5 = (f32[300,128]{1,0:T(8,128)S(1)}, f32[300,128]{1,0:T(8,128)S(1)}, u32[]{:S(2)}, u32[]{:S(2)}) collective-permute-start(f32[300,128]{1,0:T(8,128)S(1)} %bitcast.23), channel_id=1, source_target_pairs={{0,1},{1,0},{8,9},{9,8},{16,17},{17,16},{24,25},{25,24},{32,33},{3... | collective-permute-start | bytes 460808 | tf_op jit(solution)/shard_map/ppermute | solution.py:284
  46.4 0.3 collective-permute-start.6
  46.7 3.6 %all-to-all-start.4 = ((bf16[16,8,2048]{2,1,0:T(8,128)(2,1)}), bf16[16,8,2048]{2,1,0:T(8,128)(2,1)S(1)}, u32[]{:S(2)}, u32[]{:S(2)}) async-start(bf16[16,8,2048]{2,1,0:T(8,128)(2,1)} %shard_map.78), calls=%async_computation.4 | async-start | bytes 1048576 | tf_op jit(solution)/shard_map/all_to_all | solution.py:27
  50.3 1.3 %collective-permute-start.8 = (bf16[300,256]{1,0:T(8,128)(2,1)S(1)}, bf16[300,256]{1,0:T(8,128)(2,1)S(1)}, u32[]{:S(2)}, u32[]{:S(2)}) collective-permute-start(bf16[300,256]{1,0:T(8,128)(2,1)S(1)} %get-tuple-element.69), channel_id=1, source_target_pairs={{0,8},{1,9},{8,0},{9,1},{16,24},{17,25},{24,16},{25,17},{32,40},{3... | collective-permute-start | bytes 460808 | tf_op jit(solution)/shard_map/ppermute | solution.py:284
  51.6 0.2 multiply_reduce_fusion.3
  51.8 3.9 %collective-permute-done.8 = bf16[300,256]{1,0:T(8,128)(2,1)S(1)} collective-permute-done((bf16[300,256]{1,0:T(8,128)(2,1)S(1)}, bf16[300,256]{1,0:T(8,128)(2,1)S(1)}, u32[]{:S(2)}, u32[]{:S(2)}) %collective-permute-start.8) | collective-permute-done | bytes 153632 | tf_op jit(solution)/shard_map/ppermute | solution.py:284
  55.7 0.0 copy-start.2
  55.8 1.2 %collective-permute-start.9 = (bf16[300,128]{1,0:T(8,128)(2,1)S(1)}, bf16[300,128]{1,0:T(8,128)(2,1)S(1)}, u32[]{:S(2)}, u32[]{:S(2)}) collective-permute-start(bf16[300,128]{1,0:T(8,128)(2,1)S(1)} %slice.12), channel_id=1, source_target_pairs={{0,1},{1,0},{8,9},{9,8},{16,17},{17,16},{24,25},{25,24},{32,33},{3... | collective-permute-start | bytes 230408 | tf_op jit(solution)/shard_map/ppermute | solution.py:284
  57.0 0.0 collective-permute-done.6.rest_2_
  57.0 0.6 collective-permute-start.7
  57.5 0.0 collective-permute-done.3.rest_2_
  57.5 0.1 collective-permute-start.4
  57.6 0.2 multiply_reduce_fusion.1
  57.8 0.0 collective-permute-done.2.rest_1_
  57.8 0.2 multiply_reduce_fusion.2
  58.0 1.4 %collective-permute-done.4.rest_3_ = bf16[128,2048]{1,0:T(8,128)(2,1)S(1)} collective-permute-done((bf16[128,2048]{1,0:T(8,128)(2,1)S(1)}, bf16[128,2048]{1,0:T(8,128)(2,1)S(1)}, u32[]{:S(2)}, u32[]{:S(2)}) %collective-permute-start.4) | collective-permute-done | bytes 524320 | tf_op jit(solution)/shard_map/ppermute | solution.py:284
  59.5 0.2 multiply_reduce_fusion
  59.6 0.0 collective-permute-done.5.rest_1_
  59.7 0.0 collective-permute-done.9.rest_5_
  59.7 0.0 collective-permute-done.7.rest_3_
  59.7 1.6 %all-to-all-done.4 = bf16[16,8,2048]{2,1,0:T(8,128)(2,1)S(1)} async-done(((bf16[16,8,2048]{2,1,0:T(8,128)(2,1)}), bf16[16,8,2048]{2,1,0:T(8,128)(2,1)S(1)}, u32[]{:S(2)}, u32[]{:S(2)}) %all-to-all-start.4) | async-done | bytes 524320 | tf_op jit(solution)/shard_map/all_to_all | solution.py:27
  61.3 0.8 shard_map.79
  62.1 2.6 %collective-permute-start.10 = (bf16[4,128,128]{2,1,0:T(8,128)(2,1)S(1)}, bf16[4,128,128]{2,1,0:T(8,128)(2,1)S(1)}, u32[]{:S(2)}, u32[]{:S(2)}) collective-permute-start(bf16[4,128,128]{2,1,0:T(8,128)(2,1)S(1)} %get-tuple-element.86.tile), channel_id=1, source_target_pairs={{0,9},{1,8},{8,0},{9,1},{16,25},{17,24},{24,16},{25,17},{32,41},{3... | collective-permute-start | bytes 393224 | tf_op jit(solution)/shard_map/ppermute | solution.py:284
  64.7 0.0 collective-permute-start.11
  64.7 0.7 collective-permute-start.12
  65.3 0.7 shard_map.80.partial
  66.0 1.6 %collective-permute-done.10.came = bf16[4,128,128]{2,1,0:T(8,128)(2,1)S(1)} collective-permute-done((bf16[4,128,128]{2,1,0:T(8,128)(2,1)S(1)}, bf16[4,128,128]{2,1,0:T(8,128)(2,1)S(1)}, u32[]{:S(2)}, u32[]{:S(2)}) %collective-permute-start.10) | collective-permute-done | bytes 131104 | tf_op jit(solution)/shard_map/ppermute | solution.py:284
  67.6 0.2 shard_map.81
  67.8 0.8 collective-permute-done.12.beside
  68.6 12.1 %all_to_all.40 = f32[16,32,128]{2,1,0:T(8,128)S(1)} all-to-all(f32[16,32,128]{2,1,0:T(8,128)S(1)} %bitcast.22), channel_id=1, replica_groups=mesh['y'=4,'z'=8,'x'=4,'core'=2] {'y','x'}, dimensions={0} | all-to-all | bytes 524288 | tf_op jit(solution)/shard_map/all_to_all | solution.py:27
  80.7 10.4 %all_to_all.41 = f32[8,32,128]{2,1,0:T(8,128)S(1)} all-to-all(f32[8,32,128]{2,1,0:T(8,128)S(1)} %broadcast_in_dim.4), channel_id=1, replica_groups=mesh['y'=4,'z'=8,'x'=4,'core'=2] {'z'}, dimensions={0} | all-to-all | bytes 262144 | tf_op jit(solution)/shard_map/all_to_all | solution.py:27
  91.1 0.1 broadcast_in_dim.5
  91.2 11.6 %all_to_all.42.mine = f32[16,2,32,128]{3,2,1,0:T(8,128)S(1)} all-to-all(f32[16,2,32,128]{3,2,1,0:T(8,128)S(1)} %broadcast_in_dim.5), channel_id=1, replica_groups=mesh['y'=4,'z'=8,'x'=4,'core'=2] {'y','x'}, dimensions={0} | all-to-all | bytes 1048576 | tf_op jit(solution)/shard_map/all_to_all | solution.py:27
  102.8 4.5 %collective-permute-start.13 = (f32[16,2,32,128]{3,2,1,0:T(8,128)S(1)}, f32[16,2,32,128]{3,2,1,0:T(8,128)S(1)}, u32[]{:S(2)}, u32[]{:S(2)}) collective-permute-start(f32[16,2,32,128]{3,2,1,0:T(8,128)S(1)} %all_to_all.42.mine), channel_id=1, source_target_pairs={{0,1},{1,0},{8,9},{9,8},{16,17},{17,16},{24,25},{25,24},{32,33},{3... | collective-permute-start | bytes 1572872 | tf_op jit(solution)/shard_map/ppermute | solution.py:284
  107.3 1.5 %collective-permute-done.13.other = f32[16,2,32,128]{3,2,1,0:T(8,128)S(1)} collective-permute-done((f32[16,2,32,128]{3,2,1,0:T(8,128)S(1)}, f32[16,2,32,128]{3,2,1,0:T(8,128)S(1)}, u32[]{:S(2)}, u32[]{:S(2)}) %collective-permute-start.13) | collective-permute-done | bytes 524320 | tf_op jit(solution)/shard_map/ppermute | solution.py:284
  108.8 1.8 %shard_map.82 = (f32[300,128]{1,0:T(8,128)}, f32[300,2,256]{2,1,0:T(2,128)}) custom-call(s32[1]{0:T(128)} %bitcast.1.member, f32[16,2,32,128]{3,2,1,0:T(8,128)S(1)} %all_to_all.42.mine, f32[16,2,32,128]{3,2,1,0:T(8,128)S(1)} %collective-permute-done.13.other, bf16[4,128,128]{2,1,0:T(8,128)(2,1)S(1)} %get-tuple-element.79.turned.tile, ...), custom_call_target="tpu_custom_call" | custom-call | tf_op jit(solution)/shard_map/pallas_call | solution.py:254
  (20 shorter events, 0.2 us)
Async XLA Ops:
  0.6 4.3 %copy-start.4 = (s32[2]{0:T(128)S(1)}, s32[2]{0:T(128)}, u32[]{:S(2)}) copy-start(s32[2]{0:T(128)} %owners.3) | copy-start | bytes 28
  0.6 56.9 %collective-permute-start.3 = (bf16[128,2048]{1,0:T(8,128)(2,1)}, bf16[128,2048]{1,0:T(8,128)(2,1)S(1)}, u32[]{:S(2)}, u32[]{:S(2)}) collective-permute-start(bf16[128,2048]{1,0:T(8,128)(2,1)} %rest_0_), channel_id=1, source_target_pairs={{0,8},{1,9},{8,0},{9,1},{16,24},{17,25},{24,16},{25,17},{32,40},{3... | collective-permute-start | bytes 1572872 | tf_op jit(solution)/shard_map/ppermute | solution.py:284
  3.2 54.6 %collective-permute-start.2 = (bf16[128,2048]{1,0:T(8,128)(2,1)}, bf16[128,2048]{1,0:T(8,128)(2,1)S(1)}, u32[]{:S(2)}, u32[]{:S(2)}) collective-permute-start(bf16[128,2048]{1,0:T(8,128)(2,1)} %rest_0_), channel_id=1, source_target_pairs={{0,1},{1,0},{8,9},{9,8},{16,17},{17,16},{24,25},{25,24},{32,33},{3... | collective-permute-start | bytes 1572872 | tf_op jit(solution)/shard_map/ppermute | solution.py:284
  4.9 38.1 %copy-start.1 = (f32[128,300]{0,1:T(8,128)S(1)}, f32[128,300]{0,1:T(8,128)}, u32[]{:S(2)}) copy-start(f32[128,300]{0,1:T(8,128)} %param.11) | copy-start | bytes 460804
  4.9 2.0 %collective-permute-start.1 = (bf16[16,1,8,2048]{3,2,1,0:T(8,128)(2,1)S(1)}, bf16[16,1,8,2048]{3,2,1,0:T(8,128)(2,1)S(1)}, u32[]{:S(2)}, u32[]{:S(2)}) collective-permute-start(bf16[16,1,8,2048]{3,2,1,0:T(8,128)(2,1)S(1)} %get-tuple-element.28), channel_id=1, source_target_pairs={{0,1},{1,0},{8,9},{9,8},{16,17},{17,16},{24,25},{25,24},{32,33},{3... | collective-permute-start | bytes 1572872 | tf_op jit(solution)/shard_map/cond/branch_1_fun/ppermute | solution.py:284
  41.6 10.0 %copy-start = (bf16[128,2048]{1,0:T(8,128)(2,1)S(1)}, bf16[128,2048]{1,0:T(8,128)(2,1)}, u32[]{:S(2)}) copy-start(bf16[128,2048]{1,0:T(8,128)(2,1)} %rest_0_) | copy-start | bytes 1572868
  43.0 16.7 %collective-permute-start.5 = (f32[300,128]{1,0:T(8,128)S(1)}, f32[300,128]{1,0:T(8,128)S(1)}, u32[]{:S(2)}, u32[]{:S(2)}) collective-permute-start(f32[300,128]{1,0:T(8,128)S(1)} %bitcast.23), channel_id=1, source_target_pairs={{0,1},{1,0},{8,9},{9,8},{16,17},{17,16},{24,25},{25,24},{32,33},{3... | collective-permute-start | bytes 460808 | tf_op jit(solution)/shard_map/ppermute | solution.py:284
  46.4 10.6 %collective-permute-start.6 = (f32[300,128]{1,0:T(8,128)S(1)}, f32[300,128]{1,0:T(8,128)S(1)}, u32[]{:S(2)}, u32[]{:S(2)}) collective-permute-start(f32[300,128]{1,0:T(8,128)S(1)} %bitcast.24), channel_id=1, source_target_pairs={{0,8},{1,9},{8,0},{9,1},{16,24},{17,25},{24,16},{25,17},{32,40},{3... | collective-permute-start | bytes 460808 | tf_op jit(solution)/shard_map/ppermute | solution.py:284
  46.7 14.6 %all-to-all-start.4 = ((bf16[16,8,2048]{2,1,0:T(8,128)(2,1)}), bf16[16,8,2048]{2,1,0:T(8,128)(2,1)S(1)}, u32[]{:S(2)}, u32[]{:S(2)}) async-start(bf16[16,8,2048]{2,1,0:T(8,128)(2,1)} %shard_map.78), calls=%async_computation.4 | async-start | bytes 1048576 | tf_op jit(solution)/shard_map/all_to_all | solution.py:27
  50.3 5.4 %collective-permute-start.8 = (bf16[300,256]{1,0:T(8,128)(2,1)S(1)}, bf16[300,256]{1,0:T(8,128)(2,1)S(1)}, u32[]{:S(2)}, u32[]{:S(2)}) collective-permute-start(bf16[300,256]{1,0:T(8,128)(2,1)S(1)} %get-tuple-element.69), channel_id=1, source_target_pairs={{0,8},{1,9},{8,0},{9,1},{16,24},{17,25},{24,16},{25,17},{32,40},{3... | collective-permute-start | bytes 460808 | tf_op jit(solution)/shard_map/ppermute | solution.py:284
  55.7 1.3 %copy-start.2 = (bf16[300,256]{1,0:T(8,128)(2,1)}, bf16[300,256]{1,0:T(8,128)(2,1)S(1)}, u32[]{:S(2)}) copy-start(bf16[300,256]{1,0:T(8,128)(2,1)S(1)} %add.69) | copy-start | bytes 460804
  55.8 3.9 %collective-permute-start.9 = (bf16[300,128]{1,0:T(8,128)(2,1)S(1)}, bf16[300,128]{1,0:T(8,128)(2,1)S(1)}, u32[]{:S(2)}, u32[]{:S(2)}) collective-permute-start(bf16[300,128]{1,0:T(8,128)(2,1)S(1)} %slice.12), channel_id=1, source_target_pairs={{0,1},{1,0},{8,9},{9,8},{16,17},{17,16},{24,25},{25,24},{32,33},{3... | collective-permute-start | bytes 230408 | tf_op jit(solution)/shard_map/ppermute | solution.py:284
  57.0 2.7 %collective-permute-start.7 = (f32[300,128]{1,0:T(8,128)S(1)}, f32[300,128]{1,0:T(8,128)S(1)}, u32[]{:S(2)}, u32[]{:S(2)}) collective-permute-start(f32[300,128]{1,0:T(8,128)S(1)} %collective-permute-done.6.rest_2_), channel_id=1, source_target_pairs={{0,1},{1,0},{8,9},{9,8},{16,17},{17,16},{24,25},{25,24},{32,33},{3... | collective-permute-start | bytes 460808 | tf_op jit(solution)/shard_map/ppermute | solution.py:284
  57.5 1.9 %collective-permute-start.4 = (bf16[128,2048]{1,0:T(8,128)(2,1)S(1)}, bf16[128,2048]{1,0:T(8,128)(2,1)S(1)}, u32[]{:S(2)}, u32[]{:S(2)}) collective-permute-start(bf16[128,2048]{1,0:T(8,128)(2,1)S(1)} %collective-permute-done.3.rest_2_), channel_id=1, source_target_pairs={{0,1},{1,0},{8,9},{9,8},{16,17},{17,16},{24,25},{25,24},{32,33},{3... | collective-permute-start | bytes 1572872 | tf_op jit(solution)/shard_map/ppermute | solution.py:284
  61.3 4.0 %copy-start.3 = (bf16[300,256]{1,0:T(8,128)(2,1)S(1)}, bf16[300,256]{1,0:T(8,128)(2,1)}, u32[]{:S(2)}) copy-start(bf16[300,256]{1,0:T(8,128)(2,1)} %copy-done.2) | copy-start | bytes 460804
  62.1 5.5 %collective-permute-start.10 = (bf16[4,128,128]{2,1,0:T(8,128)(2,1)S(1)}, bf16[4,128,128]{2,1,0:T(8,128)(2,1)S(1)}, u32[]{:S(2)}, u32[]{:S(2)}) collective-permute-start(bf16[4,128,128]{2,1,0:T(8,128)(2,1)S(1)} %get-tuple-element.86.tile), channel_id=1, source_target_pairs={{0,9},{1,8},{8,0},{9,1},{16,25},{17,24},{24,16},{25,17},{32,41},{3... | collective-permute-start | bytes 393224 | tf_op jit(solution)/shard_map/ppermute | solution.py:284
  64.7 3.1 %collective-permute-start.11 = (bf16[128,128]{1,0:T(8,128)(2,1)S(1)}, bf16[128,128]{1,0:T(8,128)(2,1)S(1)}, u32[]{:S(2)}, u32[]{:S(2)}) collective-permute-start(bf16[128,128]{1,0:T(8,128)(2,1)S(1)} %slice_bitcast_fusion), channel_id=1, source_target_pairs={{0,1},{1,0},{8,9},{9,8},{16,17},{17,16},{24,25},{25,24},{32,33},{3... | collective-permute-start | bytes 98312 | tf_op jit(solution)/shard_map/ppermute | solution.py:284
  64.7 3.9 %collective-permute-start.12 = (bf16[128,128]{1,0:T(8,128)(2,1)S(1)}, bf16[128,128]{1,0:T(8,128)(2,1)S(1)}, u32[]{:S(2)}, u32[]{:S(2)}) collective-permute-start(bf16[128,128]{1,0:T(8,128)(2,1)S(1)} %get-tuple-element.87), channel_id=1, source_target_pairs={{0,8},{1,9},{8,1},{9,0},{16,24},{17,25},{24,17},{25,16},{32,40},{3... | collective-permute-start | bytes 98312 | tf_op jit(solution)/shard_map/ppermute | solution.py:284
  102.8 6.0 %collective-permute-start.13 = (f32[16,2,32,128]{3,2,1,0:T(8,128)S(1)}, f32[16,2,32,128]{3,2,1,0:T(8,128)S(1)}, u32[]{:S(2)}, u32[]{:S(2)}) collective-permute-start(f32[16,2,32,128]{3,2,1,0:T(8,128)S(1)} %all_to_all.42.mine), channel_id=1, source_target_pairs={{0,1},{1,0},{8,9},{9,8},{16,17},{17,16},{24,25},{25,24},{32,33},{3... | collective-permute-start | bytes 1572872 | tf_op jit(solution)/shard_map/ppermute | solution.py:284

commit v10 on v7

--- a/solution.py
+++ b/solution.py
@@ -76,11 +76,11 @@
         same_chip = owners[0] >> 1 == owners[1] >> 1
         same_z = place(owners[0], sizes)[1] == place(owners[1], sizes)[1]
         flag[0][0] = jnp.where(same_chip, 0, jnp.where(same_z, 1, 2))
-
-    @pl.when(jnp.logical_not(involved))
-    def _():
-        kept[...] = jnp.zeros_like(kept)
-        sent[...] = jnp.zeros_like(sent)
+        for t in range(ITERS):
+            root_y, root_z, root_x, _ = place(owners[t], sizes)
+            flag[1][t] = root_y * sizes[2] + root_x
+            flag[1][ITERS + t] = root_z
+        flag[1][2 * ITERS] = place(here, sizes)[1]
 
     @pl.when(involved)
     def _():
@@ -130,27 +130,28 @@
             ).astype(out.dtype)
 
 
-def pick_kernel(device, owners, scattered, piece, *, sizes):
-    _, z, _, _ = place(device[0], sizes)
+def pick_kernel(spots, scattered, piece):
     slots = scattered.shape[1]
     for t in range(ITERS):
-        root_y, root_z, root_x, _ = place(owners[t], sizes)
-        block = scattered[root_y * sizes[2] + root_x, t if slots > 1 else 0]
-        piece[t] = jnp.where(root_z == z, block, jnp.zeros_like(block))
-
-
-def along_kernel(device, owners, scattered, out, *, sizes):
-    _, z, _, _ = place(device[0], sizes)
-    t = jnp.where(place(owners[1], sizes)[1] == z, 1, 0)
-    root_y, _, root_x, _ = place(owners[t], sizes)
-    out[...] = jnp.broadcast_to(scattered[root_y * sizes[2] + root_x, 0][None], out.shape)
-
-
-def spread_kernel(owners, along, out, *, sizes):
-    plane, _, each, features = out.shape
-    for t in range(ITERS):
-        block = along[place(owners[t], sizes)[1]]
-        out[:, t] = jnp.broadcast_to(block[None], (plane, each, features))
+        block = scattered[spots[t], t if slots > 1 else 0]
+        piece[t] = jnp.where(spots[ITERS + t] == spots[2 * ITERS], block, jnp.zeros_like(block))
+
+
+def along_kernel(spots, scattered, out):
+    at = jnp.where(spots[ITERS + 1] == spots[2 * ITERS], spots[1], spots[0])
+    out[...] = jnp.broadcast_to(scattered[at, 0][None], out.shape)
+
+
+def spread_kernel(spots, along, out, sent):
+    copies_of = [
+        pltpu.make_async_copy(along.at[spots[ITERS + t]], out.at[at, t], sent.at[at * ITERS + t])
+        for at in range(out.shape[0])
+        for t in range(ITERS)
+    ]
+    for copy in copies_of:
+        copy.start()
+    for copy in copies_of:
+        copy.wait()
 
 
 def spread_steps_kernel(piece, arrived, out):
@@ -192,11 +193,10 @@
             )
 
 
-def partial_kernel(core, tile, came, own, other, kept, arrived, lines, *, root_scale):
+def partial_kernel(tile, own, other, kept, arrived, lines, *, root_scale):
     outs, width = own.shape
     count = tile.shape[1]
     step = aligned(outs)
-    lines[...] = jnp.zeros_like(lines)
     held = kept[...].astype(jnp.float32) + arrived[...].astype(jnp.float32)
     own_pieces, other_pieces = pieces_of(own[...]), pieces_of(other[...])
     for t in range(ITERS):
@@ -206,16 +206,24 @@
         lines[t * step : t * step + outs, :] = (
             total / root_scale - held[:, t * count : (t + 1) * count]
         )
-    mine = tile[0]
+        lines[t * step + outs : (t + 1) * step, :] = jnp.zeros((step - outs, count), jnp.float32)
+
+
+def join_kernel(core, partial, tile, came, lines):
+    height, count = partial.shape
+    width = tile.shape[2] // 2
+    lines[:height, :] = partial[...]
+    lines[height + 2 * count :, :] = jnp.zeros(
+        (lines.shape[0] - height - 2 * count, count), jnp.float32
+    )
     theirs = jnp.concatenate([came[0, :, width:], came[0, :, :width]], axis=1)
-    later = tile[1]
     gram = [
-        lax.dot_general(value, later, NT, preferred_element_type=jnp.float32)
-        for value in (mine, theirs)
+        lax.dot_general(value, tile[1], NT, preferred_element_type=jnp.float32)
+        for value in (tile[0], theirs)
     ]
     is_first = core[0] == 0
-    lines[2 * step : 2 * step + count, :] = jnp.where(is_first, gram[0], gram[1])
-    lines[2 * step + count : 2 * step + 2 * count, :] = jnp.where(is_first, gram[1], gram[0])
+    lines[height : height + count, :] = jnp.where(is_first, gram[0], gram[1])
+    lines[height + count : height + 2 * count, :] = jnp.where(is_first, gram[1], gram[0])
 
 
 def finish_kernel(core, mine, other, tile, came, coefficients, trained, residuals, *, total):
@@ -247,15 +255,17 @@
     trained[...] = coefficients[...] - STEP_RATE / math.sqrt(total) * update
 
 
-def call(kernel, out_shape, operands, scalars=0, out_kinds=None, in_place=(), scratch=()):
+def call(kernel, out_shape, operands, scalars=0, out_kinds=None, in_place=(), in_smem=(), scratch=()):
     outs = out_shape if isinstance(out_shape, tuple) else (out_shape,)
     out_kinds = out_kinds or [pltpu.VMEM] * len(outs)
     specs = tuple(pl.BlockSpec(memory_space=kind) for kind in out_kinds)
     kinds = [pltpu.SMEM] * scalars + [pltpu.VMEM] * (len(operands) - scalars)
     kinds = [pltpu.HBM if at in in_place else kind for at, kind in enumerate(kinds)]
     operands = [
-        value if kind is pltpu.SMEM else pltpu.with_memory_space_constraint(value, kind)
-        for value, kind in zip(operands, kinds)
+        value
+        if kind is pltpu.SMEM and at not in in_smem
+        else pltpu.with_memory_space_constraint(value, kind)
+        for at, (value, kind) in enumerate(zip(operands, kinds))
     ]
     return pl.pallas_call(
         kernel,
@@ -284,7 +294,7 @@
 
     def rows_for(slots):
         blocks = pltpu.VMEM((plane, slots, each, features), narrow)
-        flag = (pltpu.SMEM((1,), jnp.int32),) if slots == 1 else ()
+        flag = (pltpu.SMEM((1,), jnp.int32), pltpu.SMEM((8,), jnp.int32)) if slots == 1 else ()
         return call(
             functools.partial(rows_kernel, sizes=sizes),
             (blocks, blocks) + flag,
@@ -301,10 +311,11 @@
 
     def in_steps(kept, sent):
         piece = call(
-            functools.partial(pick_kernel, sizes=sizes),
+            pick_kernel,
             block,
-            (device, owners, exchange(kept + swap(sent), PLANE)),
-            scalars=2,
+            (spots, exchange(kept + swap(sent), PLANE)),
+            scalars=1,
+            in_smem=(0,),
         )
         arrived = None
         for mask in Z_MASKS:
@@ -314,19 +325,23 @@
 
     def at_once(kept, sent):
         along = call(
-            functools.partial(along_kernel, sizes=sizes),
+            along_kernel,
             pltpu.VMEM((sizes[1], each, features), narrow),
-            (device, owners, exchange(kept + swap(sent), PLANE)),
-            scalars=2,
+            (spots, exchange(kept + swap(sent), PLANE)),
+            scalars=1,
+            in_smem=(0,),
         )
         return call(
-            functools.partial(spread_kernel, sizes=sizes),
+            spread_kernel,
             whole_block,
-            (owners, exchange(along, "z")),
+            (spots, exchange(along, "z")),
             scalars=1,
-        )
-
-    kept, sent, apart = rows_for(1)
+            in_smem=(0,),
+            out_kinds=[pltpu.HBM],
+            scratch=(pltpu.SemaphoreType.DMA((plane * ITERS,)),),
+        )
+
+    kept, sent, apart, spots = rows_for(1)
     spread_out = lax.switch(
         apart[0],
         (lambda: in_steps(*rows_for(2)), lambda: in_steps(kept, sent), lambda: at_once(kept, sent)),
@@ -354,10 +369,15 @@
     )
     came = swap(tile)
     height = -(-(2 * aligned(outs) + batch) // (8 * plane)) * 8
+    partial = call(
+        functools.partial(partial_kernel, root_scale=math.sqrt(total)),
+        pltpu.VMEM((2 * aligned(outs), half), jnp.float32),
+        (tile, turned, turned_other, kept_targets, came_targets),
+    )
     lines = call(
-        functools.partial(partial_kernel, root_scale=math.sqrt(total)),
+        join_kernel,
         pltpu.VMEM((plane * height, half), jnp.float32),
-        (core, tile, came, turned, turned_other, kept_targets, came_targets),
+        (core, partial, tile, came),
         scalars=1,
     )
     own = exchange(lines.reshape(plane, height, half), PLANE).sum(axis=0)

time: 111 us -> 111 us (level)
    pallas_call x7 -> x8, Pallas kernels: 7.24 us -> 6.4 us  [call(): pl.pallas_call(kernel, in_specs=[pl.BlockSpec(memory_space=kind) for kind...]
where the time goes in v10:
time: 111 us
  blocking collectives  70.2 us (63%)
  starting transfers between devices  19.8 us (18%)
  waiting for transfers between devices  12.7 us (11%)
  Pallas kernels  6.4 us (6%)
    all_to_all x5, blocking collectives, exchange(): return lax.all_to_all(blocks, axes, 0, 0, tiled=True)  70.2 us
    ppermute x6, starting transfers between devices, swap(): return lax.ppermute(value, 'core', PAIR)  15.2 us
    all_to_all x1, waiting for transfers between devices, exchange(): return lax.all_to_all(blocks, axes, 0, 0, tiled=True)  9.36 us
    pallas_call x8, Pallas kernels, call(): pl.pallas_call(kernel, in_specs=[pl.BlockSpec(memory_space=kind) for kind...  6.4 us
    all_to_all x1, starting transfers between devices, exchange(): return lax.all_to_all(blocks, axes, 0, 0, tiled=True)  4.63 us
    ppermute x6, waiting for transfers between devices, swap(): return lax.ppermute(value, 'core', PAIR)  3.31 us
  transfers between devices with their start and end apart: 7, of which 4 were waited for; matrix products, arithmetic and copies ran while one was open for 0% of the time, Pallas kernels for 2%

profile of v10, /device:TPU:1, one launch (start us, length us, event | category | flops | bytes accessed | tf_op | source)
XLA Modules:
  0.0 110.6 jit_solution(9784474631784133782)
XLA Ops:
  0.6 0.0 copy-start.4
  0.6 0.0 copy-start.3
  0.7 0.8 shard_map.77
  1.4 0.0 copy-done.4
  1.4 0.0 copy-done.3
  1.5 40.0 %conditional.1 = (bf16[16,2,8,2048]{3,2,1,0:T(8,128)(2,1)}) conditional(s32[]{:T(128)} %bitcast.2, (s32[1]{0:T(128)}, s32[2]{0:T(128)S(1)}, s32[2,256]{1,0:T(2,128)S(1)}, bf16[512,2048]{1,0:T(8,128)(2,1)}, s32[8]{0:T(128)S(4)}) %tuple.24, (bf16[16,1,8,2048]{3,2,1,0:T(8,128)(2,1)S(1)}, bf16[16,1,8,2048]{3,2,1,0:T(8,128)(2,1)S(1)}, ...), branch_computations={%region_0.0_spmd, %region_1.0_spmd, %region_2.0_spmd} | conditional | flops 589824 | bytes 10617000 | solution.py:345
  1.5 3.3 %collective-permute-start.8 = (bf16[16,1,8,2048]{3,2,1,0:T(8,128)(2,1)S(1)}, bf16[16,1,8,2048]{3,2,1,0:T(8,128)(2,1)S(1)}, u32[]{:S(2)}, u32[]{:S(2)}) collective-permute-start(bf16[16,1,8,2048]{3,2,1,0:T(8,128)(2,1)S(1)} %get-tuple-element.38), channel_id=1, source_target_pairs={{0,1},{1,0},{2,3},{3,2},{4,5},{5,4},{6,7},{7,6},{8,9},{9,8},{10,11... | collective-permute-start | bytes 1572872 | tf_op jit(solution)/shard_map/cond/branch_2_fun/ppermute | solution.py:27
  4.8 1.5 %collective-permute-done.8 = bf16[16,1,8,2048]{3,2,1,0:T(8,128)(2,1)S(1)} collective-permute-done((bf16[16,1,8,2048]{3,2,1,0:T(8,128)(2,1)S(1)}, bf16[16,1,8,2048]{3,2,1,0:T(8,128)(2,1)S(1)}, u32[]{:S(2)}, u32[]{:S(2)}) %collective-permute-start.8) | collective-permute-done | bytes 524320 | tf_op jit(solution)/shard_map/cond/branch_2_fun/ppermute | solution.py:27
  6.3 0.1 add.46
  6.4 15.6 %all_to_all.38.scattered = bf16[16,1,8,2048]{3,2,1,0:T(8,128)(2,1)S(1)} all-to-all(bf16[16,1,8,2048]{3,2,1,0:T(8,128)(2,1)S(1)} %add.46), channel_id=1, replica_groups=mesh['y'=4,'z'=8,'x'=4,'core'=2] {'y','x'}, dimensions={0} | all-to-all | bytes 1048576 | tf_op jit(solution)/shard_map/cond/branch_2_fun/all_to_all | solution.py:31
  22.0 18.1 %all_to_all.39.along = bf16[8,8,2048]{2,1,0:T(8,128)(2,1)S(1)} all-to-all(bf16[8,8,2048]{2,1,0:T(8,128)(2,1)S(1)} %branch_2_fun.2), channel_id=1, replica_groups=mesh['y'=4,'z'=8,'x'=4,'core'=2] {'z'}, dimensions={0} | all-to-all | bytes 524288 | tf_op jit(solution)/shard_map/cond/branch_2_fun/all_to_all | solution.py:31
  40.2 1.3 %branch_2_fun.3 = bf16[16,2,8,2048]{3,2,1,0:T(8,128)(2,1)} custom-call(s32[8]{0:T(128)S(4)} %get-tuple-element.36.spots, bf16[8,8,2048]{2,1,0:T(8,128)(2,1)S(1)} %all_to_all.39.along), custom_call_target="tpu_custom_call" | custom-call | tf_op jit(solution)/shard_map/cond/branch_2_fun/pallas_call | solution.py:270
  41.4 0.0 copy-start
  41.5 0.0 copy-start.1
  41.5 0.0 copy-start.2
  41.5 4.6 %all-to-all-start.4 = ((bf16[16,2,8,2048]{3,2,1,0:T(8,128)(2,1)}), bf16[16,2,8,2048]{3,2,1,0:T(8,128)(2,1)S(1)}, u32[]{:S(2)}, u32[]{:S(2)}) async-start(bf16[16,2,8,2048]{3,2,1,0:T(8,128)(2,1)} %get-tuple-element.57), calls=%async_computation.4 | async-start | bytes 2097152 | tf_op jit(solution)/shard_map/all_to_all | solution.py:31
  46.1 0.0 copy-done
  46.1 3.0 %collective-permute-start.9 = (bf16[128,2048]{1,0:T(8,128)(2,1)S(1)}, bf16[128,2048]{1,0:T(8,128)(2,1)S(1)}, u32[]{:S(2)}, u32[]{:S(2)}) collective-permute-start(bf16[128,2048]{1,0:T(8,128)(2,1)S(1)} %copy-done), channel_id=1, source_target_pairs={{0,1},{1,0},{2,3},{3,2},{4,5},{5,4},{6,7},{7,6},{8,9},{9,8},{10,11... | collective-permute-start | bytes 1572872 | tf_op jit(solution)/shard_map/ppermute | solution.py:27
  49.1 0.0 copy-done.1
  49.1 0.1 collective-permute-start.10
  49.2 0.0 copy-done.2
  49.2 1.0 shard_map.79
  50.3 0.7 collective-permute-start.11
  50.9 0.2 multiply_reduce_fusion.1
  51.1 0.0 collective-permute-done.9.other
  51.1 0.2 multiply_reduce_fusion
  51.3 9.4 %all-to-all-done.4 = bf16[16,2,8,2048]{3,2,1,0:T(8,128)(2,1)S(1)} async-done(((bf16[16,2,8,2048]{3,2,1,0:T(8,128)(2,1)}), bf16[16,2,8,2048]{3,2,1,0:T(8,128)(2,1)S(1)}, u32[]{:S(2)}, u32[]{:S(2)}) %all-to-all-start.4) | async-done | bytes 1048608 | tf_op jit(solution)/shard_map/all_to_all | solution.py:31
  60.7 0.7 shard_map.78.tile
  61.4 4.1 %collective-permute-start.12 = (bf16[2,128,256]{2,1,0:T(8,128)(2,1)S(1)}, bf16[2,128,256]{2,1,0:T(8,128)(2,1)S(1)}, u32[]{:S(2)}, u32[]{:S(2)}) collective-permute-start(bf16[2,128,256]{2,1,0:T(8,128)(2,1)S(1)} %shard_map.78.tile), channel_id=1, source_target_pairs={{0,1},{1,0},{2,3},{3,2},{4,5},{5,4},{6,7},{7,6},{8,9},{9,8},{10,11... | collective-permute-start | bytes 393224 | tf_op jit(solution)/shard_map/ppermute | solution.py:27
  65.5 0.0 collective-permute-done.10.other
  65.5 0.0 collective-permute-done.11.arrived
  65.5 0.7 shard_map.80.partial
  66.1 0.3 collective-permute-done.12.came
  66.5 0.2 shard_map.81
  66.7 12.7 %all_to_all.40 = f32[16,56,128]{2,1,0:T(8,128)S(1)} all-to-all(f32[16,56,128]{2,1,0:T(8,128)S(1)} %bitcast.15), channel_id=1, replica_groups=mesh['y'=4,'z'=8,'x'=4,'core'=2] {'y','x'}, dimensions={0} | all-to-all | bytes 917504 | tf_op jit(solution)/shard_map/all_to_all | solution.py:31
  79.4 11.6 %all_to_all.41 = f32[8,56,128]{2,1,0:T(8,128)S(1)} all-to-all(f32[8,56,128]{2,1,0:T(8,128)S(1)} %broadcast_in_dim.4), channel_id=1, replica_groups=mesh['y'=4,'z'=8,'x'=4,'core'=2] {'z'}, dimensions={0} | all-to-all | bytes 458752 | tf_op jit(solution)/shard_map/all_to_all | solution.py:31
  91.0 12.3 %all_to_all.42 = f32[16,56,128]{2,1,0:T(8,128)S(1)} all-to-all(f32[16,56,128]{2,1,0:T(8,128)S(1)} %broadcast_in_dim.5), channel_id=1, replica_groups=mesh['y'=4,'z'=8,'x'=4,'core'=2] {'y','x'}, dimensions={0} | all-to-all | bytes 917504 | tf_op jit(solution)/shard_map/all_to_all | solution.py:31
  103.3 4.1 %collective-permute-start.13 = (f32[896,128]{1,0:T(8,128)S(1)}, f32[896,128]{1,0:T(8,128)S(1)}, u32[]{:S(2)}, u32[]{:S(2)}) collective-permute-start(f32[896,128]{1,0:T(8,128)S(1)} %bitcast.16), channel_id=1, source_target_pairs={{0,1},{1,0},{2,3},{3,2},{4,5},{5,4},{6,7},{7,6},{8,9},{9,8},{10,11... | collective-permute-start | bytes 1376264 | tf_op jit(solution)/shard_map/ppermute | solution.py:27
  107.3 1.4 %collective-permute-done.13.other = f32[896,128]{1,0:T(8,128)S(1)} collective-permute-done((f32[896,128]{1,0:T(8,128)S(1)}, f32[896,128]{1,0:T(8,128)S(1)}, u32[]{:S(2)}, u32[]{:S(2)}) %collective-permute-start.13) | collective-permute-done | bytes 458784 | tf_op jit(solution)/shard_map/ppermute | solution.py:27
  108.8 1.8 %shard_map.82 = (f32[300,128]{1,0:T(8,128)}, f32[300,2,256]{2,1,0:T(2,128)}) custom-call(s32[1]{0:T(128)} %bitcast.core, f32[896,128]{1,0:T(8,128)S(1)} %bitcast.17, f32[896,128]{1,0:T(8,128)S(1)} %collective-permute-done.13.other, bf16[2,128,256]{2,1,0:T(8,128)(2,1)S(1)} %shard_map.78.tile, bf16[2,128,256]{2,1,0:T(8,128)(2,1)S(1)} %collective-permute-done.12.came, ...), custom_call_target="tpu_custom_call" | custom-call | tf_op jit(solution)/shard_map/pallas_call | solution.py:270
  (7 shorter events, 0.1 us)
Async XLA Ops:
  0.6 0.8 copy-start.4
  0.6 0.8 copy-start.3
  1.5 4.8 %collective-permute-start.8 = (bf16[16,1,8,2048]{3,2,1,0:T(8,128)(2,1)S(1)}, bf16[16,1,8,2048]{3,2,1,0:T(8,128)(2,1)S(1)}, u32[]{:S(2)}, u32[]{:S(2)}) collective-permute-start(bf16[16,1,8,2048]{3,2,1,0:T(8,128)(2,1)S(1)} %get-tuple-element.38), channel_id=1, source_target_pairs={{0,1},{1,0},{2,3},{3,2},{4,5},{5,4},{6,7},{7,6},{8,9},{9,8},{10,11... | collective-permute-start | bytes 1572872 | tf_op jit(solution)/shard_map/cond/branch_2_fun/ppermute | solution.py:27
  41.4 4.7 %copy-start = (bf16[128,2048]{1,0:T(8,128)(2,1)S(1)}, bf16[128,2048]{1,0:T(8,128)(2,1)}, u32[]{:S(2)}) copy-start(bf16[128,2048]{1,0:T(8,128)(2,1)} %own.1) | copy-start | bytes 1572868
  41.5 7.7 %copy-start.1 = (f32[128,300]{0,1:T(8,128)S(1)}, f32[128,300]{0,1:T(8,128)}, u32[]{:S(2)}) copy-start(f32[128,300]{0,1:T(8,128)} %param.12) | copy-start | bytes 460804
  41.5 7.8 %copy-start.2 = (bf16[512,300]{0,1:T(8,128)(2,1)S(1)}, bf16[512,300]{0,1:T(8,128)(2,1)}, u32[]{:S(2)}) copy-start(bf16[512,300]{0,1:T(8,128)(2,1)} %param.10) | copy-start | bytes 921604
  41.5 19.2 %all-to-all-start.4 = ((bf16[16,2,8,2048]{3,2,1,0:T(8,128)(2,1)}), bf16[16,2,8,2048]{3,2,1,0:T(8,128)(2,1)S(1)}, u32[]{:S(2)}, u32[]{:S(2)}) async-start(bf16[16,2,8,2048]{3,2,1,0:T(8,128)(2,1)} %get-tuple-element.57), calls=%async_computation.4 | async-start | bytes 2097152 | tf_op jit(solution)/shard_map/all_to_all | solution.py:31
  46.1 5.0 %collective-permute-start.9 = (bf16[128,2048]{1,0:T(8,128)(2,1)S(1)}, bf16[128,2048]{1,0:T(8,128)(2,1)S(1)}, u32[]{:S(2)}, u32[]{:S(2)}) collective-permute-start(bf16[128,2048]{1,0:T(8,128)(2,1)S(1)} %copy-done), channel_id=1, source_target_pairs={{0,1},{1,0},{2,3},{3,2},{4,5},{5,4},{6,7},{7,6},{8,9},{9,8},{10,11... | collective-permute-start | bytes 1572872 | tf_op jit(solution)/shard_map/ppermute | solution.py:27
  49.1 16.4 %collective-permute-start.10 = (f32[300,128]{1,0:T(8,128)S(1)}, f32[300,128]{1,0:T(8,128)S(1)}, u32[]{:S(2)}, u32[]{:S(2)}) collective-permute-start(f32[300,128]{1,0:T(8,128)S(1)} %bitcast.18), channel_id=1, source_target_pairs={{0,1},{1,0},{2,3},{3,2},{4,5},{5,4},{6,7},{7,6},{8,9},{9,8},{10,11... | collective-permute-start | bytes 460808 | tf_op jit(solution)/shard_map/ppermute | solution.py:27
  50.3 15.2 %collective-permute-start.11 = (bf16[300,256]{1,0:T(8,128)(2,1)S(1)}, bf16[300,256]{1,0:T(8,128)(2,1)S(1)}, u32[]{:S(2)}, u32[]{:S(2)}) collective-permute-start(bf16[300,256]{1,0:T(8,128)(2,1)S(1)} %get-tuple-element.54), channel_id=1, source_target_pairs={{0,1},{1,0},{2,3},{3,2},{4,5},{5,4},{6,7},{7,6},{8,9},{9,8},{10,11... | collective-permute-start | bytes 460808 | tf_op jit(solution)/shard_map/ppermute | solution.py:27
  61.4 5.0 %collective-permute-start.12 = (bf16[2,128,256]{2,1,0:T(8,128)(2,1)S(1)}, bf16[2,128,256]{2,1,0:T(8,128)(2,1)S(1)}, u32[]{:S(2)}, u32[]{:S(2)}) collective-permute-start(bf16[2,128,256]{2,1,0:T(8,128)(2,1)S(1)} %shard_map.78.tile), channel_id=1, source_target_pairs={{0,1},{1,0},{2,3},{3,2},{4,5},{5,4},{6,7},{7,6},{8,9},{9,8},{10,11... | collective-permute-start | bytes 393224 | tf_op jit(solution)/shard_map/ppermute | solution.py:27
  103.3 5.5 %collective-permute-start.13 = (f32[896,128]{1,0:T(8,128)S(1)}, f32[896,128]{1,0:T(8,128)S(1)}, u32[]{:S(2)}, u32[]{:S(2)}) collective-permute-start(f32[896,128]{1,0:T(8,128)S(1)} %bitcast.16), channel_id=1, source_target_pairs={{0,1},{1,0},{2,3},{3,2},{4,5},{5,4},{6,7},{7,6},{8,9},{9,8},{10,11... | collective-permute-start | bytes 1376264 | tf_op jit(solution)/shard_map/ppermute | solution.py:27

commit v11 on v10

--- a/solution.py
+++ b/solution.py
@@ -64,9 +64,9 @@
     return -(-size // 8) * 8
 
 
-def rows_kernel(device, owners, batch_rows, spectra, kept, sent, *rest, sizes):
+def rows_kernel(owners, batch_rows, spectra, kept, sent, *rest, sizes):
     flag, (lines, listed, arrivals) = rest[:-3], rest[-3:]
-    here = device[0]
+    here = lax.axis_index(AXES)
     core = here & (sizes[3] - 1)
     plane, slots, each, features = kept.shape
     chunk = features // CHUNKS
@@ -298,10 +298,10 @@
         return call(
             functools.partial(rows_kernel, sizes=sizes),
             (blocks, blocks) + flag,
-            (device, owners, batch_rows, spectra),
-            scalars=2,
+            (owners, batch_rows, spectra),
+            scalars=1,
             out_kinds=[pltpu.VMEM, pltpu.VMEM] + [pltpu.SMEM] * len(flag),
-            in_place=(2, 3),
+            in_place=(1, 2),
             scratch=(
                 pltpu.VMEM(spectra.shape, narrow),
                 pltpu.VMEM(batch_rows.shape, jnp.int32),

time: 111 us -> 112 us (level)
  no operation moved by 1% of the time
where the time goes in v11:
time: 112 us; the launch traced here: 111 us
  blocking collectives  70.6 us (63%)
  starting transfers between devices  19.6 us (18%)
  waiting for transfers between devices  12.9 us (12%)
  Pallas kernels  6.5 us (6%)
    all_to_all x5, blocking collectives, exchange(): return lax.all_to_all(blocks, axes, 0, 0, tiled=True)  70.6 us
    ppermute x6, starting transfers between devices, swap(): return lax.ppermute(value, 'core', PAIR)  15 us
    all_to_all x1, waiting for transfers between devices, exchange(): return lax.all_to_all(blocks, axes, 0, 0, tiled=True)  9.54 us
    pallas_call x8, Pallas kernels, call(): pl.pallas_call(kernel, in_specs=[pl.BlockSpec(memory_space=kind) for kind...  6.5 us
    all_to_all x1, starting transfers between devices, exchange(): return lax.all_to_all(blocks, axes, 0, 0, tiled=True)  4.63 us
    ppermute x6, waiting for transfers between devices, swap(): return lax.ppermute(value, 'core', PAIR)  3.31 us
  transfers between devices with their start and end apart: 7, of which 4 were waited for; matrix products, arithmetic and copies ran while one was open for 0% of the time, Pallas kernels for 2%

profile of v11, /device:TPU:1, one launch (start us, length us, event | category | flops | bytes accessed | tf_op | source)
XLA Modules:
  0.0 111.1 jit_solution(15007082786069672893)
XLA Ops:
  0.6 0.0 copy-start.4
  0.6 0.0 copy-start.3
  0.6 0.9 shard_map.77
  1.5 0.0 copy-done.4
  1.5 0.0 copy-done.3
  1.5 40.4 %conditional.1 = (bf16[16,2,8,2048]{3,2,1,0:T(8,128)(2,1)}) conditional(s32[]{:T(128)} %bitcast.1, (s32[2]{0:T(128)S(1)}, s32[2,256]{1,0:T(2,128)S(1)}, bf16[512,2048]{1,0:T(8,128)(2,1)}, s32[8]{0:T(128)S(4)}) %tuple.24, (bf16[16,1,8,2048]{3,2,1,0:T(8,128)(2,1)S(1)}, bf16[16,1,8,2048]{3,2,1,0:T(8,128)(2,1)S(1)}, ...), branch_computations={%region_0.0_spmd, %region_1.0_spmd, %region_2.0_spmd} | conditional | flops 589824 | bytes 10617000 | solution.py:345
  1.6 3.3 %collective-permute-start.8 = (bf16[16,1,8,2048]{3,2,1,0:T(8,128)(2,1)S(1)}, bf16[16,1,8,2048]{3,2,1,0:T(8,128)(2,1)S(1)}, u32[]{:S(2)}, u32[]{:S(2)}) collective-permute-start(bf16[16,1,8,2048]{3,2,1,0:T(8,128)(2,1)S(1)} %get-tuple-element.35), channel_id=1, source_target_pairs={{0,1},{1,0},{2,3},{3,2},{4,5},{5,4},{6,7},{7,6},{8,9},{9,8},{10,11... | collective-permute-start | bytes 1572872 | tf_op jit(solution)/shard_map/cond/branch_2_fun/ppermute | solution.py:27
  4.9 1.5 %collective-permute-done.8 = bf16[16,1,8,2048]{3,2,1,0:T(8,128)(2,1)S(1)} collective-permute-done((bf16[16,1,8,2048]{3,2,1,0:T(8,128)(2,1)S(1)}, bf16[16,1,8,2048]{3,2,1,0:T(8,128)(2,1)S(1)}, u32[]{:S(2)}, u32[]{:S(2)}) %collective-permute-start.8) | collective-permute-done | bytes 524320 | tf_op jit(solution)/shard_map/cond/branch_2_fun/ppermute | solution.py:27
  6.4 0.1 add.46
  6.5 15.6 %all_to_all.38.scattered = bf16[16,1,8,2048]{3,2,1,0:T(8,128)(2,1)S(1)} all-to-all(bf16[16,1,8,2048]{3,2,1,0:T(8,128)(2,1)S(1)} %add.46), channel_id=1, replica_groups=mesh['y'=4,'z'=8,'x'=4,'core'=2] {'y','x'}, dimensions={0} | all-to-all | bytes 1048576 | tf_op jit(solution)/shard_map/cond/branch_2_fun/all_to_all | solution.py:31
  22.1 18.6 %all_to_all.39.along = bf16[8,8,2048]{2,1,0:T(8,128)(2,1)S(1)} all-to-all(bf16[8,8,2048]{2,1,0:T(8,128)(2,1)S(1)} %branch_2_fun.2), channel_id=1, replica_groups=mesh['y'=4,'z'=8,'x'=4,'core'=2] {'z'}, dimensions={0} | all-to-all | bytes 524288 | tf_op jit(solution)/shard_map/cond/branch_2_fun/all_to_all | solution.py:31
  40.7 1.3 %branch_2_fun.3 = bf16[16,2,8,2048]{3,2,1,0:T(8,128)(2,1)} custom-call(s32[8]{0:T(128)S(4)} %get-tuple-element.33.spots, bf16[8,8,2048]{2,1,0:T(8,128)(2,1)S(1)} %all_to_all.39.along), custom_call_target="tpu_custom_call" | custom-call | tf_op jit(solution)/shard_map/cond/branch_2_fun/pallas_call | solution.py:270
  42.0 0.0 copy-start
  42.0 0.0 copy-start.2
  42.0 0.0 copy-start.1
  42.0 4.6 %all-to-all-start.4 = ((bf16[16,2,8,2048]{3,2,1,0:T(8,128)(2,1)}), bf16[16,2,8,2048]{3,2,1,0:T(8,128)(2,1)S(1)}, u32[]{:S(2)}, u32[]{:S(2)}) async-start(bf16[16,2,8,2048]{3,2,1,0:T(8,128)(2,1)} %get-tuple-element.54), calls=%async_computation.4 | async-start | bytes 2097152 | tf_op jit(solution)/shard_map/all_to_all | solution.py:31
  46.6 0.0 copy-done
  46.7 3.0 %collective-permute-start.9 = (bf16[128,2048]{1,0:T(8,128)(2,1)S(1)}, bf16[128,2048]{1,0:T(8,128)(2,1)S(1)}, u32[]{:S(2)}, u32[]{:S(2)}) collective-permute-start(bf16[128,2048]{1,0:T(8,128)(2,1)S(1)} %copy-done), channel_id=1, source_target_pairs={{0,1},{1,0},{2,3},{3,2},{4,5},{5,4},{6,7},{7,6},{8,9},{9,8},{10,11... | collective-permute-start | bytes 1572872 | tf_op jit(solution)/shard_map/ppermute | solution.py:27
  49.6 0.0 copy-done.2
  49.6 1.0 shard_map.79
  50.7 0.1 collective-permute-start.11
  50.8 0.0 copy-done.1
  50.8 0.5 collective-permute-start.10
  51.3 0.2 multiply_reduce_fusion.1
  51.5 0.0 collective-permute-done.9.other
  51.5 0.2 multiply_reduce_fusion
  51.7 9.5 %all-to-all-done.4 = bf16[16,2,8,2048]{3,2,1,0:T(8,128)(2,1)S(1)} async-done(((bf16[16,2,8,2048]{3,2,1,0:T(8,128)(2,1)}), bf16[16,2,8,2048]{3,2,1,0:T(8,128)(2,1)S(1)}, u32[]{:S(2)}, u32[]{:S(2)}) %all-to-all-start.4) | async-done | bytes 1048608 | tf_op jit(solution)/shard_map/all_to_all | solution.py:31
  61.2 0.7 shard_map.78.tile
  62.0 4.0 %collective-permute-start.12 = (bf16[2,128,256]{2,1,0:T(8,128)(2,1)S(1)}, bf16[2,128,256]{2,1,0:T(8,128)(2,1)S(1)}, u32[]{:S(2)}, u32[]{:S(2)}) collective-permute-start(bf16[2,128,256]{2,1,0:T(8,128)(2,1)S(1)} %shard_map.78.tile), channel_id=1, source_target_pairs={{0,1},{1,0},{2,3},{3,2},{4,5},{5,4},{6,7},{7,6},{8,9},{9,8},{10,11... | collective-permute-start | bytes 393224 | tf_op jit(solution)/shard_map/ppermute | solution.py:27
  66.0 0.0 collective-permute-done.11.arrived
  66.0 0.0 collective-permute-done.10.other
  66.0 0.6 shard_map.80.partial
  66.7 0.3 collective-permute-done.12.came
  67.0 0.2 shard_map.81
  67.2 12.7 %all_to_all.40 = f32[16,56,128]{2,1,0:T(8,128)S(1)} all-to-all(f32[16,56,128]{2,1,0:T(8,128)S(1)} %bitcast.15), channel_id=1, replica_groups=mesh['y'=4,'z'=8,'x'=4,'core'=2] {'y','x'}, dimensions={0} | all-to-all | bytes 917504 | tf_op jit(solution)/shard_map/all_to_all | solution.py:31
  79.9 11.6 %all_to_all.41 = f32[8,56,128]{2,1,0:T(8,128)S(1)} all-to-all(f32[8,56,128]{2,1,0:T(8,128)S(1)} %broadcast_in_dim.4), channel_id=1, replica_groups=mesh['y'=4,'z'=8,'x'=4,'core'=2] {'z'}, dimensions={0} | all-to-all | bytes 458752 | tf_op jit(solution)/shard_map/all_to_all | solution.py:31
  91.5 12.3 %all_to_all.42 = f32[16,56,128]{2,1,0:T(8,128)S(1)} all-to-all(f32[16,56,128]{2,1,0:T(8,128)S(1)} %broadcast_in_dim.5), channel_id=1, replica_groups=mesh['y'=4,'z'=8,'x'=4,'core'=2] {'y','x'}, dimensions={0} | all-to-all | bytes 917504 | tf_op jit(solution)/shard_map/all_to_all | solution.py:31
  103.8 4.1 %collective-permute-start.13 = (f32[896,128]{1,0:T(8,128)S(1)}, f32[896,128]{1,0:T(8,128)S(1)}, u32[]{:S(2)}, u32[]{:S(2)}) collective-permute-start(f32[896,128]{1,0:T(8,128)S(1)} %bitcast.16), channel_id=1, source_target_pairs={{0,1},{1,0},{2,3},{3,2},{4,5},{5,4},{6,7},{7,6},{8,9},{9,8},{10,11... | collective-permute-start | bytes 1376264 | tf_op jit(solution)/shard_map/ppermute | solution.py:27
  107.9 1.4 %collective-permute-done.13.other = f32[896,128]{1,0:T(8,128)S(1)} collective-permute-done((f32[896,128]{1,0:T(8,128)S(1)}, f32[896,128]{1,0:T(8,128)S(1)}, u32[]{:S(2)}, u32[]{:S(2)}) %collective-permute-start.13) | collective-permute-done | bytes 458784 | tf_op jit(solution)/shard_map/ppermute | solution.py:27
  109.3 1.8 %shard_map.82 = (f32[300,128]{1,0:T(8,128)}, f32[300,2,256]{2,1,0:T(2,128)}) custom-call(s32[1]{0:T(128)} %bitcast.core, f32[896,128]{1,0:T(8,128)S(1)} %bitcast.17, f32[896,128]{1,0:T(8,128)S(1)} %collective-permute-done.13.other, bf16[2,128,256]{2,1,0:T(8,128)(2,1)S(1)} %shard_map.78.tile, bf16[2,128,256]{2,1,0:T(8,128)(2,1)S(1)} %collective-permute-done.12.came, ...), custom_call_target="tpu_custom_call" | custom-call | tf_op jit(solution)/shard_map/pallas_call | solution.py:270
  (7 shorter events, 0.1 us)
Async XLA Ops:
  0.6 0.9 copy-start.4
  0.6 0.9 copy-start.3
  1.6 4.8 %collective-permute-start.8 = (bf16[16,1,8,2048]{3,2,1,0:T(8,128)(2,1)S(1)}, bf16[16,1,8,2048]{3,2,1,0:T(8,128)(2,1)S(1)}, u32[]{:S(2)}, u32[]{:S(2)}) collective-permute-start(bf16[16,1,8,2048]{3,2,1,0:T(8,128)(2,1)S(1)} %get-tuple-element.35), channel_id=1, source_target_pairs={{0,1},{1,0},{2,3},{3,2},{4,5},{5,4},{6,7},{7,6},{8,9},{9,8},{10,11... | collective-permute-start | bytes 1572872 | tf_op jit(solution)/shard_map/cond/branch_2_fun/ppermute | solution.py:27
  42.0 4.7 %copy-start = (bf16[128,2048]{1,0:T(8,128)(2,1)S(1)}, bf16[128,2048]{1,0:T(8,128)(2,1)}, u32[]{:S(2)}) copy-start(bf16[128,2048]{1,0:T(8,128)(2,1)} %own.1) | copy-start | bytes 1572868
  42.0 7.7 %copy-start.2 = (bf16[512,300]{0,1:T(8,128)(2,1)S(1)}, bf16[512,300]{0,1:T(8,128)(2,1)}, u32[]{:S(2)}) copy-start(bf16[512,300]{0,1:T(8,128)(2,1)} %param.10) | copy-start | bytes 921604
  42.0 8.8 %copy-start.1 = (f32[128,300]{0,1:T(8,128)S(1)}, f32[128,300]{0,1:T(8,128)}, u32[]{:S(2)}) copy-start(f32[128,300]{0,1:T(8,128)} %param.12) | copy-start | bytes 460804
  42.0 19.2 %all-to-all-start.4 = ((bf16[16,2,8,2048]{3,2,1,0:T(8,128)(2,1)}), bf16[16,2,8,2048]{3,2,1,0:T(8,128)(2,1)S(1)}, u32[]{:S(2)}, u32[]{:S(2)}) async-start(bf16[16,2,8,2048]{3,2,1,0:T(8,128)(2,1)} %get-tuple-element.54), calls=%async_computation.4 | async-start | bytes 2097152 | tf_op jit(solution)/shard_map/all_to_all | solution.py:31
  46.7 4.8 %collective-permute-start.9 = (bf16[128,2048]{1,0:T(8,128)(2,1)S(1)}, bf16[128,2048]{1,0:T(8,128)(2,1)S(1)}, u32[]{:S(2)}, u32[]{:S(2)}) collective-permute-start(bf16[128,2048]{1,0:T(8,128)(2,1)S(1)} %copy-done), channel_id=1, source_target_pairs={{0,1},{1,0},{2,3},{3,2},{4,5},{5,4},{6,7},{7,6},{8,9},{9,8},{10,11... | collective-permute-start | bytes 1572872 | tf_op jit(solution)/shard_map/ppermute | solution.py:27
  50.7 15.3 %collective-permute-start.11 = (bf16[300,256]{1,0:T(8,128)(2,1)S(1)}, bf16[300,256]{1,0:T(8,128)(2,1)S(1)}, u32[]{:S(2)}, u32[]{:S(2)}) collective-permute-start(bf16[300,256]{1,0:T(8,128)(2,1)S(1)} %get-tuple-element.51), channel_id=1, source_target_pairs={{0,1},{1,0},{2,3},{3,2},{4,5},{5,4},{6,7},{7,6},{8,9},{9,8},{10,11... | collective-permute-start | bytes 460808 | tf_op jit(solution)/shard_map/ppermute | solution.py:27
  50.8 15.2 %collective-permute-start.10 = (f32[300,128]{1,0:T(8,128)S(1)}, f32[300,128]{1,0:T(8,128)S(1)}, u32[]{:S(2)}, u32[]{:S(2)}) collective-permute-start(f32[300,128]{1,0:T(8,128)S(1)} %bitcast.18), channel_id=1, source_target_pairs={{0,1},{1,0},{2,3},{3,2},{4,5},{5,4},{6,7},{7,6},{8,9},{9,8},{10,11... | collective-permute-start | bytes 460808 | tf_op jit(solution)/shard_map/ppermute | solution.py:27
  62.0 5.0 %collective-permute-start.12 = (bf16[2,128,256]{2,1,0:T(8,128)(2,1)S(1)}, bf16[2,128,256]{2,1,0:T(8,128)(2,1)S(1)}, u32[]{:S(2)}, u32[]{:S(2)}) collective-permute-start(bf16[2,128,256]{2,1,0:T(8,128)(2,1)S(1)} %shard_map.78.tile), channel_id=1, source_target_pairs={{0,1},{1,0},{2,3},{3,2},{4,5},{5,4},{6,7},{7,6},{8,9},{9,8},{10,11... | collective-permute-start | bytes 393224 | tf_op jit(solution)/shard_map/ppermute | solution.py:27
  103.8 5.5 %collective-permute-start.13 = (f32[896,128]{1,0:T(8,128)S(1)}, f32[896,128]{1,0:T(8,128)S(1)}, u32[]{:S(2)}, u32[]{:S(2)}) collective-permute-start(f32[896,128]{1,0:T(8,128)S(1)} %bitcast.16), channel_id=1, source_target_pairs={{0,1},{1,0},{2,3},{3,2},{4,5},{5,4},{6,7},{7,6},{8,9},{9,8},{10,11... | collective-permute-start | bytes 1376264 | tf_op jit(solution)/shard_map/ppermute | solution.py:27
